TPU v7x, 32 devices: a whole 2x2x4 slice. The times are simulated.
32 devices in a mesh: replica: 4 (over y, x), fsdp: 8 (over z, core).
Axes of the slice: x: 2, y: 2, z: 4, core: 2. Of those that a mesh axis runs over, the one named last changes fastest.
Arguments:
- partner: int32 [4], replicated, may hold values from 0 to 3, as said below
- tokens: bfloat16 [4, 128, 4096], P('replica', 'fsdp'), may hold values from -6 to 6
- w_gate: bfloat16 [4, 7168, 4096], P('replica', 'fsdp'), may hold values from -0.09375 to 0.09375
- w_up: bfloat16 [4, 7168, 4096], P('replica', 'fsdp'), may hold values from -0.09375 to 0.09375
- w_down: bfloat16 [4, 7168, 4096], P('replica', 'fsdp'), may hold values from -0.0625 to 0.0625
Outputs:
- grad_gate: bfloat16 [4, 7168, 4096], P('replica', 'fsdp')
- grad_up: bfloat16 [4, 7168, 4096], P('replica', 'fsdp')
- grad_down: bfloat16 [4, 7168, 4096], P('replica', 'fsdp')
Inputs may be any that keep to these rules, and one draw needn't show every extreme that they name: partner is a permutation of the 4 replicas that forms one single cycle through all of them; no replica is its own partner.
All inputs are finite; a program needn't handle non-finite values.
Results may differ from a plain program's by a relative error of at most 0.025.
Values may be sent and summed in bfloat16 or wider, within the bound.
No kernel may reach another device: no remote copies, remote signals or barrier semaphores. Data moves between devices by JAX's collectives and lax.ppermute only.
A program may use at most 128 MiB of HBM per device.

v0:
```python
import functools
import math

import jax
import jax.numpy as jnp
from jax import lax
from jax.experimental import pallas as pl
from jax.experimental.pallas import tpu as pltpu
from jax.sharding import PartitionSpec as P


CHUNKS = 2
ANY = pl.BlockSpec(memory_space=pl.ANY)
VMEM = pl.BlockSpec(memory_space=pltpu.VMEM)


def peer(index, step, count):
    return index ^ step if count & (count - 1) == 0 else (index + step) % count


def fetch(value, axis, step, count, stride=1):
    pairs = [
        (peer(i, step, count) * stride + low, i * stride + low)
        for i in range(count)
        for low in range(stride)
    ]
    return lax.ppermute(value, axis, pairs)


def give(value, axis, step, count, stride=1):
    pairs = [
        (i * stride + low, peer(i, step, count) * stride + low)
        for i in range(count)
        for low in range(stride)
    ]
    return lax.ppermute(value, axis, pairs)


def swap(value, members):
    return lax.ppermute(value, "fsdp", [(i, i ^ 1) for i in range(members)])


def gather_rows(rows, chips, members):
    mine = [rows] + [fetch(rows, "fsdp", k, chips, 2) for k in range(1, chips)]
    return mine + [swap(piece, members) for piece in mine]


def scatter_rows(mine, theirs, chips, members):
    other = swap(theirs, members)
    rows, wide = mine.shape[0] // chips, mine.shape[1]
    terms = small_call(
        chip_kernel,
        [mine, other],
        [jax.ShapeDtypeStruct((rows, wide), jnp.float32)]
        + [jax.ShapeDtypeStruct((rows, wide), jnp.bfloat16)] * (chips - 1),
    )
    return [terms[0]] + [give(terms[k], "fsdp", k, chips, 2) for k in range(1, chips)]


def spread(value, replicas):
    return [fetch(value, "replica", k, replicas) for k in range(1, replicas)]


def small_call(kernel, operands, shapes, partner=None):
    head = [] if partner is None else [partner]
    flat = shapes if isinstance(shapes, list) else [shapes]
    size = sum(x.size for x in operands) + sum(x.size for x in flat)
    return pl.pallas_call(
        kernel,
        out_shape=shapes,
        in_specs=[pl.BlockSpec(memory_space=pltpu.SMEM)] * len(head) + [VMEM] * len(operands),
        out_specs=[VMEM] * len(flat) if isinstance(shapes, list) else VMEM,
        compiler_params=pltpu.CompilerParams(vmem_limit_bytes=4 << 20),
        cost_estimate=pl.CostEstimate(flops=size, bytes_accessed=2 * size, transcendentals=0),
    )(*head, *operands)


def chip_kernel(mine, other, own, *pieces):
    rows = own.shape[0]
    for k, target in enumerate((own,) + pieces):
        part = pl.ds(k * rows, rows)
        target[...] = (mine[part] + other[part].astype(jnp.float32)).astype(target.dtype)


def sum_kernel(*refs):
    total = refs[0][...]
    for term in refs[1:-1]:
        total = total + term[...].astype(jnp.float32)
    refs[-1][...] = total.astype(refs[-1].dtype)


def choose(candidates, step):
    chosen = candidates[0][...]
    for k in range(1, len(candidates)):
        chosen = jnp.where(step == k + 1, candidates[k][...], chosen)
    return chosen


def step_to(wanted, here, replicas):
    return here ^ wanted if replicas & (replicas - 1) == 0 else (wanted - here + replicas) % replicas


def foreign_kernel(partner, *refs):
    replicas = partner.shape[0]
    here = lax.axis_index("replica")
    taught = sum(jnp.where(partner[r] == here, r, 0) for r in range(replicas))
    refs[-1][...] = choose(refs[:-1], step_to(taught, here, replicas))


def cotangent_kernel(chips, start, scale, partner, *refs):
    replicas = partner.shape[0]
    here = lax.axis_index("replica")
    wanted = sum(jnp.where(here == r, partner[r], 0) for r in range(replicas))
    target = refs[-1]
    columns = pl.ds(start, target.shape[1])
    student = refs[0][:, columns]
    for term in refs[1:chips]:
        student = student + term[:, columns].astype(jnp.float32)
    teacher = choose(refs[chips:-1], step_to(wanted, here, replicas)).astype(jnp.float32)
    target[...] = ((student - teacher) * scale).astype(target.dtype)


def contract(left, right, left_dim, right_dim):
    return lax.dot_general(
        left, right, (((left_dim,), (right_dim,)), ((), ())), preferred_element_type=jnp.float32
    )


def block_of(count):
    return 128 if count % 128 == 0 else count


def put_together(pieces, whole):
    rows = pieces[0].shape[0]
    for i, piece in enumerate(pieces):
        whole[i * rows : (i + 1) * rows, :] = piece[...]


def load_kernel(*refs):
    count = len(refs) // 2
    sems = refs[-1]
    copies = [
        pltpu.make_async_copy(refs[i], refs[count + i], sems.at[i]) for i in range(count)
    ]
    for copy in copies:
        copy.start()
    for copy in copies:
        copy.wait()


def in_hbm(array):
    return pltpu.with_memory_space_constraint(array, pltpu.HBM)


def in_vmem(array):
    return pltpu.with_memory_space_constraint(array, pltpu.VMEM)


def load(*weights):
    return pl.pallas_call(
        load_kernel,
        out_shape=[pltpu.VMEM(w.shape, w.dtype) for w in weights],
        in_specs=[ANY] * len(weights),
        out_specs=[VMEM] * len(weights),
        scratch_shapes=[pltpu.SemaphoreType.DMA((len(weights),))],
        compiler_params=pltpu.CompilerParams(vmem_limit_bytes=1 << 20),
        cost_estimate=pl.CostEstimate(
            flops=0, bytes_accessed=sum(2 * w.size for w in weights), transcendentals=0
        ),
        name="load",
    )(*[in_hbm(w) for w in weights])


def forward_kernel(count, chunks, keep, *refs):
    pieces, (gate_w, up_w, down_w) = refs[:count], refs[count : count + 3]
    rest = list(refs[count + 3 :])
    if keep:
        down_hbm = down_w
        down_w, rows_all, pre_gate, pre_up, hidden = rest[:5]
        outs, sem = rest[5:-1], rest[-1]
        fill = pltpu.make_async_copy(down_hbm, down_w, sem)
        fill.start()
    else:
        outs, (rows_all, hidden) = rest[: 2 * chunks], rest[2 * chunks :]
    height = gate_w.shape[0]
    step = block_of(height)
    put_together(pieces, rows_all)
    for j in range(height // step):
        part = pl.ds(j * step, step)
        gate = contract(gate_w[part], rows_all[...], 1, 1)
        up = contract(up_w[part], rows_all[...], 1, 1)
        if keep:
            pre_gate[part] = gate
            pre_up[part] = up
        hidden[part] = (gate * jax.nn.sigmoid(gate) * up).astype(hidden.dtype)
    if keep:
        fill.wait()
    half = rows_all.shape[0] // 2
    wide = down_w.shape[1] // chunks
    tile = min(512, wide)
    across = hidden[...].T
    for c in range(chunks):
        for start in range(0, wide, tile):
            value = contract(across, down_w[:, pl.ds(c * wide + start, tile)], 1, 0)
            outs[2 * c][:, start : start + tile] = value[:half]
            outs[2 * c + 1][:, start : start + tile] = value[half:].astype(jnp.bfloat16)


def forward(pieces, gate_w, up_w, down_w, chunks, keep):
    height, depth = gate_w.shape
    rows = len(pieces) * pieces[0].shape[0]
    wide = depth // chunks
    shapes, scratch = [], []
    if keep:
        scratch += [pltpu.SemaphoreType.DMA]
        shapes += [
            pltpu.VMEM((height, depth), jnp.bfloat16),
            jax.ShapeDtypeStruct((rows, depth), jnp.bfloat16),
            jax.ShapeDtypeStruct((height, rows), jnp.float32),
            jax.ShapeDtypeStruct((height, rows), jnp.float32),
            jax.ShapeDtypeStruct((height, rows), jnp.bfloat16),
        ]
    else:
        scratch += [pltpu.VMEM((rows, depth), jnp.bfloat16), pltpu.VMEM((height, rows), jnp.bfloat16)]
    for _ in range(chunks):
        shapes.append(jax.ShapeDtypeStruct((rows // 2, wide), jnp.float32))
        shapes.append(jax.ShapeDtypeStruct((rows // 2, wide), jnp.bfloat16))
    return pl.pallas_call(
        functools.partial(forward_kernel, len(pieces), chunks, keep),
        out_shape=shapes,
        in_specs=[VMEM] * (len(pieces) + 2) + [ANY if keep else VMEM],
        out_specs=[VMEM] * len(shapes),
        scratch_shapes=scratch,
        compiler_params=pltpu.CompilerParams(vmem_limit_bytes=12 << 20),
        cost_estimate=pl.CostEstimate(
            flops=6 * rows * height * depth,
            bytes_accessed=6 * height * depth,
            transcendentals=rows * height,
        ),
        name="student_forward" if keep else "teacher_forward",
    )(*pieces, in_vmem(gate_w), in_vmem(up_w), (in_hbm if keep else in_vmem)(down_w))


def backward_kernel(count, first, final, start, *refs):
    pieces, refs = refs[:count], list(refs[count:])
    hidden, down_w = refs[:2]
    refs = refs[2:]
    if not first:
        before = refs[0]
        refs = refs[2:]
    if final:
        pre_gate, pre_up, rows_all = refs[:3]
        refs = refs[3:]
        grad_down, grad_gate, grad_up = refs[:3]
        refs = refs[3:]
        cotangent, stage_down, stage_gate, stage_up, sems = refs
    else:
        grad_down, after = refs[:2]
        cotangent, stage_down, sems = refs[2:]
    height = hidden.shape[0]
    wide = cotangent.shape[1]
    columns = pl.ds(start, wide)
    step = block_of(height)
    blocks = height // step
    put_together(pieces, cotangent)
    copies = []

    def send(source, target):
        copies.append(pltpu.make_async_copy(source, target, sems.at[len(copies)]))
        copies[-1].start()

    for j in range(blocks):
        part = pl.ds(j * step, step)
        stage_down[part] = contract(hidden[part], cotangent[...], 1, 0).astype(jnp.bfloat16)
        send(stage_down.at[part], grad_down.at[part, columns])
    for j in range(blocks):
        part = pl.ds(j * step, step)
        d_hidden = contract(down_w[part, columns], cotangent[...], 1, 1)
        if not first:
            d_hidden = d_hidden + before[part]
        if not final:
            after[part] = d_hidden
            continue
        gate, up = pre_gate[part], pre_up[part]
        sigma = jax.nn.sigmoid(gate)
        d_gate = (d_hidden * up * sigma * (1.0 + gate * (1.0 - sigma))).astype(jnp.bfloat16)
        d_up = (d_hidden * gate * sigma).astype(jnp.bfloat16)
        stage_gate[part] = contract(d_gate, rows_all[...], 1, 0).astype(jnp.bfloat16)
        send(stage_gate.at[part], grad_gate.at[part])
        stage_up[part] = contract(d_up, rows_all[...], 1, 0).astype(jnp.bfloat16)
        send(stage_up.at[part], grad_up.at[part])
    for copy in copies:
        copy.wait()


def backward(pieces, hidden, down_w, carried, saved, start):
    height, depth = down_w.shape
    rows = hidden.shape[1]
    wide = pieces[0].shape[1]
    blocks = height // block_of(height)
    first, final = carried is None, saved is not None
    operands = list(pieces) + [hidden, in_vmem(down_w)]
    in_specs = [VMEM] * (len(pieces) + 2)
    aliases = {}
    if not first:
        aliases = {len(operands) + 1: 0}
        operands += [carried[0], in_hbm(carried[1])]
        in_specs += [VMEM, ANY]
    whole = jax.ShapeDtypeStruct((height, depth), jnp.bfloat16)
    scratch = [
        pltpu.VMEM((rows, wide), jnp.bfloat16),
        pltpu.VMEM((height, wide), jnp.bfloat16),
    ]
    sends = blocks
    if final:
        operands += list(saved)
        in_specs += [VMEM] * 3
        shapes, out_specs = [whole] * 3, [ANY] * 3
        scratch += [pltpu.VMEM((height, depth), jnp.bfloat16)] * 2
        sends = 3 * blocks
    else:
        shapes = [whole, jax.ShapeDtypeStruct((height, rows), jnp.float32)]
        out_specs = [ANY, VMEM]
    scratch += [pltpu.SemaphoreType.DMA((sends,))]
    products = 4 * wide + (4 * depth if final else 0)
    return pl.pallas_call(
        functools.partial(backward_kernel, len(pieces), first, final, start),
        out_shape=shapes,
        in_specs=in_specs,
        out_specs=out_specs,
        scratch_shapes=scratch,
        input_output_aliases=aliases,
        compiler_params=pltpu.CompilerParams(vmem_limit_bytes=(26 if final else 8) << 20),
        cost_estimate=pl.CostEstimate(
            flops=products * rows * height,
            bytes_accessed=products * height,
            transcendentals=rows * height if final else 0,
        ),
    )(*operands)


def local(partner, tokens, w_gate, w_up, w_down):
    rows = tokens[0]
    gate_w, up_w, down_w = w_gate[0], w_up[0], w_down[0]
    replicas = lax.axis_size("replica")
    members = lax.axis_size("fsdp")
    chips = members // 2
    scale = 1.0 / math.sqrt(rows.shape[0] * members)
    foreign = small_call(
        foreign_kernel,
        spread(rows, replicas),
        jax.ShapeDtypeStruct(rows.shape, rows.dtype),
        partner,
    )
    gate_w, up_w = load(gate_w, up_w)
    own_pieces = gather_rows(rows, chips, members)
    down_w, rows_all, pre_gate, pre_up, hidden, mine, theirs = forward(
        own_pieces, gate_w, up_w, down_w, 1, True
    )
    student = scatter_rows(mine, theirs, chips, members)
    foreign_pieces = gather_rows(foreign, chips, members)
    parts = forward(foreign_pieces, gate_w, up_w, down_w, CHUNKS, False)
    wide = rows.shape[1] // CHUNKS
    part = jax.ShapeDtypeStruct((rows.shape[0], wide), jnp.bfloat16)
    carried = None
    for c in range(CHUNKS):
        terms = scatter_rows(parts[2 * c], parts[2 * c + 1], chips, members)
        taught = small_call(sum_kernel, terms, part)
        cotangent = small_call(
            functools.partial(cotangent_kernel, chips, c * wide, scale),
            student + spread(taught, replicas),
            part,
            partner,
        )
        pieces = gather_rows(cotangent, chips, members)
        saved = (pre_gate, pre_up, rows_all) if c == CHUNKS - 1 else None
        grads = backward(pieces, hidden, down_w, carried, saved, c * wide)
        carried = (grads[1], grads[0])
    grad_down, grad_gate, grad_up = grads
    return (grad_gate[None], grad_up[None], grad_down[None])


def solution(mesh):
    in_specs = (P(),) + (P("replica", "fsdp", None),) * 4
    out_specs = (P("replica", "fsdp", None),) * 3
    return jax.shard_map(local, mesh=mesh, in_specs=in_specs, out_specs=out_specs, check_vma=False)
```

profile of v0, /device:TPU:0, one launch (start us, length us, event | category | flops | bytes accessed | tf_op | source)
XLA Modules:
  0.0 103.1 jit_solution(16277080064470061659)
XLA Ops:
  0.6 4.0 %collective-permute-start.13 = (bf16[16,4096]{1,0:T(8,128)(2,1)}, bf16[16,4096]{1,0:T(8,128)(2,1)S(1)}, u32[]{:S(2)}, u32[]{:S(2)}) collective-permute-start(bf16[16,4096]{1,0:T(8,128)(2,1)} %bitcast.7), channel_id=1, source_target_pairs={{24,0},{16,8},{8,16},{0,24},{25,1},{17,9},{9,17},{1,25},{26,2},{18... | collective-permute-start | bytes 393224 | tf_op jit(solution)/shard_map/ppermute | solution.py:27
  4.6 0.5 collective-permute-start.12
  5.3 4.0 %collective-permute-start.2 = (bf16[16,4096]{1,0:T(8,128)(2,1)}, bf16[16,4096]{1,0:T(8,128)(2,1)S(1)}, u32[]{:S(2)}, u32[]{:S(2)}) collective-permute-start(bf16[16,4096]{1,0:T(8,128)(2,1)} %bitcast.11), channel_id=1, source_target_pairs={{6,0},{7,1},{4,2},{5,3},{2,4},{3,5},{0,6},{1,7},{14,8},{15,9},{12,... | collective-permute-start | bytes 393224 | tf_op jit(solution)/shard_map/ppermute | solution.py:27
  9.3 2.2 %collective-permute-start.1 = (bf16[16,4096]{1,0:T(8,128)(2,1)}, bf16[16,4096]{1,0:T(8,128)(2,1)S(1)}, u32[]{:S(2)}, u32[]{:S(2)}) collective-permute-start(bf16[16,4096]{1,0:T(8,128)(2,1)} %bitcast.12), channel_id=1, source_target_pairs={{4,0},{5,1},{6,2},{7,3},{0,4},{1,5},{2,6},{3,7},{12,8},{13,9},{14,... | collective-permute-start | bytes 393224 | tf_op jit(solution)/shard_map/ppermute | solution.py:27
  11.5 1.6 %collective-permute-start = (bf16[16,4096]{1,0:T(8,128)(2,1)}, bf16[16,4096]{1,0:T(8,128)(2,1)S(1)}, u32[]{:S(2)}, u32[]{:S(2)}) collective-permute-start(bf16[16,4096]{1,0:T(8,128)(2,1)} %bitcast.13), channel_id=1, source_target_pairs={{2,0},{3,1},{0,2},{1,3},{6,4},{7,5},{4,6},{5,7},{10,8},{11,9},{8,1... | collective-permute-start | bytes 393224 | tf_op jit(solution)/shard_map/ppermute | solution.py:27
  13.0 0.7 copy-done.1
  13.7 0.6 shard_map.77.refs_0_
  14.3 2.4 %collective-permute-start.16 = (bf16[16,4096]{1,0:T(8,128)(2,1)S(1)}, bf16[16,4096]{1,0:T(8,128)(2,1)S(1)}, u32[]{:S(2)}, u32[]{:S(2)}) collective-permute-start(bf16[16,4096]{1,0:T(8,128)(2,1)S(1)} %shard_map.77.refs_0_), channel_id=1, source_target_pairs={{6,0},{7,1},{4,2},{5,3},{2,4},{3,5},{0,6},{1,7},{14,8},{15,9},{12,... | collective-permute-start | bytes 393224 | tf_op jit(solution)/shard_map/ppermute | solution.py:27
  16.9 2.7 %collective-permute-start.14 = (bf16[16,4096]{1,0:T(8,128)(2,1)S(1)}, bf16[16,4096]{1,0:T(8,128)(2,1)S(1)}, u32[]{:S(2)}, u32[]{:S(2)}) collective-permute-start(bf16[16,4096]{1,0:T(8,128)(2,1)S(1)} %shard_map.77.refs_0_), channel_id=1, source_target_pairs={{2,0},{3,1},{0,2},{1,3},{6,4},{7,5},{4,6},{5,7},{10,8},{11,9},{8,1... | collective-permute-start | bytes 393224 | tf_op jit(solution)/shard_map/ppermute | solution.py:27
  19.6 7.7 %collective-permute-done.1.refs_2_ = bf16[16,4096]{1,0:T(8,128)(2,1)S(1)} collective-permute-done((bf16[16,4096]{1,0:T(8,128)(2,1)}, bf16[16,4096]{1,0:T(8,128)(2,1)S(1)}, u32[]{:S(2)}, u32[]{:S(2)}) %collective-permute-start.1) | collective-permute-done | bytes 131104 | tf_op jit(solution)/shard_map/ppermute | solution.py:27
  27.4 0.5 collective-permute-start.5
  27.9 5.2 %load.1 = (bf16[896,4096]{1,0:T(8,128)(2,1)S(1)}, bf16[896,4096]{1,0:T(8,128)(2,1)S(1)}) custom-call(bf16[896,4096]{1,0:T(8,128)(2,1)} %bitcast.15, bf16[896,4096]{1,0:T(8,128)(2,1)} %bitcast.16), custom_call_target="tpu_custom_call" | custom-call | bytes 14680064 | tf_op jit(solution)/shard_map/load/pallas_call | solution.py:160
  33.2 0.5 collective-permute-start.17
  33.8 0.4 collective-permute-start.19
  34.3 5.3 %student_forward.1 = (bf16[896,4096]{1,0:T(8,128)(2,1)S(1)}, bf16[128,4096]{1,0:T(8,128)(2,1)S(1)}, f32[896,128]{1,0:T(8,128)S(1)}, f32[896,128]{1,0:T(8,128)S(1...) custom-call(bf16[16,4096]{1,0:T(8,128)(2,1)S(1)} %bitcast.14, ...), custom_call_target="tpu_custom_call" | custom-call | flops 2818572288 | bytes 22020096 | tf_op jit(solution)/shard_map/student_forward/pallas_call | solution.py:228
  39.6 0.5 collective-permute-start.7
  40.1 5.2 %teacher_forward.1 = (f32[64,2048]{1,0:T(8,128)S(1)}, bf16[64,2048]{1,0:T(8,128)(2,1)S(1)}, f32[64,2048]{1,0:T(8,128)S(1)}, bf16[64,2048]{1,0:T(8,128)(2,1)S(1)}) custom-call(bf16[16,4096]{1,0:T(8,128)(2,1)S(1)} %shard_map.77.refs_0_, bf16[16,4096]{1,0:T(8,128)(2,1)S(1)} %collective-permute-done.14.refs_1_, ...), custom_call_target="tpu_custom_call" | custom-call | flops 2818572288 | bytes 22020096 | tf_op jit(solution)/shard_map/teacher_forward/pallas_call | solution.py:228
  45.9 1.0 collective-permute-done.21.other
  47.0 2.9 %collective-permute-start.22 = (bf16[16,2048]{1,0:T(8,128)(2,1)S(1)}, bf16[16,2048]{1,0:T(8,128)(2,1)S(1)}, u32[]{:S(2)}, u32[]{:S(2)}) collective-permute-start(bf16[16,2048]{1,0:T(8,128)(2,1)S(1)} %get-tuple-element.45), channel_id=1, source_target_pairs={{0,2},{1,3},{2,0},{3,1},{4,6},{5,7},{6,4},{7,5},{8,10},{9,11},{10,... | collective-permute-start | bytes 196616 | tf_op jit(solution)/shard_map/ppermute | solution.py:36
  49.9 1.1 %collective-permute-start.23 = (bf16[16,2048]{1,0:T(8,128)(2,1)S(1)}, bf16[16,2048]{1,0:T(8,128)(2,1)S(1)}, u32[]{:S(2)}, u32[]{:S(2)}) collective-permute-start(bf16[16,2048]{1,0:T(8,128)(2,1)S(1)} %get-tuple-element.46), channel_id=1, source_target_pairs={{0,4},{1,5},{2,6},{3,7},{4,0},{5,1},{6,2},{7,3},{8,12},{9,13},{10,... | collective-permute-start | bytes 196616 | tf_op jit(solution)/shard_map/ppermute | solution.py:36
  51.0 1.4 %collective-permute-start.24 = (bf16[16,2048]{1,0:T(8,128)(2,1)S(1)}, bf16[16,2048]{1,0:T(8,128)(2,1)S(1)}, u32[]{:S(2)}, u32[]{:S(2)}) collective-permute-start(bf16[16,2048]{1,0:T(8,128)(2,1)S(1)} %get-tuple-element.47), channel_id=1, source_target_pairs={{0,6},{1,7},{2,4},{3,5},{4,2},{5,3},{6,0},{7,1},{8,14},{9,15},{10,... | collective-permute-start | bytes 196616 | tf_op jit(solution)/shard_map/ppermute | solution.py:36
  52.4 1.1 %collective-permute-start.36 = (bf16[16,2048]{1,0:T(8,128)(2,1)S(1)}, bf16[16,2048]{1,0:T(8,128)(2,1)S(1)}, u32[]{:S(2)}, u32[]{:S(2)}) collective-permute-start(bf16[16,2048]{1,0:T(8,128)(2,1)S(1)} %get-tuple-element.52), channel_id=1, source_target_pairs={{0,2},{1,3},{2,0},{3,1},{4,6},{5,7},{6,4},{7,5},{8,10},{9,11},{10,... | collective-permute-start | bytes 196616 | tf_op jit(solution)/shard_map/ppermute | solution.py:36
  53.5 2.2 %collective-permute-start.37 = (bf16[16,2048]{1,0:T(8,128)(2,1)S(1)}, bf16[16,2048]{1,0:T(8,128)(2,1)S(1)}, u32[]{:S(2)}, u32[]{:S(2)}) collective-permute-start(bf16[16,2048]{1,0:T(8,128)(2,1)S(1)} %get-tuple-element.53), channel_id=1, source_target_pairs={{0,4},{1,5},{2,6},{3,7},{4,0},{5,1},{6,2},{7,3},{8,12},{9,13},{10,... | collective-permute-start | bytes 196616 | tf_op jit(solution)/shard_map/ppermute | solution.py:36
  55.8 2.5 %collective-permute-done.23.refs_2_ = bf16[16,2048]{1,0:T(8,128)(2,1)S(1)} collective-permute-done((bf16[16,2048]{1,0:T(8,128)(2,1)S(1)}, bf16[16,2048]{1,0:T(8,128)(2,1)S(1)}, u32[]{:S(2)}, u32[]{:S(2)}) %collective-permute-start.23) | collective-permute-done | bytes 65568 | tf_op jit(solution)/shard_map/ppermute | solution.py:36
  58.2 2.6 %collective-permute-start.38 = (bf16[16,2048]{1,0:T(8,128)(2,1)S(1)}, bf16[16,2048]{1,0:T(8,128)(2,1)S(1)}, u32[]{:S(2)}, u32[]{:S(2)}) collective-permute-start(bf16[16,2048]{1,0:T(8,128)(2,1)S(1)} %get-tuple-element.54), channel_id=1, source_target_pairs={{0,6},{1,7},{2,4},{3,5},{4,2},{5,3},{6,0},{7,1},{8,14},{9,15},{10,... | collective-permute-start | bytes 196616 | tf_op jit(solution)/shard_map/ppermute | solution.py:36
  60.8 2.5 %collective-permute-start.27 = (bf16[16,2048]{1,0:T(8,128)(2,1)S(1)}, bf16[16,2048]{1,0:T(8,128)(2,1)S(1)}, u32[]{:S(2)}, u32[]{:S(2)}) collective-permute-start(bf16[16,2048]{1,0:T(8,128)(2,1)S(1)} %shard_map.79), channel_id=1, source_target_pairs={{24,0},{16,8},{8,16},{0,24},{25,1},{17,9},{9,17},{1,25},{26,2},{18... | collective-permute-start | bytes 196616 | tf_op jit(solution)/shard_map/ppermute | solution.py:27
  63.4 1.5 %collective-permute-start.8 = (bf16[16,4096]{1,0:T(8,128)(2,1)S(1)}, bf16[16,4096]{1,0:T(8,128)(2,1)S(1)}, u32[]{:S(2)}, u32[]{:S(2)}) collective-permute-start(bf16[16,4096]{1,0:T(8,128)(2,1)S(1)} %get-tuple-element.38), channel_id=1, source_target_pairs={{0,2},{1,3},{2,0},{3,1},{4,6},{5,7},{6,4},{7,5},{8,10},{9,11},{10,... | collective-permute-start | bytes 393224 | tf_op jit(solution)/shard_map/ppermute | solution.py:36
  65.2 2.6 %collective-permute-start.10 = (bf16[16,4096]{1,0:T(8,128)(2,1)S(1)}, bf16[16,4096]{1,0:T(8,128)(2,1)S(1)}, u32[]{:S(2)}, u32[]{:S(2)}) collective-permute-start(bf16[16,4096]{1,0:T(8,128)(2,1)S(1)} %get-tuple-element.40), channel_id=1, source_target_pairs={{0,6},{1,7},{2,4},{3,5},{4,2},{5,3},{6,0},{7,1},{8,14},{9,15},{10,... | collective-permute-start | bytes 393224 | tf_op jit(solution)/shard_map/ppermute | solution.py:36
  67.8 0.6 collective-permute-start.26
  68.4 0.5 collective-permute-start.25
  69.0 4.2 %collective-permute-done.26.refs_5_ = bf16[16,2048]{1,0:T(8,128)(2,1)S(1)} collective-permute-done((bf16[16,2048]{1,0:T(8,128)(2,1)S(1)}, bf16[16,2048]{1,0:T(8,128)(2,1)S(1)}, u32[]{:S(2)}, u32[]{:S(2)}) %collective-permute-start.26) | collective-permute-done | bytes 65568 | tf_op jit(solution)/shard_map/ppermute | solution.py:27
  73.2 1.6 %collective-permute-start.40 = (bf16[16,2048]{1,0:T(8,128)(2,1)S(1)}, bf16[16,2048]{1,0:T(8,128)(2,1)S(1)}, u32[]{:S(2)}, u32[]{:S(2)}) collective-permute-start(bf16[16,2048]{1,0:T(8,128)(2,1)S(1)} %shard_map.82), channel_id=1, source_target_pairs={{16,0},{24,8},{0,16},{8,24},{17,1},{25,9},{1,17},{9,25},{18,2},{26... | collective-permute-start | bytes 196616 | tf_op jit(solution)/shard_map/ppermute | solution.py:27
  74.8 1.9 %collective-permute-start.39 = (bf16[16,2048]{1,0:T(8,128)(2,1)S(1)}, bf16[16,2048]{1,0:T(8,128)(2,1)S(1)}, u32[]{:S(2)}, u32[]{:S(2)}) collective-permute-start(bf16[16,2048]{1,0:T(8,128)(2,1)S(1)} %shard_map.82), channel_id=1, source_target_pairs={{8,0},{0,8},{24,16},{16,24},{9,1},{1,9},{25,17},{17,25},{10,2},{2,... | collective-permute-start | bytes 196616 | tf_op jit(solution)/shard_map/ppermute | solution.py:27
  76.7 0.6 shard_map.80.refs_0_
  77.3 0.7 collective-permute-start.30
  78.0 1.9 %collective-permute-start.29 = (bf16[16,2048]{1,0:T(8,128)(2,1)S(1)}, bf16[16,2048]{1,0:T(8,128)(2,1)S(1)}, u32[]{:S(2)}, u32[]{:S(2)}) collective-permute-start(bf16[16,2048]{1,0:T(8,128)(2,1)S(1)} %shard_map.80.refs_0_), channel_id=1, source_target_pairs={{4,0},{5,1},{6,2},{7,3},{0,4},{1,5},{2,6},{3,7},{12,8},{13,9},{14,... | collective-permute-start | bytes 196616 | tf_op jit(solution)/shard_map/ppermute | solution.py:27
  79.9 0.6 shard_map.83.refs_0_
  80.5 2.7 %collective-permute-start.44 = (bf16[16,2048]{1,0:T(8,128)(2,1)S(1)}, bf16[16,2048]{1,0:T(8,128)(2,1)S(1)}, u32[]{:S(2)}, u32[]{:S(2)}) collective-permute-start(bf16[16,2048]{1,0:T(8,128)(2,1)S(1)} %shard_map.83.refs_0_), channel_id=1, source_target_pairs={{6,0},{7,1},{4,2},{5,3},{2,4},{3,5},{0,6},{1,7},{14,8},{15,9},{12,... | collective-permute-start | bytes 196616 | tf_op jit(solution)/shard_map/ppermute | solution.py:27
  83.2 0.9 collective-permute-start.43
  84.1 1.1 %collective-permute-start.42 = (bf16[16,2048]{1,0:T(8,128)(2,1)S(1)}, bf16[16,2048]{1,0:T(8,128)(2,1)S(1)}, u32[]{:S(2)}, u32[]{:S(2)}) collective-permute-start(bf16[16,2048]{1,0:T(8,128)(2,1)S(1)} %shard_map.83.refs_0_), channel_id=1, source_target_pairs={{2,0},{3,1},{0,2},{1,3},{6,4},{7,5},{4,6},{5,7},{10,8},{11,9},{8,1... | collective-permute-start | bytes 196616 | tf_op jit(solution)/shard_map/ppermute | solution.py:27
  85.1 0.9 collective-permute-start.28
  86.1 2.6 %collective-permute-done.29.refs_2_ = bf16[16,2048]{1,0:T(8,128)(2,1)S(1)} collective-permute-done((bf16[16,2048]{1,0:T(8,128)(2,1)S(1)}, bf16[16,2048]{1,0:T(8,128)(2,1)S(1)}, u32[]{:S(2)}, u32[]{:S(2)}) %collective-permute-start.29) | collective-permute-done | bytes 65568 | tf_op jit(solution)/shard_map/ppermute | solution.py:27
  88.7 0.5 collective-permute-start.48
  89.2 1.5 %collective-permute-done.43.refs_2_ = bf16[16,2048]{1,0:T(8,128)(2,1)S(1)} collective-permute-done((bf16[16,2048]{1,0:T(8,128)(2,1)S(1)}, bf16[16,2048]{1,0:T(8,128)(2,1)S(1)}, u32[]{:S(2)}, u32[]{:S(2)}) %collective-permute-start.43) | collective-permute-done | bytes 65568 | tf_op jit(solution)/shard_map/ppermute | solution.py:27
  90.7 0.5 collective-permute-start.46
  91.3 0.4 collective-permute-start.34
  92.2 2.4 %shard_map.84 = (bf16[896,4096]{1,0:T(8,128)(2,1)}, f32[896,128]{1,0:T(8,128)S(1)}) custom-call(bf16[16,2048]{1,0:T(8,128)(2,1)S(1)} %shard_map.83.refs_0_, bf16[16,2048]{1,0:T(8,128)(2,1)S(1)} %collective-permute-done.42.refs_1_, bf16[16,2048]{1,0:T(8,128)(2,1)S(1)} %collective-permute-done.43.refs_2_, ...), custom_call_target="tpu_custom_call" | custom-call | flops 939524096 | bytes 7340032 | tf_op jit(solution)/shard_map/pallas_call | solution.py:326
  94.7 8.2 %shard_map.85 = (bf16[896,4096]{1,0:T(8,128)(2,1)}, bf16[896,4096]{1,0:T(8,128)(2,1)}, bf16[896,4096]{1,0:T(8,128)(2,1)}) custom-call(bf16[16,2048]{1,0:T(8,128)(2,1)S(1)} %shard_map.80.refs_0_, bf16[16,2048]{1,0:T(8,128)(2,1)S(1)} %collective-permute-done.28.refs_1_, ...), custom_call_target="tpu_custom_call", output_to_operand_aliasing={{0}: (11, {})} | custom-call | flops 2818572288 | bytes 22020096 | tf_op jit(solution)/shard_map/pallas_call | solution.py:326
  (67 shorter events, 2.5 us)
Async XLA Ops:
  0.6 8.6 %collective-permute-start.13 = (bf16[16,4096]{1,0:T(8,128)(2,1)}, bf16[16,4096]{1,0:T(8,128)(2,1)S(1)}, u32[]{:S(2)}, u32[]{:S(2)}) collective-permute-start(bf16[16,4096]{1,0:T(8,128)(2,1)} %bitcast.7), channel_id=1, source_target_pairs={{24,0},{16,8},{8,16},{0,24},{25,1},{17,9},{9,17},{1,25},{26,2},{18... | collective-permute-start | bytes 393224 | tf_op jit(solution)/shard_map/ppermute | solution.py:27
  4.6 6.8 %collective-permute-start.12 = (bf16[16,4096]{1,0:T(8,128)(2,1)}, bf16[16,4096]{1,0:T(8,128)(2,1)S(1)}, u32[]{:S(2)}, u32[]{:S(2)}) collective-permute-start(bf16[16,4096]{1,0:T(8,128)(2,1)} %bitcast.8), channel_id=1, source_target_pairs={{16,0},{24,8},{0,16},{8,24},{17,1},{25,9},{1,17},{9,25},{18,2},{26... | collective-permute-start | bytes 393224 | tf_op jit(solution)/shard_map/ppermute | solution.py:27
  5.1 7.9 %collective-permute-start.11 = (bf16[16,4096]{1,0:T(8,128)(2,1)}, bf16[16,4096]{1,0:T(8,128)(2,1)S(1)}, u32[]{:S(2)}, u32[]{:S(2)}) collective-permute-start(bf16[16,4096]{1,0:T(8,128)(2,1)} %bitcast.9), channel_id=1, source_target_pairs={{8,0},{0,8},{24,16},{16,24},{9,1},{1,9},{25,17},{17,25},{10,2},{2,... | collective-permute-start | bytes 393224 | tf_op jit(solution)/shard_map/ppermute | solution.py:27
  5.3 11.4 %collective-permute-start.3 = (bf16[16,4096]{1,0:T(8,128)(2,1)}, bf16[16,4096]{1,0:T(8,128)(2,1)S(1)}, u32[]{:S(2)}, u32[]{:S(2)}) collective-permute-start(bf16[16,4096]{1,0:T(8,128)(2,1)} %bitcast.10), channel_id=1, source_target_pairs={{0,1},{1,0},{2,3},{3,2},{4,5},{5,4},{6,7},{7,6},{8,9},{9,8},{10,11... | collective-permute-start | bytes 393224 | tf_op jit(solution)/shard_map/ppermute | solution.py:40
  5.3 11.6 %collective-permute-start.2 = (bf16[16,4096]{1,0:T(8,128)(2,1)}, bf16[16,4096]{1,0:T(8,128)(2,1)S(1)}, u32[]{:S(2)}, u32[]{:S(2)}) collective-permute-start(bf16[16,4096]{1,0:T(8,128)(2,1)} %bitcast.11), channel_id=1, source_target_pairs={{6,0},{7,1},{4,2},{5,3},{2,4},{3,5},{0,6},{1,7},{14,8},{15,9},{12,... | collective-permute-start | bytes 393224 | tf_op jit(solution)/shard_map/ppermute | solution.py:27
  9.3 18.1 %collective-permute-start.1 = (bf16[16,4096]{1,0:T(8,128)(2,1)}, bf16[16,4096]{1,0:T(8,128)(2,1)S(1)}, u32[]{:S(2)}, u32[]{:S(2)}) collective-permute-start(bf16[16,4096]{1,0:T(8,128)(2,1)} %bitcast.12), channel_id=1, source_target_pairs={{4,0},{5,1},{6,2},{7,3},{0,4},{1,5},{2,6},{3,7},{12,8},{13,9},{14,... | collective-permute-start | bytes 393224 | tf_op jit(solution)/shard_map/ppermute | solution.py:27
  11.5 15.9 %collective-permute-start = (bf16[16,4096]{1,0:T(8,128)(2,1)}, bf16[16,4096]{1,0:T(8,128)(2,1)S(1)}, u32[]{:S(2)}, u32[]{:S(2)}) collective-permute-start(bf16[16,4096]{1,0:T(8,128)(2,1)} %bitcast.13), channel_id=1, source_target_pairs={{2,0},{3,1},{0,2},{1,3},{6,4},{7,5},{4,6},{5,7},{10,8},{11,9},{8,1... | collective-permute-start | bytes 393224 | tf_op jit(solution)/shard_map/ppermute | solution.py:27
  14.3 13.6 %collective-permute-start.16 = (bf16[16,4096]{1,0:T(8,128)(2,1)S(1)}, bf16[16,4096]{1,0:T(8,128)(2,1)S(1)}, u32[]{:S(2)}, u32[]{:S(2)}) collective-permute-start(bf16[16,4096]{1,0:T(8,128)(2,1)S(1)} %shard_map.77.refs_0_), channel_id=1, source_target_pairs={{6,0},{7,1},{4,2},{5,3},{2,4},{3,5},{0,6},{1,7},{14,8},{15,9},{12,... | collective-permute-start | bytes 393224 | tf_op jit(solution)/shard_map/ppermute | solution.py:27
  16.7 16.5 %collective-permute-start.15 = (bf16[16,4096]{1,0:T(8,128)(2,1)S(1)}, bf16[16,4096]{1,0:T(8,128)(2,1)S(1)}, u32[]{:S(2)}, u32[]{:S(2)}) collective-permute-start(bf16[16,4096]{1,0:T(8,128)(2,1)S(1)} %shard_map.77.refs_0_), channel_id=1, source_target_pairs={{4,0},{5,1},{6,2},{7,3},{0,4},{1,5},{2,6},{3,7},{12,8},{13,9},{14,... | collective-permute-start | bytes 393224 | tf_op jit(solution)/shard_map/ppermute | solution.py:27
  16.9 16.8 %collective-permute-start.14 = (bf16[16,4096]{1,0:T(8,128)(2,1)S(1)}, bf16[16,4096]{1,0:T(8,128)(2,1)S(1)}, u32[]{:S(2)}, u32[]{:S(2)}) collective-permute-start(bf16[16,4096]{1,0:T(8,128)(2,1)S(1)} %shard_map.77.refs_0_), channel_id=1, source_target_pairs={{2,0},{3,1},{0,2},{1,3},{6,4},{7,5},{4,6},{5,7},{10,8},{11,9},{8,1... | collective-permute-start | bytes 393224 | tf_op jit(solution)/shard_map/ppermute | solution.py:27
  27.3 6.4 %collective-permute-start.6 = (bf16[16,4096]{1,0:T(8,128)(2,1)S(1)}, bf16[16,4096]{1,0:T(8,128)(2,1)S(1)}, u32[]{:S(2)}, u32[]{:S(2)}) collective-permute-start(bf16[16,4096]{1,0:T(8,128)(2,1)S(1)} %collective-permute-done.2.refs_3_), channel_id=1, source_target_pairs={{0,1},{1,0},{2,3},{3,2},{4,5},{5,4},{6,7},{7,6},{8,9},{9,8},{10,11... | collective-permute-start | bytes 393224 | tf_op jit(solution)/shard_map/ppermute | solution.py:40
  27.4 6.9 %collective-permute-start.5 = (bf16[16,4096]{1,0:T(8,128)(2,1)S(1)}, bf16[16,4096]{1,0:T(8,128)(2,1)S(1)}, u32[]{:S(2)}, u32[]{:S(2)}) collective-permute-start(bf16[16,4096]{1,0:T(8,128)(2,1)S(1)} %collective-permute-done.1.refs_2_), channel_id=1, source_target_pairs={{0,1},{1,0},{2,3},{3,2},{4,5},{5,4},{6,7},{7,6},{8,9},{9,8},{10,11... | collective-permute-start | bytes 393224 | tf_op jit(solution)/shard_map/ppermute | solution.py:40
  27.9 6.4 %collective-permute-start.4 = (bf16[16,4096]{1,0:T(8,128)(2,1)S(1)}, bf16[16,4096]{1,0:T(8,128)(2,1)S(1)}, u32[]{:S(2)}, u32[]{:S(2)}) collective-permute-start(bf16[16,4096]{1,0:T(8,128)(2,1)S(1)} %collective-permute-done.refs_1_), channel_id=1, source_target_pairs={{0,1},{1,0},{2,3},{3,2},{4,5},{5,4},{6,7},{7,6},{8,9},{9,8},{10,11... | collective-permute-start | bytes 393224 | tf_op jit(solution)/shard_map/ppermute | solution.py:40
  33.2 6.9 %collective-permute-start.17 = (bf16[16,4096]{1,0:T(8,128)(2,1)S(1)}, bf16[16,4096]{1,0:T(8,128)(2,1)S(1)}, u32[]{:S(2)}, u32[]{:S(2)}) collective-permute-start(bf16[16,4096]{1,0:T(8,128)(2,1)S(1)} %shard_map.77.refs_0_), channel_id=1, source_target_pairs={{0,1},{1,0},{2,3},{3,2},{4,5},{5,4},{6,7},{7,6},{8,9},{9,8},{10,11... | collective-permute-start | bytes 393224 | tf_op jit(solution)/shard_map/ppermute | solution.py:40
  33.7 6.4 %collective-permute-start.20 = (bf16[16,4096]{1,0:T(8,128)(2,1)S(1)}, bf16[16,4096]{1,0:T(8,128)(2,1)S(1)}, u32[]{:S(2)}, u32[]{:S(2)}) collective-permute-start(bf16[16,4096]{1,0:T(8,128)(2,1)S(1)} %collective-permute-done.16.refs_3_), channel_id=1, source_target_pairs={{0,1},{1,0},{2,3},{3,2},{4,5},{5,4},{6,7},{7,6},{8,9},{9,8},{10,11... | collective-permute-start | bytes 393224 | tf_op jit(solution)/shard_map/ppermute | solution.py:40
  33.8 6.3 %collective-permute-start.19 = (bf16[16,4096]{1,0:T(8,128)(2,1)S(1)}, bf16[16,4096]{1,0:T(8,128)(2,1)S(1)}, u32[]{:S(2)}, u32[]{:S(2)}) collective-permute-start(bf16[16,4096]{1,0:T(8,128)(2,1)S(1)} %collective-permute-done.15.refs_2_), channel_id=1, source_target_pairs={{0,1},{1,0},{2,3},{3,2},{4,5},{5,4},{6,7},{7,6},{8,9},{9,8},{10,11... | collective-permute-start | bytes 393224 | tf_op jit(solution)/shard_map/ppermute | solution.py:40
  34.2 5.9 %collective-permute-start.18 = (bf16[16,4096]{1,0:T(8,128)(2,1)S(1)}, bf16[16,4096]{1,0:T(8,128)(2,1)S(1)}, u32[]{:S(2)}, u32[]{:S(2)}) collective-permute-start(bf16[16,4096]{1,0:T(8,128)(2,1)S(1)} %collective-permute-done.14.refs_1_), channel_id=1, source_target_pairs={{0,1},{1,0},{2,3},{3,2},{4,5},{5,4},{6,7},{7,6},{8,9},{9,8},{10,11... | collective-permute-start | bytes 393224 | tf_op jit(solution)/shard_map/ppermute | solution.py:40
  39.6 23.7 %collective-permute-start.7 = (bf16[64,4096]{1,0:T(8,128)(2,1)S(1)}, bf16[64,4096]{1,0:T(8,128)(2,1)S(1)}, u32[]{:S(2)}, u32[]{:S(2)}) collective-permute-start(bf16[64,4096]{1,0:T(8,128)(2,1)S(1)} %get-tuple-element.36), channel_id=1, source_target_pairs={{0,1},{1,0},{2,3},{3,2},{4,5},{5,4},{6,7},{7,6},{8,9},{9,8},{10,11... | collective-permute-start | bytes 1572872 | tf_op jit(solution)/shard_map/ppermute | solution.py:40
  45.3 1.6 %collective-permute-start.21 = (bf16[64,2048]{1,0:T(8,128)(2,1)S(1)}, bf16[64,2048]{1,0:T(8,128)(2,1)S(1)}, u32[]{:S(2)}, u32[]{:S(2)}) collective-permute-start(bf16[64,2048]{1,0:T(8,128)(2,1)S(1)} %get-tuple-element.43), channel_id=1, source_target_pairs={{0,1},{1,0},{2,3},{3,2},{4,5},{5,4},{6,7},{7,6},{8,9},{9,8},{10,11... | collective-permute-start | bytes 786440 | tf_op jit(solution)/shard_map/ppermute | solution.py:40
  45.5 6.9 %collective-permute-start.35 = (bf16[64,2048]{1,0:T(8,128)(2,1)S(1)}, bf16[64,2048]{1,0:T(8,128)(2,1)S(1)}, u32[]{:S(2)}, u32[]{:S(2)}) collective-permute-start(bf16[64,2048]{1,0:T(8,128)(2,1)S(1)} %get-tuple-element.50), channel_id=1, source_target_pairs={{0,1},{1,0},{2,3},{3,2},{4,5},{5,4},{6,7},{7,6},{8,9},{9,8},{10,11... | collective-permute-start | bytes 786440 | tf_op jit(solution)/shard_map/ppermute | solution.py:40
  47.0 6.5 %collective-permute-start.22 = (bf16[16,2048]{1,0:T(8,128)(2,1)S(1)}, bf16[16,2048]{1,0:T(8,128)(2,1)S(1)}, u32[]{:S(2)}, u32[]{:S(2)}) collective-permute-start(bf16[16,2048]{1,0:T(8,128)(2,1)S(1)} %get-tuple-element.45), channel_id=1, source_target_pairs={{0,2},{1,3},{2,0},{3,1},{4,6},{5,7},{6,4},{7,5},{8,10},{9,11},{10,... | collective-permute-start | bytes 196616 | tf_op jit(solution)/shard_map/ppermute | solution.py:36
  49.9 8.3 %collective-permute-start.23 = (bf16[16,2048]{1,0:T(8,128)(2,1)S(1)}, bf16[16,2048]{1,0:T(8,128)(2,1)S(1)}, u32[]{:S(2)}, u32[]{:S(2)}) collective-permute-start(bf16[16,2048]{1,0:T(8,128)(2,1)S(1)} %get-tuple-element.46), channel_id=1, source_target_pairs={{0,4},{1,5},{2,6},{3,7},{4,0},{5,1},{6,2},{7,3},{8,12},{9,13},{10,... | collective-permute-start | bytes 196616 | tf_op jit(solution)/shard_map/ppermute | solution.py:36
  51.0 9.8 %collective-permute-start.24 = (bf16[16,2048]{1,0:T(8,128)(2,1)S(1)}, bf16[16,2048]{1,0:T(8,128)(2,1)S(1)}, u32[]{:S(2)}, u32[]{:S(2)}) collective-permute-start(bf16[16,2048]{1,0:T(8,128)(2,1)S(1)} %get-tuple-element.47), channel_id=1, source_target_pairs={{0,6},{1,7},{2,4},{3,5},{4,2},{5,3},{6,0},{7,1},{8,14},{9,15},{10,... | collective-permute-start | bytes 196616 | tf_op jit(solution)/shard_map/ppermute | solution.py:36
  52.4 12.4 %collective-permute-start.36 = (bf16[16,2048]{1,0:T(8,128)(2,1)S(1)}, bf16[16,2048]{1,0:T(8,128)(2,1)S(1)}, u32[]{:S(2)}, u32[]{:S(2)}) collective-permute-start(bf16[16,2048]{1,0:T(8,128)(2,1)S(1)} %get-tuple-element.52), channel_id=1, source_target_pairs={{0,2},{1,3},{2,0},{3,1},{4,6},{5,7},{6,4},{7,5},{8,10},{9,11},{10,... | collective-permute-start | bytes 196616 | tf_op jit(solution)/shard_map/ppermute | solution.py:36
  53.5 11.7 %collective-permute-start.37 = (bf16[16,2048]{1,0:T(8,128)(2,1)S(1)}, bf16[16,2048]{1,0:T(8,128)(2,1)S(1)}, u32[]{:S(2)}, u32[]{:S(2)}) collective-permute-start(bf16[16,2048]{1,0:T(8,128)(2,1)S(1)} %get-tuple-element.53), channel_id=1, source_target_pairs={{0,4},{1,5},{2,6},{3,7},{4,0},{5,1},{6,2},{7,3},{8,12},{9,13},{10,... | collective-permute-start | bytes 196616 | tf_op jit(solution)/shard_map/ppermute | solution.py:36
  58.2 9.6 %collective-permute-start.38 = (bf16[16,2048]{1,0:T(8,128)(2,1)S(1)}, bf16[16,2048]{1,0:T(8,128)(2,1)S(1)}, u32[]{:S(2)}, u32[]{:S(2)}) collective-permute-start(bf16[16,2048]{1,0:T(8,128)(2,1)S(1)} %get-tuple-element.54), channel_id=1, source_target_pairs={{0,6},{1,7},{2,4},{3,5},{4,2},{5,3},{6,0},{7,1},{8,14},{9,15},{10,... | collective-permute-start | bytes 196616 | tf_op jit(solution)/shard_map/ppermute | solution.py:36
  60.8 7.6 %collective-permute-start.27 = (bf16[16,2048]{1,0:T(8,128)(2,1)S(1)}, bf16[16,2048]{1,0:T(8,128)(2,1)S(1)}, u32[]{:S(2)}, u32[]{:S(2)}) collective-permute-start(bf16[16,2048]{1,0:T(8,128)(2,1)S(1)} %shard_map.79), channel_id=1, source_target_pairs={{24,0},{16,8},{8,16},{0,24},{25,1},{17,9},{9,17},{1,25},{26,2},{18... | collective-permute-start | bytes 196616 | tf_op jit(solution)/shard_map/ppermute | solution.py:27
  63.4 11.5 %collective-permute-start.8 = (bf16[16,4096]{1,0:T(8,128)(2,1)S(1)}, bf16[16,4096]{1,0:T(8,128)(2,1)S(1)}, u32[]{:S(2)}, u32[]{:S(2)}) collective-permute-start(bf16[16,4096]{1,0:T(8,128)(2,1)S(1)} %get-tuple-element.38), channel_id=1, source_target_pairs={{0,2},{1,3},{2,0},{3,1},{4,6},{5,7},{6,4},{7,5},{8,10},{9,11},{10,... | collective-permute-start | bytes 393224 | tf_op jit(solution)/shard_map/ppermute | solution.py:36
  64.9 11.8 %collective-permute-start.9 = (bf16[16,4096]{1,0:T(8,128)(2,1)S(1)}, bf16[16,4096]{1,0:T(8,128)(2,1)S(1)}, u32[]{:S(2)}, u32[]{:S(2)}) collective-permute-start(bf16[16,4096]{1,0:T(8,128)(2,1)S(1)} %get-tuple-element.39), channel_id=1, source_target_pairs={{0,4},{1,5},{2,6},{3,7},{4,0},{5,1},{6,2},{7,3},{8,12},{9,13},{10,... | collective-permute-start | bytes 393224 | tf_op jit(solution)/shard_map/ppermute | solution.py:36
  65.2 11.5 %collective-permute-start.10 = (bf16[16,4096]{1,0:T(8,128)(2,1)S(1)}, bf16[16,4096]{1,0:T(8,128)(2,1)S(1)}, u32[]{:S(2)}, u32[]{:S(2)}) collective-permute-start(bf16[16,4096]{1,0:T(8,128)(2,1)S(1)} %get-tuple-element.40), channel_id=1, source_target_pairs={{0,6},{1,7},{2,4},{3,5},{4,2},{5,3},{6,0},{7,1},{8,14},{9,15},{10,... | collective-permute-start | bytes 393224 | tf_op jit(solution)/shard_map/ppermute | solution.py:36
  67.8 5.4 %collective-permute-start.26 = (bf16[16,2048]{1,0:T(8,128)(2,1)S(1)}, bf16[16,2048]{1,0:T(8,128)(2,1)S(1)}, u32[]{:S(2)}, u32[]{:S(2)}) collective-permute-start(bf16[16,2048]{1,0:T(8,128)(2,1)S(1)} %shard_map.79), channel_id=1, source_target_pairs={{16,0},{24,8},{0,16},{8,24},{17,1},{25,9},{1,17},{9,25},{18,2},{26... | collective-permute-start | bytes 196616 | tf_op jit(solution)/shard_map/ppermute | solution.py:27
  68.4 4.8 %collective-permute-start.25 = (bf16[16,2048]{1,0:T(8,128)(2,1)S(1)}, bf16[16,2048]{1,0:T(8,128)(2,1)S(1)}, u32[]{:S(2)}, u32[]{:S(2)}) collective-permute-start(bf16[16,2048]{1,0:T(8,128)(2,1)S(1)} %shard_map.79), channel_id=1, source_target_pairs={{8,0},{0,8},{24,16},{16,24},{9,1},{1,9},{25,17},{17,25},{10,2},{2,... | collective-permute-start | bytes 196616 | tf_op jit(solution)/shard_map/ppermute | solution.py:27
  73.2 6.7 %collective-permute-start.41 = (bf16[16,2048]{1,0:T(8,128)(2,1)S(1)}, bf16[16,2048]{1,0:T(8,128)(2,1)S(1)}, u32[]{:S(2)}, u32[]{:S(2)}) collective-permute-start(bf16[16,2048]{1,0:T(8,128)(2,1)S(1)} %shard_map.82), channel_id=1, source_target_pairs={{24,0},{16,8},{8,16},{0,24},{25,1},{17,9},{9,17},{1,25},{26,2},{18... | collective-permute-start | bytes 196616 | tf_op jit(solution)/shard_map/ppermute | solution.py:27
  73.2 6.7 %collective-permute-start.40 = (bf16[16,2048]{1,0:T(8,128)(2,1)S(1)}, bf16[16,2048]{1,0:T(8,128)(2,1)S(1)}, u32[]{:S(2)}, u32[]{:S(2)}) collective-permute-start(bf16[16,2048]{1,0:T(8,128)(2,1)S(1)} %shard_map.82), channel_id=1, source_target_pairs={{16,0},{24,8},{0,16},{8,24},{17,1},{25,9},{1,17},{9,25},{18,2},{26... | collective-permute-start | bytes 196616 | tf_op jit(solution)/shard_map/ppermute | solution.py:27
  74.8 5.1 %collective-permute-start.39 = (bf16[16,2048]{1,0:T(8,128)(2,1)S(1)}, bf16[16,2048]{1,0:T(8,128)(2,1)S(1)}, u32[]{:S(2)}, u32[]{:S(2)}) collective-permute-start(bf16[16,2048]{1,0:T(8,128)(2,1)S(1)} %shard_map.82), channel_id=1, source_target_pairs={{8,0},{0,8},{24,16},{16,24},{9,1},{1,9},{25,17},{17,25},{10,2},{2,... | collective-permute-start | bytes 196616 | tf_op jit(solution)/shard_map/ppermute | solution.py:27
  77.3 7.9 %collective-permute-start.30 = (bf16[16,2048]{1,0:T(8,128)(2,1)S(1)}, bf16[16,2048]{1,0:T(8,128)(2,1)S(1)}, u32[]{:S(2)}, u32[]{:S(2)}) collective-permute-start(bf16[16,2048]{1,0:T(8,128)(2,1)S(1)} %shard_map.80.refs_0_), channel_id=1, source_target_pairs={{6,0},{7,1},{4,2},{5,3},{2,4},{3,5},{0,6},{1,7},{14,8},{15,9},{12,... | collective-permute-start | bytes 196616 | tf_op jit(solution)/shard_map/ppermute | solution.py:27
  78.0 10.8 %collective-permute-start.29 = (bf16[16,2048]{1,0:T(8,128)(2,1)S(1)}, bf16[16,2048]{1,0:T(8,128)(2,1)S(1)}, u32[]{:S(2)}, u32[]{:S(2)}) collective-permute-start(bf16[16,2048]{1,0:T(8,128)(2,1)S(1)} %shard_map.80.refs_0_), channel_id=1, source_target_pairs={{4,0},{5,1},{6,2},{7,3},{0,4},{1,5},{2,6},{3,7},{12,8},{13,9},{14,... | collective-permute-start | bytes 196616 | tf_op jit(solution)/shard_map/ppermute | solution.py:27
  80.5 8.2 %collective-permute-start.44 = (bf16[16,2048]{1,0:T(8,128)(2,1)S(1)}, bf16[16,2048]{1,0:T(8,128)(2,1)S(1)}, u32[]{:S(2)}, u32[]{:S(2)}) collective-permute-start(bf16[16,2048]{1,0:T(8,128)(2,1)S(1)} %shard_map.83.refs_0_), channel_id=1, source_target_pairs={{6,0},{7,1},{4,2},{5,3},{2,4},{3,5},{0,6},{1,7},{14,8},{15,9},{12,... | collective-permute-start | bytes 196616 | tf_op jit(solution)/shard_map/ppermute | solution.py:27
  83.2 7.5 %collective-permute-start.43 = (bf16[16,2048]{1,0:T(8,128)(2,1)S(1)}, bf16[16,2048]{1,0:T(8,128)(2,1)S(1)}, u32[]{:S(2)}, u32[]{:S(2)}) collective-permute-start(bf16[16,2048]{1,0:T(8,128)(2,1)S(1)} %shard_map.83.refs_0_), channel_id=1, source_target_pairs={{4,0},{5,1},{6,2},{7,3},{0,4},{1,5},{2,6},{3,7},{12,8},{13,9},{14,... | collective-permute-start | bytes 196616 | tf_op jit(solution)/shard_map/ppermute | solution.py:27
  84.1 6.6 %collective-permute-start.42 = (bf16[16,2048]{1,0:T(8,128)(2,1)S(1)}, bf16[16,2048]{1,0:T(8,128)(2,1)S(1)}, u32[]{:S(2)}, u32[]{:S(2)}) collective-permute-start(bf16[16,2048]{1,0:T(8,128)(2,1)S(1)} %shard_map.83.refs_0_), channel_id=1, source_target_pairs={{2,0},{3,1},{0,2},{1,3},{6,4},{7,5},{4,6},{5,7},{10,8},{11,9},{8,1... | collective-permute-start | bytes 196616 | tf_op jit(solution)/shard_map/ppermute | solution.py:27
  85.1 6.1 %collective-permute-start.28 = (bf16[16,2048]{1,0:T(8,128)(2,1)S(1)}, bf16[16,2048]{1,0:T(8,128)(2,1)S(1)}, u32[]{:S(2)}, u32[]{:S(2)}) collective-permute-start(bf16[16,2048]{1,0:T(8,128)(2,1)S(1)} %shard_map.80.refs_0_), channel_id=1, source_target_pairs={{2,0},{3,1},{0,2},{1,3},{6,4},{7,5},{4,6},{5,7},{10,8},{11,9},{8,1... | collective-permute-start | bytes 196616 | tf_op jit(solution)/shard_map/ppermute | solution.py:27
  88.7 2.6 %collective-permute-start.45 = (bf16[16,2048]{1,0:T(8,128)(2,1)S(1)}, bf16[16,2048]{1,0:T(8,128)(2,1)S(1)}, u32[]{:S(2)}, u32[]{:S(2)}) collective-permute-start(bf16[16,2048]{1,0:T(8,128)(2,1)S(1)} %shard_map.83.refs_0_), channel_id=1, source_target_pairs={{0,1},{1,0},{2,3},{3,2},{4,5},{5,4},{6,7},{7,6},{8,9},{9,8},{10,11... | collective-permute-start | bytes 196616 | tf_op jit(solution)/shard_map/ppermute | solution.py:40
  88.7 3.0 %collective-permute-start.48 = (bf16[16,2048]{1,0:T(8,128)(2,1)S(1)}, bf16[16,2048]{1,0:T(8,128)(2,1)S(1)}, u32[]{:S(2)}, u32[]{:S(2)}) collective-permute-start(bf16[16,2048]{1,0:T(8,128)(2,1)S(1)} %collective-permute-done.44.refs_3_), channel_id=1, source_target_pairs={{0,1},{1,0},{2,3},{3,2},{4,5},{5,4},{6,7},{7,6},{8,9},{9,8},{10,11... | collective-permute-start | bytes 196616 | tf_op jit(solution)/shard_map/ppermute | solution.py:40
  90.7 1.5 %collective-permute-start.46 = (bf16[16,2048]{1,0:T(8,128)(2,1)S(1)}, bf16[16,2048]{1,0:T(8,128)(2,1)S(1)}, u32[]{:S(2)}, u32[]{:S(2)}) collective-permute-start(bf16[16,2048]{1,0:T(8,128)(2,1)S(1)} %collective-permute-done.42.refs_1_), channel_id=1, source_target_pairs={{0,1},{1,0},{2,3},{3,2},{4,5},{5,4},{6,7},{7,6},{8,9},{9,8},{10,11... | collective-permute-start | bytes 196616 | tf_op jit(solution)/shard_map/ppermute | solution.py:40
  91.2 3.5 %collective-permute-start.31 = (bf16[16,2048]{1,0:T(8,128)(2,1)S(1)}, bf16[16,2048]{1,0:T(8,128)(2,1)S(1)}, u32[]{:S(2)}, u32[]{:S(2)}) collective-permute-start(bf16[16,2048]{1,0:T(8,128)(2,1)S(1)} %shard_map.80.refs_0_), channel_id=1, source_target_pairs={{0,1},{1,0},{2,3},{3,2},{4,5},{5,4},{6,7},{7,6},{8,9},{9,8},{10,11... | collective-permute-start | bytes 196616 | tf_op jit(solution)/shard_map/ppermute | solution.py:40
  91.3 3.4 %collective-permute-start.34 = (bf16[16,2048]{1,0:T(8,128)(2,1)S(1)}, bf16[16,2048]{1,0:T(8,128)(2,1)S(1)}, u32[]{:S(2)}, u32[]{:S(2)}) collective-permute-start(bf16[16,2048]{1,0:T(8,128)(2,1)S(1)} %collective-permute-done.30.refs_3_), channel_id=1, source_target_pairs={{0,1},{1,0},{2,3},{3,2},{4,5},{5,4},{6,7},{7,6},{8,9},{9,8},{10,11... | collective-permute-start | bytes 196616 | tf_op jit(solution)/shard_map/ppermute | solution.py:40
  91.7 3.0 %collective-permute-start.33 = (bf16[16,2048]{1,0:T(8,128)(2,1)S(1)}, bf16[16,2048]{1,0:T(8,128)(2,1)S(1)}, u32[]{:S(2)}, u32[]{:S(2)}) collective-permute-start(bf16[16,2048]{1,0:T(8,128)(2,1)S(1)} %collective-permute-done.29.refs_2_), channel_id=1, source_target_pairs={{0,1},{1,0},{2,3},{3,2},{4,5},{5,4},{6,7},{7,6},{8,9},{9,8},{10,11... | collective-permute-start | bytes 196616 | tf_op jit(solution)/shard_map/ppermute | solution.py:40
  91.9 2.8 %collective-permute-start.32 = (bf16[16,2048]{1,0:T(8,128)(2,1)S(1)}, bf16[16,2048]{1,0:T(8,128)(2,1)S(1)}, u32[]{:S(2)}, u32[]{:S(2)}) collective-permute-start(bf16[16,2048]{1,0:T(8,128)(2,1)S(1)} %collective-permute-done.28.refs_1_), channel_id=1, source_target_pairs={{0,1},{1,0},{2,3},{3,2},{4,5},{5,4},{6,7},{7,6},{8,9},{9,8},{10,11... | collective-permute-start | bytes 196616 | tf_op jit(solution)/shard_map/ppermute | solution.py:40
  (3 other events, 8.3 us)
where the time goes:
time: 103 us
  starting transfers between devices  53.3 us (52%)
  Pallas kernels  28.4 us (28%)
  waiting for transfers between devices  19.7 us (19%)
    ppermute x21, starting transfers between devices, fetch(): return lax.ppermute(value, axis, pairs)  33 us
    ppermute x21, waiting for transfers between devices, fetch(): return lax.ppermute(value, axis, pairs)  16.1 us
    ppermute x9, starting transfers between devices, give(): return lax.ppermute(value, axis, pairs)  15.7 us
    pallas_call x2, Pallas kernels, backward(): pl.pallas_call(functools.partial(backward_kernel, len(pieces), first, fin...  10.7 us
    pallas_call x2, Pallas kernels, forward(): pl.pallas_call(functools.partial(forward_kernel, len(pieces), chunks, kee...  10.5 us
    pallas_call x1, Pallas kernels, load(): pl.pallas_call(load_kernel, out_shape=[pltpu.VMEM(w.shape, w.dtype) for w...  5.22 us
    ppermute x19, starting transfers between devices, swap(): return lax.ppermute(value, 'fsdp', [(i, i ^ 1) for i in range(members)])  4.64 us
    ppermute x9, waiting for transfers between devices, give(): return lax.ppermute(value, axis, pairs)  2.47 us
  transfers between devices with their start and end apart: 49, of which 7 were waited for; matrix products, arithmetic and copies ran while one was open for 0% of the time, Pallas kernels for 20%

commit v1 on v0

--- a/solution.py
+++ b/solution.py
@@ -14,51 +14,81 @@
 VMEM = pl.BlockSpec(memory_space=pltpu.VMEM)
 
 
-def peer(index, step, count):
-    return index ^ step if count & (count - 1) == 0 else (index + step) % count
-
-
-def fetch(value, axis, step, count, stride=1):
+def exchange(value, axis, step, stride, count):
     pairs = [
-        (peer(i, step, count) * stride + low, i * stride + low)
-        for i in range(count)
-        for low in range(stride)
+        ((i ^ step) * stride + low, i * stride + low) for i in range(count) for low in range(stride)
     ]
     return lax.ppermute(value, axis, pairs)
 
 
-def give(value, axis, step, count, stride=1):
-    pairs = [
-        (i * stride + low, peer(i, step, count) * stride + low)
-        for i in range(count)
-        for low in range(stride)
-    ]
-    return lax.ppermute(value, axis, pairs)
+def levels(count):
+    assert count & (count - 1) == 0
+    return [1 << level for level in range(count.bit_length() - 1)]
+
+
+def arrangement(count):
+    order = [0]
+    for step in levels(count)[::-1]:
+        order += [held + step for held in order]
+    return order
 
 
 def swap(value, members):
     return lax.ppermute(value, "fsdp", [(i, i ^ 1) for i in range(members)])
 
 
-def gather_rows(rows, chips, members):
-    mine = [rows] + [fetch(rows, "fsdp", k, chips, 2) for k in range(1, chips)]
-    return mine + [swap(piece, members) for piece in mine]
-
-
-def scatter_rows(mine, theirs, chips, members):
+def gather_rows(rows, chips, members, relay=False):
+    mine, theirs = [rows], []
+    for step in arrangement(chips)[1:] if not relay else []:
+        mine.append(exchange(rows, "fsdp", step, 2, chips))
+    for step in levels(chips)[::-1] if relay else []:
+        fresh = []
+        for piece in mine:
+            fresh.append(exchange(piece, "fsdp", step, 2, chips))
+        mine += fresh
+    for step, piece in zip(arrangement(chips), mine):
+        theirs.append(swap(piece, members))
+    return mine + theirs
+
+
+def chip_sum(mine, theirs, chips, kept, members):
     other = swap(theirs, members)
     rows, wide = mine.shape[0] // chips, mine.shape[1]
-    terms = small_call(
+    part = jax.ShapeDtypeStruct((rows, wide), jnp.bfloat16)
+    return small_call(
         chip_kernel,
         [mine, other],
-        [jax.ShapeDtypeStruct((rows, wide), jnp.float32)]
-        + [jax.ShapeDtypeStruct((rows, wide), jnp.bfloat16)] * (chips - 1),
+        [jax.ShapeDtypeStruct((rows, wide), jnp.float32)] * kept + [part] * (chips - kept),
     )
-    return [terms[0]] + [give(terms[k], "fsdp", k, chips, 2) for k in range(1, chips)]
+
+
+def scatter_rows(mine, theirs, chips, members):
+    terms = list(chip_sum(mine, theirs, chips, 1, members))
+    for i, step in enumerate(arrangement(chips)[1:]):
+        terms[i + 1] = exchange(terms[i + 1], "fsdp", step, 2, chips)
+    return terms
+
+
+def scatter_halving(mine, theirs, chips, members):
+    first = chip_sum(mine, theirs, chips, chips // 2, members)
+    part = jax.ShapeDtypeStruct(first[0].shape, jnp.bfloat16)
+    terms = [[term] for term in first]
+    for step in levels(chips):
+        kept = len(terms) // 2
+        for i in reversed(range(kept)):
+            sent = terms[kept + i]
+            if len(sent) > 1:
+                sent = [small_call(sum_kernel, sent, part)]
+            terms[i].append(exchange(sent[0], "fsdp", step, 2, chips))
+        terms = terms[:kept]
+    return terms[0]
 
 
 def spread(value, replicas):
-    return [fetch(value, "replica", k, replicas) for k in range(1, replicas)]
+    others = []
+    for step in range(1, replicas):
+        others.append(exchange(value, "replica", step, 1, replicas))
+    return others
 
 
 def small_call(kernel, operands, shapes, partner=None):
@@ -96,27 +126,23 @@
     return chosen
 
 
-def step_to(wanted, here, replicas):
-    return here ^ wanted if replicas & (replicas - 1) == 0 else (wanted - here + replicas) % replicas
-
-
 def foreign_kernel(partner, *refs):
     replicas = partner.shape[0]
     here = lax.axis_index("replica")
     taught = sum(jnp.where(partner[r] == here, r, 0) for r in range(replicas))
-    refs[-1][...] = choose(refs[:-1], step_to(taught, here, replicas))
-
-
-def cotangent_kernel(chips, start, scale, partner, *refs):
+    refs[-1][...] = choose(refs[:-1], here ^ taught)
+
+
+def cotangent_kernel(count, start, scale, partner, *refs):
     replicas = partner.shape[0]
     here = lax.axis_index("replica")
     wanted = sum(jnp.where(here == r, partner[r], 0) for r in range(replicas))
     target = refs[-1]
     columns = pl.ds(start, target.shape[1])
     student = refs[0][:, columns]
-    for term in refs[1:chips]:
+    for term in refs[1:count]:
         student = student + term[:, columns].astype(jnp.float32)
-    teacher = choose(refs[chips:-1], step_to(wanted, here, replicas)).astype(jnp.float32)
+    teacher = choose(refs[count:-1], here ^ wanted).astype(jnp.float32)
     target[...] = ((student - teacher) * scale).astype(target.dtype)
 
 
@@ -353,11 +379,11 @@
         partner,
     )
     gate_w, up_w = load(gate_w, up_w)
-    own_pieces = gather_rows(rows, chips, members)
+    own_pieces = gather_rows(rows, chips, members, relay=True)
     down_w, rows_all, pre_gate, pre_up, hidden, mine, theirs = forward(
         own_pieces, gate_w, up_w, down_w, 1, True
     )
-    student = scatter_rows(mine, theirs, chips, members)
+    student = scatter_halving(mine, theirs, chips, members)
     foreign_pieces = gather_rows(foreign, chips, members)
     parts = forward(foreign_pieces, gate_w, up_w, down_w, CHUNKS, False)
     wide = rows.shape[1] // CHUNKS
@@ -367,7 +393,7 @@
         terms = scatter_rows(parts[2 * c], parts[2 * c + 1], chips, members)
         taught = small_call(sum_kernel, terms, part)
         cotangent = small_call(
-            functools.partial(cotangent_kernel, chips, c * wide, scale),
+            functools.partial(cotangent_kernel, len(student), c * wide, scale),
             student + spread(taught, replicas),
             part,
             partner,

time: 103 us -> 95.6 us (0.928)
  starting transfers between devices: 53.3 us -> 45.7 us
    ppermute x30, starting transfers between devices: 48.7 us -> 41.9 us  [exchange(): return lax.ppermute(value, axis, pairs)]
  transfers between devices with their start and end apart: 49 -> 49, of which waited for: 7 -> 13; matrix products, arithmetic and copies ran while one was open for 0% -> 0% of each run, Pallas kernels for 20% -> 21%
where the time goes in v1:
time: 95.6 us; the launch traced here: 95.4 us
  starting transfers between devices  45.7 us (48%)
  Pallas kernels  28.5 us (30%)
  waiting for transfers between devices  19.6 us (21%)
  between operations  0.98 us (1%)
    ppermute x30, starting transfers between devices, exchange(): return lax.ppermute(value, axis, pairs)  41.9 us
    ppermute x30, waiting for transfers between devices, exchange(): return lax.ppermute(value, axis, pairs)  18.7 us
    pallas_call x2, Pallas kernels, backward(): pl.pallas_call(functools.partial(backward_kernel, len(pieces), first, fin...  10.7 us
    pallas_call x2, Pallas kernels, forward(): pl.pallas_call(functools.partial(forward_kernel, len(pieces), chunks, kee...  10.5 us
    pallas_call x1, Pallas kernels, load(): pl.pallas_call(load_kernel, out_shape=[pltpu.VMEM(w.shape, w.dtype) for w...  5.22 us
    ppermute x19, starting transfers between devices, swap(): return lax.ppermute(value, 'fsdp', [(i, i ^ 1) for i in range(members)])  3.85 us
    pallas_call x9, Pallas kernels, small_call(): pl.pallas_call(kernel, out_shape=shapes, in_specs=[pl.BlockSpec(memory_sp...  2.02 us
  transfers between devices with their start and end apart: 49, of which 13 were waited for; matrix products, arithmetic and copies ran while one was open for 0% of the time, Pallas kernels for 21%

profile of v1, /device:TPU:0, one launch (start us, length us, event | category | flops | bytes accessed | tf_op | source)
XLA Modules:
  0.0 95.4 jit_solution(11912926157253422752)
XLA Ops:
  0.6 4.0 %collective-permute-start.13 = (bf16[16,4096]{1,0:T(8,128)(2,1)}, bf16[16,4096]{1,0:T(8,128)(2,1)S(1)}, u32[]{:S(2)}, u32[]{:S(2)}) collective-permute-start(bf16[16,4096]{1,0:T(8,128)(2,1)} %bitcast.7), channel_id=1, source_target_pairs={{24,0},{16,8},{8,16},{0,24},{25,1},{17,9},{9,17},{1,25},{26,2},{18... | collective-permute-start | bytes 393224 | tf_op jit(solution)/shard_map/ppermute | solution.py:21
  4.6 0.5 collective-permute-start.12
  5.3 3.0 %collective-permute-start = (bf16[16,4096]{1,0:T(8,128)(2,1)}, bf16[16,4096]{1,0:T(8,128)(2,1)S(1)}, u32[]{:S(2)}, u32[]{:S(2)}) collective-permute-start(bf16[16,4096]{1,0:T(8,128)(2,1)} %bitcast.10), channel_id=1, source_target_pairs={{4,0},{5,1},{6,2},{7,3},{0,4},{1,5},{2,6},{3,7},{12,8},{13,9},{14,... | collective-permute-start | bytes 393224 | tf_op jit(solution)/shard_map/ppermute | solution.py:21
  8.3 0.6 collective-permute-done.13.refs_2_
  8.8 1.6 %collective-permute-start.1 = (bf16[16,4096]{1,0:T(8,128)(2,1)}, bf16[16,4096]{1,0:T(8,128)(2,1)S(1)}, u32[]{:S(2)}, u32[]{:S(2)}) collective-permute-start(bf16[16,4096]{1,0:T(8,128)(2,1)} %bitcast.12), channel_id=1, source_target_pairs={{2,0},{3,1},{0,2},{1,3},{6,4},{7,5},{4,6},{5,7},{10,8},{11,9},{8,1... | collective-permute-start | bytes 393224 | tf_op jit(solution)/shard_map/ppermute | solution.py:21
  10.5 0.7 collective-permute-done.12.refs_1_
  11.4 0.7 copy-done.1
  12.0 0.6 shard_map.78.refs_0_
  12.6 3.7 %collective-permute-start.16 = (bf16[16,4096]{1,0:T(8,128)(2,1)S(1)}, bf16[16,4096]{1,0:T(8,128)(2,1)S(1)}, u32[]{:S(2)}, u32[]{:S(2)}) collective-permute-start(bf16[16,4096]{1,0:T(8,128)(2,1)S(1)} %shard_map.78.refs_0_), channel_id=1, source_target_pairs={{6,0},{7,1},{4,2},{5,3},{2,4},{3,5},{0,6},{1,7},{14,8},{15,9},{12,... | collective-permute-start | bytes 393224 | tf_op jit(solution)/shard_map/ppermute | solution.py:21
  16.3 2.0 %collective-permute-start.15 = (bf16[16,4096]{1,0:T(8,128)(2,1)S(1)}, bf16[16,4096]{1,0:T(8,128)(2,1)S(1)}, u32[]{:S(2)}, u32[]{:S(2)}) collective-permute-start(bf16[16,4096]{1,0:T(8,128)(2,1)S(1)} %shard_map.78.refs_0_), channel_id=1, source_target_pairs={{2,0},{3,1},{0,2},{1,3},{6,4},{7,5},{4,6},{5,7},{10,8},{11,9},{8,1... | collective-permute-start | bytes 393224 | tf_op jit(solution)/shard_map/ppermute | solution.py:21
  18.4 2.5 %collective-permute-done.16.refs_3_ = bf16[16,4096]{1,0:T(8,128)(2,1)S(1)} collective-permute-done((bf16[16,4096]{1,0:T(8,128)(2,1)S(1)}, bf16[16,4096]{1,0:T(8,128)(2,1)S(1)}, u32[]{:S(2)}, u32[]{:S(2)}) %collective-permute-start.16) | collective-permute-done | bytes 131104 | tf_op jit(solution)/shard_map/ppermute | solution.py:21
  20.9 5.1 %collective-permute-done.2.refs_3_ = bf16[16,4096]{1,0:T(8,128)(2,1)S(1)} collective-permute-done((bf16[16,4096]{1,0:T(8,128)(2,1)S(1)}, bf16[16,4096]{1,0:T(8,128)(2,1)S(1)}, u32[]{:S(2)}, u32[]{:S(2)}) %collective-permute-start.2) | collective-permute-done | bytes 131104 | tf_op jit(solution)/shard_map/ppermute | solution.py:21
  26.0 5.2 %load.1 = (bf16[896,4096]{1,0:T(8,128)(2,1)S(1)}, bf16[896,4096]{1,0:T(8,128)(2,1)S(1)}) custom-call(bf16[896,4096]{1,0:T(8,128)(2,1)} %bitcast.14, bf16[896,4096]{1,0:T(8,128)(2,1)} %bitcast.15), custom_call_target="tpu_custom_call" | custom-call | bytes 14680064 | tf_op jit(solution)/shard_map/load/pallas_call | solution.py:186
  31.2 0.6 collective-permute-start.17
  32.4 5.3 %student_forward.1 = (bf16[896,4096]{1,0:T(8,128)(2,1)S(1)}, bf16[128,4096]{1,0:T(8,128)(2,1)S(1)}, f32[896,128]{1,0:T(8,128)S(1)}, f32[896,128]{1,0:T(8,128)S(1...) custom-call(bf16[16,4096]{1,0:T(8,128)(2,1)S(1)} %bitcast.13, ...), custom_call_target="tpu_custom_call" | custom-call | flops 2818572288 | bytes 22020096 | tf_op jit(solution)/shard_map/student_forward/pallas_call | solution.py:254
  37.7 0.5 collective-permute-start.7
  38.2 5.2 %teacher_forward.1 = (f32[64,2048]{1,0:T(8,128)S(1)}, bf16[64,2048]{1,0:T(8,128)(2,1)S(1)}, f32[64,2048]{1,0:T(8,128)S(1)}, bf16[64,2048]{1,0:T(8,128)(2,1)S(1)}) custom-call(bf16[16,4096]{1,0:T(8,128)(2,1)S(1)} %shard_map.78.refs_0_, bf16[16,4096]{1,0:T(8,128)(2,1)S(1)} %collective-permute-done.14.refs_1_, ...), custom_call_target="tpu_custom_call" | custom-call | flops 2818572288 | bytes 22020096 | tf_op jit(solution)/shard_map/teacher_forward/pallas_call | solution.py:254
  44.2 0.8 collective-permute-done.21.other
  45.1 2.9 %collective-permute-start.22 = (bf16[16,2048]{1,0:T(8,128)(2,1)S(1)}, bf16[16,2048]{1,0:T(8,128)(2,1)S(1)}, u32[]{:S(2)}, u32[]{:S(2)}) collective-permute-start(bf16[16,2048]{1,0:T(8,128)(2,1)S(1)} %get-tuple-element.45), channel_id=1, source_target_pairs={{4,0},{5,1},{6,2},{7,3},{0,4},{1,5},{2,6},{3,7},{12,8},{13,9},{14,... | collective-permute-start | bytes 196616 | tf_op jit(solution)/shard_map/ppermute | solution.py:21
  48.0 0.9 collective-permute-start.23
  48.9 0.7 collective-permute-start.24
  49.6 2.0 %collective-permute-start.36 = (bf16[16,2048]{1,0:T(8,128)(2,1)S(1)}, bf16[16,2048]{1,0:T(8,128)(2,1)S(1)}, u32[]{:S(2)}, u32[]{:S(2)}) collective-permute-start(bf16[16,2048]{1,0:T(8,128)(2,1)S(1)} %get-tuple-element.52), channel_id=1, source_target_pairs={{4,0},{5,1},{6,2},{7,3},{0,4},{1,5},{2,6},{3,7},{12,8},{13,9},{14,... | collective-permute-start | bytes 196616 | tf_op jit(solution)/shard_map/ppermute | solution.py:21
  51.6 2.0 %collective-permute-start.37 = (bf16[16,2048]{1,0:T(8,128)(2,1)S(1)}, bf16[16,2048]{1,0:T(8,128)(2,1)S(1)}, u32[]{:S(2)}, u32[]{:S(2)}) collective-permute-start(bf16[16,2048]{1,0:T(8,128)(2,1)S(1)} %get-tuple-element.53), channel_id=1, source_target_pairs={{2,0},{3,1},{0,2},{1,3},{6,4},{7,5},{4,6},{5,7},{10,8},{11,9},{8,1... | collective-permute-start | bytes 196616 | tf_op jit(solution)/shard_map/ppermute | solution.py:21
  53.7 2.3 %collective-permute-start.38 = (bf16[16,2048]{1,0:T(8,128)(2,1)S(1)}, bf16[16,2048]{1,0:T(8,128)(2,1)S(1)}, u32[]{:S(2)}, u32[]{:S(2)}) collective-permute-start(bf16[16,2048]{1,0:T(8,128)(2,1)S(1)} %get-tuple-element.54), channel_id=1, source_target_pairs={{6,0},{7,1},{4,2},{5,3},{2,4},{3,5},{0,6},{1,7},{14,8},{15,9},{12,... | collective-permute-start | bytes 196616 | tf_op jit(solution)/shard_map/ppermute | solution.py:21
  56.0 1.2 %collective-permute-start.8 = (bf16[16,4096]{1,0:T(8,128)(2,1)S(1)}, bf16[16,4096]{1,0:T(8,128)(2,1)S(1)}, u32[]{:S(2)}, u32[]{:S(2)}) collective-permute-start(bf16[16,4096]{1,0:T(8,128)(2,1)S(1)} %get-tuple-element.38), channel_id=1, source_target_pairs={{2,0},{3,1},{0,2},{1,3},{6,4},{7,5},{4,6},{5,7},{10,8},{11,9},{8,1... | collective-permute-start | bytes 393224 | tf_op jit(solution)/shard_map/ppermute | solution.py:21
  57.2 1.9 %collective-permute-start.10 = (bf16[16,4096]{1,0:T(8,128)(2,1)S(1)}, bf16[16,4096]{1,0:T(8,128)(2,1)S(1)}, u32[]{:S(2)}, u32[]{:S(2)}) collective-permute-start(bf16[16,4096]{1,0:T(8,128)(2,1)S(1)} %shard_map.77), channel_id=1, source_target_pairs={{4,0},{5,1},{6,2},{7,3},{0,4},{1,5},{2,6},{3,7},{12,8},{13,9},{14,... | collective-permute-start | bytes 393224 | tf_op jit(solution)/shard_map/ppermute | solution.py:21
  59.2 0.6 collective-permute-done.36.refs_1_
  59.8 1.0 %collective-permute-start.27 = (bf16[16,2048]{1,0:T(8,128)(2,1)S(1)}, bf16[16,2048]{1,0:T(8,128)(2,1)S(1)}, u32[]{:S(2)}, u32[]{:S(2)}) collective-permute-start(bf16[16,2048]{1,0:T(8,128)(2,1)S(1)} %shard_map.80), channel_id=1, source_target_pairs={{24,0},{16,8},{8,16},{0,24},{25,1},{17,9},{9,17},{1,25},{26,2},{18... | collective-permute-start | bytes 196616 | tf_op jit(solution)/shard_map/ppermute | solution.py:21
  60.8 1.9 %collective-permute-start.26 = (bf16[16,2048]{1,0:T(8,128)(2,1)S(1)}, bf16[16,2048]{1,0:T(8,128)(2,1)S(1)}, u32[]{:S(2)}, u32[]{:S(2)}) collective-permute-start(bf16[16,2048]{1,0:T(8,128)(2,1)S(1)} %shard_map.80), channel_id=1, source_target_pairs={{16,0},{24,8},{0,16},{8,24},{17,1},{25,9},{1,17},{9,25},{18,2},{26... | collective-permute-start | bytes 196616 | tf_op jit(solution)/shard_map/ppermute | solution.py:21
  62.7 0.5 collective-permute-start.25
  63.3 1.8 %collective-permute-done.27.refs_5_ = bf16[16,2048]{1,0:T(8,128)(2,1)S(1)} collective-permute-done((bf16[16,2048]{1,0:T(8,128)(2,1)S(1)}, bf16[16,2048]{1,0:T(8,128)(2,1)S(1)}, u32[]{:S(2)}, u32[]{:S(2)}) %collective-permute-start.27) | collective-permute-done | bytes 65568 | tf_op jit(solution)/shard_map/ppermute | solution.py:21
  65.1 0.8 collective-permute-start.41
  66.0 1.0 %collective-permute-done.26.refs_4_ = bf16[16,2048]{1,0:T(8,128)(2,1)S(1)} collective-permute-done((bf16[16,2048]{1,0:T(8,128)(2,1)S(1)}, bf16[16,2048]{1,0:T(8,128)(2,1)S(1)}, u32[]{:S(2)}, u32[]{:S(2)}) %collective-permute-start.26) | collective-permute-done | bytes 65568 | tf_op jit(solution)/shard_map/ppermute | solution.py:21
  66.9 1.6 %collective-permute-start.40 = (bf16[16,2048]{1,0:T(8,128)(2,1)S(1)}, bf16[16,2048]{1,0:T(8,128)(2,1)S(1)}, u32[]{:S(2)}, u32[]{:S(2)}) collective-permute-start(bf16[16,2048]{1,0:T(8,128)(2,1)S(1)} %shard_map.83), channel_id=1, source_target_pairs={{16,0},{24,8},{0,16},{8,24},{17,1},{25,9},{1,17},{9,25},{18,2},{26... | collective-permute-start | bytes 196616 | tf_op jit(solution)/shard_map/ppermute | solution.py:21
  68.6 0.6 shard_map.81.refs_0_
  69.2 2.0 %collective-permute-start.30 = (bf16[16,2048]{1,0:T(8,128)(2,1)S(1)}, bf16[16,2048]{1,0:T(8,128)(2,1)S(1)}, u32[]{:S(2)}, u32[]{:S(2)}) collective-permute-start(bf16[16,2048]{1,0:T(8,128)(2,1)S(1)} %shard_map.81.refs_0_), channel_id=1, source_target_pairs={{6,0},{7,1},{4,2},{5,3},{2,4},{3,5},{0,6},{1,7},{14,8},{15,9},{12,... | collective-permute-start | bytes 196616 | tf_op jit(solution)/shard_map/ppermute | solution.py:21
  71.2 1.6 %collective-permute-done.39.refs_3_ = bf16[16,2048]{1,0:T(8,128)(2,1)S(1)} collective-permute-done((bf16[16,2048]{1,0:T(8,128)(2,1)S(1)}, bf16[16,2048]{1,0:T(8,128)(2,1)S(1)}, u32[]{:S(2)}, u32[]{:S(2)}) %collective-permute-start.39) | collective-permute-done | bytes 65568 | tf_op jit(solution)/shard_map/ppermute | solution.py:21
  72.8 0.6 shard_map.84.refs_0_
  73.4 2.0 %collective-permute-start.44 = (bf16[16,2048]{1,0:T(8,128)(2,1)S(1)}, bf16[16,2048]{1,0:T(8,128)(2,1)S(1)}, u32[]{:S(2)}, u32[]{:S(2)}) collective-permute-start(bf16[16,2048]{1,0:T(8,128)(2,1)S(1)} %shard_map.84.refs_0_), channel_id=1, source_target_pairs={{6,0},{7,1},{4,2},{5,3},{2,4},{3,5},{0,6},{1,7},{14,8},{15,9},{12,... | collective-permute-start | bytes 196616 | tf_op jit(solution)/shard_map/ppermute | solution.py:21
  75.4 2.6 %collective-permute-start.42 = (bf16[16,2048]{1,0:T(8,128)(2,1)S(1)}, bf16[16,2048]{1,0:T(8,128)(2,1)S(1)}, u32[]{:S(2)}, u32[]{:S(2)}) collective-permute-start(bf16[16,2048]{1,0:T(8,128)(2,1)S(1)} %shard_map.84.refs_0_), channel_id=1, source_target_pairs={{4,0},{5,1},{6,2},{7,3},{0,4},{1,5},{2,6},{3,7},{12,8},{13,9},{14,... | collective-permute-start | bytes 196616 | tf_op jit(solution)/shard_map/ppermute | solution.py:21
  78.3 1.5 %collective-permute-done.44.refs_3_ = bf16[16,2048]{1,0:T(8,128)(2,1)S(1)} collective-permute-done((bf16[16,2048]{1,0:T(8,128)(2,1)S(1)}, bf16[16,2048]{1,0:T(8,128)(2,1)S(1)}, u32[]{:S(2)}, u32[]{:S(2)}) %collective-permute-start.44) | collective-permute-done | bytes 65568 | tf_op jit(solution)/shard_map/ppermute | solution.py:21
  79.9 1.4 %collective-permute-done.43.refs_2_ = bf16[16,2048]{1,0:T(8,128)(2,1)S(1)} collective-permute-done((bf16[16,2048]{1,0:T(8,128)(2,1)S(1)}, bf16[16,2048]{1,0:T(8,128)(2,1)S(1)}, u32[]{:S(2)}, u32[]{:S(2)}) %collective-permute-start.43) | collective-permute-done | bytes 65568 | tf_op jit(solution)/shard_map/ppermute | solution.py:21
  81.3 0.5 collective-permute-start.46
  81.8 1.7 %collective-permute-done.28.refs_1_ = bf16[16,2048]{1,0:T(8,128)(2,1)S(1)} collective-permute-done((bf16[16,2048]{1,0:T(8,128)(2,1)S(1)}, bf16[16,2048]{1,0:T(8,128)(2,1)S(1)}, u32[]{:S(2)}, u32[]{:S(2)}) %collective-permute-start.28) | collective-permute-done | bytes 65568 | tf_op jit(solution)/shard_map/ppermute | solution.py:21
  83.4 0.5 collective-permute-start.34
  84.0 0.4 collective-permute-start.32
  84.5 2.5 %shard_map.85 = (bf16[896,4096]{1,0:T(8,128)(2,1)}, f32[896,128]{1,0:T(8,128)S(1)}) custom-call(bf16[16,2048]{1,0:T(8,128)(2,1)S(1)} %shard_map.84.refs_0_, bf16[16,2048]{1,0:T(8,128)(2,1)S(1)} %collective-permute-done.42.refs_1_, bf16[16,2048]{1,0:T(8,128)(2,1)S(1)} %collective-permute-done.43.refs_2_, ...), custom_call_target="tpu_custom_call" | custom-call | flops 939524096 | bytes 7340032 | tf_op jit(solution)/shard_map/pallas_call | solution.py:352
  87.0 8.2 %shard_map.86 = (bf16[896,4096]{1,0:T(8,128)(2,1)}, bf16[896,4096]{1,0:T(8,128)(2,1)}, bf16[896,4096]{1,0:T(8,128)(2,1)}) custom-call(bf16[16,2048]{1,0:T(8,128)(2,1)S(1)} %shard_map.81.refs_0_, bf16[16,2048]{1,0:T(8,128)(2,1)S(1)} %collective-permute-done.28.refs_1_, ...), custom_call_target="tpu_custom_call", output_to_operand_aliasing={{0}: (11, {})} | custom-call | flops 2818572288 | bytes 22020096 | tf_op jit(solution)/shard_map/pallas_call | solution.py:352
  (68 shorter events, 2.5 us)
Async XLA Ops:
  0.6 8.2 %collective-permute-start.13 = (bf16[16,4096]{1,0:T(8,128)(2,1)}, bf16[16,4096]{1,0:T(8,128)(2,1)S(1)}, u32[]{:S(2)}, u32[]{:S(2)}) collective-permute-start(bf16[16,4096]{1,0:T(8,128)(2,1)} %bitcast.7), channel_id=1, source_target_pairs={{24,0},{16,8},{8,16},{0,24},{25,1},{17,9},{9,17},{1,25},{26,2},{18... | collective-permute-start | bytes 393224 | tf_op jit(solution)/shard_map/ppermute | solution.py:21
  4.6 6.5 %collective-permute-start.12 = (bf16[16,4096]{1,0:T(8,128)(2,1)}, bf16[16,4096]{1,0:T(8,128)(2,1)S(1)}, u32[]{:S(2)}, u32[]{:S(2)}) collective-permute-start(bf16[16,4096]{1,0:T(8,128)(2,1)} %bitcast.8), channel_id=1, source_target_pairs={{16,0},{24,8},{0,16},{8,24},{17,1},{25,9},{1,17},{9,25},{18,2},{26... | collective-permute-start | bytes 393224 | tf_op jit(solution)/shard_map/ppermute | solution.py:21
  5.1 6.3 %collective-permute-start.11 = (bf16[16,4096]{1,0:T(8,128)(2,1)}, bf16[16,4096]{1,0:T(8,128)(2,1)S(1)}, u32[]{:S(2)}, u32[]{:S(2)}) collective-permute-start(bf16[16,4096]{1,0:T(8,128)(2,1)} %bitcast.9), channel_id=1, source_target_pairs={{8,0},{0,8},{24,16},{16,24},{9,1},{1,9},{25,17},{17,25},{10,2},{2,... | collective-permute-start | bytes 393224 | tf_op jit(solution)/shard_map/ppermute | solution.py:21
  5.3 11.0 %collective-permute-start = (bf16[16,4096]{1,0:T(8,128)(2,1)}, bf16[16,4096]{1,0:T(8,128)(2,1)S(1)}, u32[]{:S(2)}, u32[]{:S(2)}) collective-permute-start(bf16[16,4096]{1,0:T(8,128)(2,1)} %bitcast.10), channel_id=1, source_target_pairs={{4,0},{5,1},{6,2},{7,3},{0,4},{1,5},{2,6},{3,7},{12,8},{13,9},{14,... | collective-permute-start | bytes 393224 | tf_op jit(solution)/shard_map/ppermute | solution.py:21
  8.2 10.1 %collective-permute-start.3 = (bf16[16,4096]{1,0:T(8,128)(2,1)}, bf16[16,4096]{1,0:T(8,128)(2,1)S(1)}, u32[]{:S(2)}, u32[]{:S(2)}) collective-permute-start(bf16[16,4096]{1,0:T(8,128)(2,1)} %bitcast.11), channel_id=1, source_target_pairs={{0,1},{1,0},{2,3},{3,2},{4,5},{5,4},{6,7},{7,6},{8,9},{9,8},{10,11... | collective-permute-start | bytes 393224 | tf_op jit(solution)/shard_map/ppermute | solution.py:37
  8.8 9.5 %collective-permute-start.1 = (bf16[16,4096]{1,0:T(8,128)(2,1)}, bf16[16,4096]{1,0:T(8,128)(2,1)S(1)}, u32[]{:S(2)}, u32[]{:S(2)}) collective-permute-start(bf16[16,4096]{1,0:T(8,128)(2,1)} %bitcast.12), channel_id=1, source_target_pairs={{2,0},{3,1},{0,2},{1,3},{6,4},{7,5},{4,6},{5,7},{10,8},{11,9},{8,1... | collective-permute-start | bytes 393224 | tf_op jit(solution)/shard_map/ppermute | solution.py:21
  12.6 8.3 %collective-permute-start.16 = (bf16[16,4096]{1,0:T(8,128)(2,1)S(1)}, bf16[16,4096]{1,0:T(8,128)(2,1)S(1)}, u32[]{:S(2)}, u32[]{:S(2)}) collective-permute-start(bf16[16,4096]{1,0:T(8,128)(2,1)S(1)} %shard_map.78.refs_0_), channel_id=1, source_target_pairs={{6,0},{7,1},{4,2},{5,3},{2,4},{3,5},{0,6},{1,7},{14,8},{15,9},{12,... | collective-permute-start | bytes 393224 | tf_op jit(solution)/shard_map/ppermute | solution.py:21
  16.3 9.7 %collective-permute-start.2 = (bf16[16,4096]{1,0:T(8,128)(2,1)S(1)}, bf16[16,4096]{1,0:T(8,128)(2,1)S(1)}, u32[]{:S(2)}, u32[]{:S(2)}) collective-permute-start(bf16[16,4096]{1,0:T(8,128)(2,1)S(1)} %collective-permute-done.refs_1_), channel_id=1, source_target_pairs={{2,0},{3,1},{0,2},{1,3},{6,4},{7,5},{4,6},{5,7},{10,8},{11,9},{8,1... | collective-permute-start | bytes 393224 | tf_op jit(solution)/shard_map/ppermute | solution.py:21
  16.3 14.9 %collective-permute-start.15 = (bf16[16,4096]{1,0:T(8,128)(2,1)S(1)}, bf16[16,4096]{1,0:T(8,128)(2,1)S(1)}, u32[]{:S(2)}, u32[]{:S(2)}) collective-permute-start(bf16[16,4096]{1,0:T(8,128)(2,1)S(1)} %shard_map.78.refs_0_), channel_id=1, source_target_pairs={{2,0},{3,1},{0,2},{1,3},{6,4},{7,5},{4,6},{5,7},{10,8},{11,9},{8,1... | collective-permute-start | bytes 393224 | tf_op jit(solution)/shard_map/ppermute | solution.py:21
  18.3 13.5 %collective-permute-start.14 = (bf16[16,4096]{1,0:T(8,128)(2,1)S(1)}, bf16[16,4096]{1,0:T(8,128)(2,1)S(1)}, u32[]{:S(2)}, u32[]{:S(2)}) collective-permute-start(bf16[16,4096]{1,0:T(8,128)(2,1)S(1)} %shard_map.78.refs_0_), channel_id=1, source_target_pairs={{4,0},{5,1},{6,2},{7,3},{0,4},{1,5},{2,6},{3,7},{12,8},{13,9},{14,... | collective-permute-start | bytes 393224 | tf_op jit(solution)/shard_map/ppermute | solution.py:21
  18.3 13.6 %collective-permute-start.5 = (bf16[16,4096]{1,0:T(8,128)(2,1)S(1)}, bf16[16,4096]{1,0:T(8,128)(2,1)S(1)}, u32[]{:S(2)}, u32[]{:S(2)}) collective-permute-start(bf16[16,4096]{1,0:T(8,128)(2,1)S(1)} %collective-permute-done.1.refs_2_), channel_id=1, source_target_pairs={{0,1},{1,0},{2,3},{3,2},{4,5},{5,4},{6,7},{7,6},{8,9},{9,8},{10,11... | collective-permute-start | bytes 393224 | tf_op jit(solution)/shard_map/ppermute | solution.py:37
  20.9 11.4 %collective-permute-start.4 = (bf16[16,4096]{1,0:T(8,128)(2,1)S(1)}, bf16[16,4096]{1,0:T(8,128)(2,1)S(1)}, u32[]{:S(2)}, u32[]{:S(2)}) collective-permute-start(bf16[16,4096]{1,0:T(8,128)(2,1)S(1)} %collective-permute-done.refs_1_), channel_id=1, source_target_pairs={{0,1},{1,0},{2,3},{3,2},{4,5},{5,4},{6,7},{7,6},{8,9},{9,8},{10,11... | collective-permute-start | bytes 393224 | tf_op jit(solution)/shard_map/ppermute | solution.py:37
  26.0 6.4 %collective-permute-start.6 = (bf16[16,4096]{1,0:T(8,128)(2,1)S(1)}, bf16[16,4096]{1,0:T(8,128)(2,1)S(1)}, u32[]{:S(2)}, u32[]{:S(2)}) collective-permute-start(bf16[16,4096]{1,0:T(8,128)(2,1)S(1)} %collective-permute-done.2.refs_3_), channel_id=1, source_target_pairs={{0,1},{1,0},{2,3},{3,2},{4,5},{5,4},{6,7},{7,6},{8,9},{9,8},{10,11... | collective-permute-start | bytes 393224 | tf_op jit(solution)/shard_map/ppermute | solution.py:37
  31.2 7.0 %collective-permute-start.17 = (bf16[16,4096]{1,0:T(8,128)(2,1)S(1)}, bf16[16,4096]{1,0:T(8,128)(2,1)S(1)}, u32[]{:S(2)}, u32[]{:S(2)}) collective-permute-start(bf16[16,4096]{1,0:T(8,128)(2,1)S(1)} %shard_map.78.refs_0_), channel_id=1, source_target_pairs={{0,1},{1,0},{2,3},{3,2},{4,5},{5,4},{6,7},{7,6},{8,9},{9,8},{10,11... | collective-permute-start | bytes 393224 | tf_op jit(solution)/shard_map/ppermute | solution.py:37
  31.8 6.4 %collective-permute-start.20 = (bf16[16,4096]{1,0:T(8,128)(2,1)S(1)}, bf16[16,4096]{1,0:T(8,128)(2,1)S(1)}, u32[]{:S(2)}, u32[]{:S(2)}) collective-permute-start(bf16[16,4096]{1,0:T(8,128)(2,1)S(1)} %collective-permute-done.16.refs_3_), channel_id=1, source_target_pairs={{0,1},{1,0},{2,3},{3,2},{4,5},{5,4},{6,7},{7,6},{8,9},{9,8},{10,11... | collective-permute-start | bytes 393224 | tf_op jit(solution)/shard_map/ppermute | solution.py:37
  31.9 6.3 %collective-permute-start.19 = (bf16[16,4096]{1,0:T(8,128)(2,1)S(1)}, bf16[16,4096]{1,0:T(8,128)(2,1)S(1)}, u32[]{:S(2)}, u32[]{:S(2)}) collective-permute-start(bf16[16,4096]{1,0:T(8,128)(2,1)S(1)} %collective-permute-done.15.refs_2_), channel_id=1, source_target_pairs={{0,1},{1,0},{2,3},{3,2},{4,5},{5,4},{6,7},{7,6},{8,9},{9,8},{10,11... | collective-permute-start | bytes 393224 | tf_op jit(solution)/shard_map/ppermute | solution.py:37
  32.3 5.9 %collective-permute-start.18 = (bf16[16,4096]{1,0:T(8,128)(2,1)S(1)}, bf16[16,4096]{1,0:T(8,128)(2,1)S(1)}, u32[]{:S(2)}, u32[]{:S(2)}) collective-permute-start(bf16[16,4096]{1,0:T(8,128)(2,1)S(1)} %collective-permute-done.14.refs_1_), channel_id=1, source_target_pairs={{0,1},{1,0},{2,3},{3,2},{4,5},{5,4},{6,7},{7,6},{8,9},{9,8},{10,11... | collective-permute-start | bytes 393224 | tf_op jit(solution)/shard_map/ppermute | solution.py:37
  37.7 6.3 %collective-permute-start.7 = (bf16[64,4096]{1,0:T(8,128)(2,1)S(1)}, bf16[64,4096]{1,0:T(8,128)(2,1)S(1)}, u32[]{:S(2)}, u32[]{:S(2)}) collective-permute-start(bf16[64,4096]{1,0:T(8,128)(2,1)S(1)} %get-tuple-element.36), channel_id=1, source_target_pairs={{0,1},{1,0},{2,3},{3,2},{4,5},{5,4},{6,7},{7,6},{8,9},{9,8},{10,11... | collective-permute-start | bytes 1572872 | tf_op jit(solution)/shard_map/ppermute | solution.py:37
  43.6 6.0 %collective-permute-start.35 = (bf16[64,2048]{1,0:T(8,128)(2,1)S(1)}, bf16[64,2048]{1,0:T(8,128)(2,1)S(1)}, u32[]{:S(2)}, u32[]{:S(2)}) collective-permute-start(bf16[64,2048]{1,0:T(8,128)(2,1)S(1)} %get-tuple-element.50), channel_id=1, source_target_pairs={{0,1},{1,0},{2,3},{3,2},{4,5},{5,4},{6,7},{7,6},{8,9},{9,8},{10,11... | collective-permute-start | bytes 786440 | tf_op jit(solution)/shard_map/ppermute | solution.py:37
  44.1 9.5 %collective-permute-start.9 = (bf16[16,4096]{1,0:T(8,128)(2,1)S(1)}, bf16[16,4096]{1,0:T(8,128)(2,1)S(1)}, u32[]{:S(2)}, u32[]{:S(2)}) collective-permute-start(bf16[16,4096]{1,0:T(8,128)(2,1)S(1)} %get-tuple-element.40), channel_id=1, source_target_pairs={{2,0},{3,1},{0,2},{1,3},{6,4},{7,5},{4,6},{5,7},{10,8},{11,9},{8,1... | collective-permute-start | bytes 393224 | tf_op jit(solution)/shard_map/ppermute | solution.py:21
  45.1 6.5 %collective-permute-start.22 = (bf16[16,2048]{1,0:T(8,128)(2,1)S(1)}, bf16[16,2048]{1,0:T(8,128)(2,1)S(1)}, u32[]{:S(2)}, u32[]{:S(2)}) collective-permute-start(bf16[16,2048]{1,0:T(8,128)(2,1)S(1)} %get-tuple-element.45), channel_id=1, source_target_pairs={{4,0},{5,1},{6,2},{7,3},{0,4},{1,5},{2,6},{3,7},{12,8},{13,9},{14,... | collective-permute-start | bytes 196616 | tf_op jit(solution)/shard_map/ppermute | solution.py:21
  48.0 8.0 %collective-permute-start.23 = (bf16[16,2048]{1,0:T(8,128)(2,1)S(1)}, bf16[16,2048]{1,0:T(8,128)(2,1)S(1)}, u32[]{:S(2)}, u32[]{:S(2)}) collective-permute-start(bf16[16,2048]{1,0:T(8,128)(2,1)S(1)} %get-tuple-element.46), channel_id=1, source_target_pairs={{2,0},{3,1},{0,2},{1,3},{6,4},{7,5},{4,6},{5,7},{10,8},{11,9},{8,1... | collective-permute-start | bytes 196616 | tf_op jit(solution)/shard_map/ppermute | solution.py:21
  48.9 8.3 %collective-permute-start.24 = (bf16[16,2048]{1,0:T(8,128)(2,1)S(1)}, bf16[16,2048]{1,0:T(8,128)(2,1)S(1)}, u32[]{:S(2)}, u32[]{:S(2)}) collective-permute-start(bf16[16,2048]{1,0:T(8,128)(2,1)S(1)} %get-tuple-element.47), channel_id=1, source_target_pairs={{6,0},{7,1},{4,2},{5,3},{2,4},{3,5},{0,6},{1,7},{14,8},{15,9},{12,... | collective-permute-start | bytes 196616 | tf_op jit(solution)/shard_map/ppermute | solution.py:21
  49.6 10.1 %collective-permute-start.36 = (bf16[16,2048]{1,0:T(8,128)(2,1)S(1)}, bf16[16,2048]{1,0:T(8,128)(2,1)S(1)}, u32[]{:S(2)}, u32[]{:S(2)}) collective-permute-start(bf16[16,2048]{1,0:T(8,128)(2,1)S(1)} %get-tuple-element.52), channel_id=1, source_target_pairs={{4,0},{5,1},{6,2},{7,3},{0,4},{1,5},{2,6},{3,7},{12,8},{13,9},{14,... | collective-permute-start | bytes 196616 | tf_op jit(solution)/shard_map/ppermute | solution.py:21
  51.6 9.2 %collective-permute-start.37 = (bf16[16,2048]{1,0:T(8,128)(2,1)S(1)}, bf16[16,2048]{1,0:T(8,128)(2,1)S(1)}, u32[]{:S(2)}, u32[]{:S(2)}) collective-permute-start(bf16[16,2048]{1,0:T(8,128)(2,1)S(1)} %get-tuple-element.53), channel_id=1, source_target_pairs={{2,0},{3,1},{0,2},{1,3},{6,4},{7,5},{4,6},{5,7},{10,8},{11,9},{8,1... | collective-permute-start | bytes 196616 | tf_op jit(solution)/shard_map/ppermute | solution.py:21
  53.7 9.1 %collective-permute-start.38 = (bf16[16,2048]{1,0:T(8,128)(2,1)S(1)}, bf16[16,2048]{1,0:T(8,128)(2,1)S(1)}, u32[]{:S(2)}, u32[]{:S(2)}) collective-permute-start(bf16[16,2048]{1,0:T(8,128)(2,1)S(1)} %get-tuple-element.54), channel_id=1, source_target_pairs={{6,0},{7,1},{4,2},{5,3},{2,4},{3,5},{0,6},{1,7},{14,8},{15,9},{12,... | collective-permute-start | bytes 196616 | tf_op jit(solution)/shard_map/ppermute | solution.py:21
  56.0 12.6 %collective-permute-start.8 = (bf16[16,4096]{1,0:T(8,128)(2,1)S(1)}, bf16[16,4096]{1,0:T(8,128)(2,1)S(1)}, u32[]{:S(2)}, u32[]{:S(2)}) collective-permute-start(bf16[16,4096]{1,0:T(8,128)(2,1)S(1)} %get-tuple-element.38), channel_id=1, source_target_pairs={{2,0},{3,1},{0,2},{1,3},{6,4},{7,5},{4,6},{5,7},{10,8},{11,9},{8,1... | collective-permute-start | bytes 393224 | tf_op jit(solution)/shard_map/ppermute | solution.py:21
  57.2 11.4 %collective-permute-start.10 = (bf16[16,4096]{1,0:T(8,128)(2,1)S(1)}, bf16[16,4096]{1,0:T(8,128)(2,1)S(1)}, u32[]{:S(2)}, u32[]{:S(2)}) collective-permute-start(bf16[16,4096]{1,0:T(8,128)(2,1)S(1)} %shard_map.77), channel_id=1, source_target_pairs={{4,0},{5,1},{6,2},{7,3},{0,4},{1,5},{2,6},{3,7},{12,8},{13,9},{14,... | collective-permute-start | bytes 393224 | tf_op jit(solution)/shard_map/ppermute | solution.py:21
  59.8 5.4 %collective-permute-start.27 = (bf16[16,2048]{1,0:T(8,128)(2,1)S(1)}, bf16[16,2048]{1,0:T(8,128)(2,1)S(1)}, u32[]{:S(2)}, u32[]{:S(2)}) collective-permute-start(bf16[16,2048]{1,0:T(8,128)(2,1)S(1)} %shard_map.80), channel_id=1, source_target_pairs={{24,0},{16,8},{8,16},{0,24},{25,1},{17,9},{9,17},{1,25},{26,2},{18... | collective-permute-start | bytes 196616 | tf_op jit(solution)/shard_map/ppermute | solution.py:21
  60.8 6.1 %collective-permute-start.26 = (bf16[16,2048]{1,0:T(8,128)(2,1)S(1)}, bf16[16,2048]{1,0:T(8,128)(2,1)S(1)}, u32[]{:S(2)}, u32[]{:S(2)}) collective-permute-start(bf16[16,2048]{1,0:T(8,128)(2,1)S(1)} %shard_map.80), channel_id=1, source_target_pairs={{16,0},{24,8},{0,16},{8,24},{17,1},{25,9},{1,17},{9,25},{18,2},{26... | collective-permute-start | bytes 196616 | tf_op jit(solution)/shard_map/ppermute | solution.py:21
  62.7 5.8 %collective-permute-start.25 = (bf16[16,2048]{1,0:T(8,128)(2,1)S(1)}, bf16[16,2048]{1,0:T(8,128)(2,1)S(1)}, u32[]{:S(2)}, u32[]{:S(2)}) collective-permute-start(bf16[16,2048]{1,0:T(8,128)(2,1)S(1)} %shard_map.80), channel_id=1, source_target_pairs={{8,0},{0,8},{24,16},{16,24},{9,1},{1,9},{25,17},{17,25},{10,2},{2,... | collective-permute-start | bytes 196616 | tf_op jit(solution)/shard_map/ppermute | solution.py:21
  65.1 6.1 %collective-permute-start.41 = (bf16[16,2048]{1,0:T(8,128)(2,1)S(1)}, bf16[16,2048]{1,0:T(8,128)(2,1)S(1)}, u32[]{:S(2)}, u32[]{:S(2)}) collective-permute-start(bf16[16,2048]{1,0:T(8,128)(2,1)S(1)} %shard_map.83), channel_id=1, source_target_pairs={{24,0},{16,8},{8,16},{0,24},{25,1},{17,9},{9,17},{1,25},{26,2},{18... | collective-permute-start | bytes 196616 | tf_op jit(solution)/shard_map/ppermute | solution.py:21
  66.9 4.3 %collective-permute-start.40 = (bf16[16,2048]{1,0:T(8,128)(2,1)S(1)}, bf16[16,2048]{1,0:T(8,128)(2,1)S(1)}, u32[]{:S(2)}, u32[]{:S(2)}) collective-permute-start(bf16[16,2048]{1,0:T(8,128)(2,1)S(1)} %shard_map.83), channel_id=1, source_target_pairs={{16,0},{24,8},{0,16},{8,24},{17,1},{25,9},{1,17},{9,25},{18,2},{26... | collective-permute-start | bytes 196616 | tf_op jit(solution)/shard_map/ppermute | solution.py:21
  68.6 4.3 %collective-permute-start.39 = (bf16[16,2048]{1,0:T(8,128)(2,1)S(1)}, bf16[16,2048]{1,0:T(8,128)(2,1)S(1)}, u32[]{:S(2)}, u32[]{:S(2)}) collective-permute-start(bf16[16,2048]{1,0:T(8,128)(2,1)S(1)} %shard_map.83), channel_id=1, source_target_pairs={{8,0},{0,8},{24,16},{16,24},{9,1},{1,9},{25,17},{17,25},{10,2},{2,... | collective-permute-start | bytes 196616 | tf_op jit(solution)/shard_map/ppermute | solution.py:21
  69.2 8.8 %collective-permute-start.30 = (bf16[16,2048]{1,0:T(8,128)(2,1)S(1)}, bf16[16,2048]{1,0:T(8,128)(2,1)S(1)}, u32[]{:S(2)}, u32[]{:S(2)}) collective-permute-start(bf16[16,2048]{1,0:T(8,128)(2,1)S(1)} %shard_map.81.refs_0_), channel_id=1, source_target_pairs={{6,0},{7,1},{4,2},{5,3},{2,4},{3,5},{0,6},{1,7},{14,8},{15,9},{12,... | collective-permute-start | bytes 196616 | tf_op jit(solution)/shard_map/ppermute | solution.py:21
  71.2 7.1 %collective-permute-start.29 = (bf16[16,2048]{1,0:T(8,128)(2,1)S(1)}, bf16[16,2048]{1,0:T(8,128)(2,1)S(1)}, u32[]{:S(2)}, u32[]{:S(2)}) collective-permute-start(bf16[16,2048]{1,0:T(8,128)(2,1)S(1)} %shard_map.81.refs_0_), channel_id=1, source_target_pairs={{2,0},{3,1},{0,2},{1,3},{6,4},{7,5},{4,6},{5,7},{10,8},{11,9},{8,1... | collective-permute-start | bytes 196616 | tf_op jit(solution)/shard_map/ppermute | solution.py:21
  73.4 6.5 %collective-permute-start.44 = (bf16[16,2048]{1,0:T(8,128)(2,1)S(1)}, bf16[16,2048]{1,0:T(8,128)(2,1)S(1)}, u32[]{:S(2)}, u32[]{:S(2)}) collective-permute-start(bf16[16,2048]{1,0:T(8,128)(2,1)S(1)} %shard_map.84.refs_0_), channel_id=1, source_target_pairs={{6,0},{7,1},{4,2},{5,3},{2,4},{3,5},{0,6},{1,7},{14,8},{15,9},{12,... | collective-permute-start | bytes 196616 | tf_op jit(solution)/shard_map/ppermute | solution.py:21
  75.4 5.9 %collective-permute-start.43 = (bf16[16,2048]{1,0:T(8,128)(2,1)S(1)}, bf16[16,2048]{1,0:T(8,128)(2,1)S(1)}, u32[]{:S(2)}, u32[]{:S(2)}) collective-permute-start(bf16[16,2048]{1,0:T(8,128)(2,1)S(1)} %shard_map.84.refs_0_), channel_id=1, source_target_pairs={{2,0},{3,1},{0,2},{1,3},{6,4},{7,5},{4,6},{5,7},{10,8},{11,9},{8,1... | collective-permute-start | bytes 196616 | tf_op jit(solution)/shard_map/ppermute | solution.py:21
  75.4 5.9 %collective-permute-start.42 = (bf16[16,2048]{1,0:T(8,128)(2,1)S(1)}, bf16[16,2048]{1,0:T(8,128)(2,1)S(1)}, u32[]{:S(2)}, u32[]{:S(2)}) collective-permute-start(bf16[16,2048]{1,0:T(8,128)(2,1)S(1)} %shard_map.84.refs_0_), channel_id=1, source_target_pairs={{4,0},{5,1},{6,2},{7,3},{0,4},{1,5},{2,6},{3,7},{12,8},{13,9},{14,... | collective-permute-start | bytes 196616 | tf_op jit(solution)/shard_map/ppermute | solution.py:21
  78.1 5.4 %collective-permute-start.28 = (bf16[16,2048]{1,0:T(8,128)(2,1)S(1)}, bf16[16,2048]{1,0:T(8,128)(2,1)S(1)}, u32[]{:S(2)}, u32[]{:S(2)}) collective-permute-start(bf16[16,2048]{1,0:T(8,128)(2,1)S(1)} %shard_map.81.refs_0_), channel_id=1, source_target_pairs={{4,0},{5,1},{6,2},{7,3},{0,4},{1,5},{2,6},{3,7},{12,8},{13,9},{14,... | collective-permute-start | bytes 196616 | tf_op jit(solution)/shard_map/ppermute | solution.py:21
  78.3 5.1 %collective-permute-start.45 = (bf16[16,2048]{1,0:T(8,128)(2,1)S(1)}, bf16[16,2048]{1,0:T(8,128)(2,1)S(1)}, u32[]{:S(2)}, u32[]{:S(2)}) collective-permute-start(bf16[16,2048]{1,0:T(8,128)(2,1)S(1)} %shard_map.84.refs_0_), channel_id=1, source_target_pairs={{0,1},{1,0},{2,3},{3,2},{4,5},{5,4},{6,7},{7,6},{8,9},{9,8},{10,11... | collective-permute-start | bytes 196616 | tf_op jit(solution)/shard_map/ppermute | solution.py:37
  79.9 4.1 %collective-permute-start.48 = (bf16[16,2048]{1,0:T(8,128)(2,1)S(1)}, bf16[16,2048]{1,0:T(8,128)(2,1)S(1)}, u32[]{:S(2)}, u32[]{:S(2)}) collective-permute-start(bf16[16,2048]{1,0:T(8,128)(2,1)S(1)} %collective-permute-done.44.refs_3_), channel_id=1, source_target_pairs={{0,1},{1,0},{2,3},{3,2},{4,5},{5,4},{6,7},{7,6},{8,9},{9,8},{10,11... | collective-permute-start | bytes 196616 | tf_op jit(solution)/shard_map/ppermute | solution.py:37
  81.3 2.8 %collective-permute-start.47 = (bf16[16,2048]{1,0:T(8,128)(2,1)S(1)}, bf16[16,2048]{1,0:T(8,128)(2,1)S(1)}, u32[]{:S(2)}, u32[]{:S(2)}) collective-permute-start(bf16[16,2048]{1,0:T(8,128)(2,1)S(1)} %collective-permute-done.43.refs_2_), channel_id=1, source_target_pairs={{0,1},{1,0},{2,3},{3,2},{4,5},{5,4},{6,7},{7,6},{8,9},{9,8},{10,11... | collective-permute-start | bytes 196616 | tf_op jit(solution)/shard_map/ppermute | solution.py:37
  81.3 3.2 %collective-permute-start.46 = (bf16[16,2048]{1,0:T(8,128)(2,1)S(1)}, bf16[16,2048]{1,0:T(8,128)(2,1)S(1)}, u32[]{:S(2)}, u32[]{:S(2)}) collective-permute-start(bf16[16,2048]{1,0:T(8,128)(2,1)S(1)} %collective-permute-done.42.refs_1_), channel_id=1, source_target_pairs={{0,1},{1,0},{2,3},{3,2},{4,5},{5,4},{6,7},{7,6},{8,9},{9,8},{10,11... | collective-permute-start | bytes 196616 | tf_op jit(solution)/shard_map/ppermute | solution.py:37
  83.4 3.5 %collective-permute-start.31 = (bf16[16,2048]{1,0:T(8,128)(2,1)S(1)}, bf16[16,2048]{1,0:T(8,128)(2,1)S(1)}, u32[]{:S(2)}, u32[]{:S(2)}) collective-permute-start(bf16[16,2048]{1,0:T(8,128)(2,1)S(1)} %shard_map.81.refs_0_), channel_id=1, source_target_pairs={{0,1},{1,0},{2,3},{3,2},{4,5},{5,4},{6,7},{7,6},{8,9},{9,8},{10,11... | collective-permute-start | bytes 196616 | tf_op jit(solution)/shard_map/ppermute | solution.py:37
  83.4 3.5 %collective-permute-start.34 = (bf16[16,2048]{1,0:T(8,128)(2,1)S(1)}, bf16[16,2048]{1,0:T(8,128)(2,1)S(1)}, u32[]{:S(2)}, u32[]{:S(2)}) collective-permute-start(bf16[16,2048]{1,0:T(8,128)(2,1)S(1)} %collective-permute-done.30.refs_3_), channel_id=1, source_target_pairs={{0,1},{1,0},{2,3},{3,2},{4,5},{5,4},{6,7},{7,6},{8,9},{9,8},{10,11... | collective-permute-start | bytes 196616 | tf_op jit(solution)/shard_map/ppermute | solution.py:37
  84.0 3.0 %collective-permute-start.33 = (bf16[16,2048]{1,0:T(8,128)(2,1)S(1)}, bf16[16,2048]{1,0:T(8,128)(2,1)S(1)}, u32[]{:S(2)}, u32[]{:S(2)}) collective-permute-start(bf16[16,2048]{1,0:T(8,128)(2,1)S(1)} %collective-permute-done.29.refs_2_), channel_id=1, source_target_pairs={{0,1},{1,0},{2,3},{3,2},{4,5},{5,4},{6,7},{7,6},{8,9},{9,8},{10,11... | collective-permute-start | bytes 196616 | tf_op jit(solution)/shard_map/ppermute | solution.py:37
  84.0 2.9 %collective-permute-start.32 = (bf16[16,2048]{1,0:T(8,128)(2,1)S(1)}, bf16[16,2048]{1,0:T(8,128)(2,1)S(1)}, u32[]{:S(2)}, u32[]{:S(2)}) collective-permute-start(bf16[16,2048]{1,0:T(8,128)(2,1)S(1)} %collective-permute-done.28.refs_1_), channel_id=1, source_target_pairs={{0,1},{1,0},{2,3},{3,2},{4,5},{5,4},{6,7},{7,6},{8,9},{9,8},{10,11... | collective-permute-start | bytes 196616 | tf_op jit(solution)/shard_map/ppermute | solution.py:37
  (3 other events, 8.7 us)

commit v2 on v1

--- a/solution.py
+++ b/solution.py
@@ -37,16 +37,26 @@
     return lax.ppermute(value, "fsdp", [(i, i ^ 1) for i in range(members)])
 
 
-def gather_rows(rows, chips, members, relay=False):
-    mine, theirs = [rows], []
-    for step in arrangement(chips)[1:] if not relay else []:
+def gather_direct(rows, chips):
+    mine = [rows]
+    for step in arrangement(chips)[1:]:
         mine.append(exchange(rows, "fsdp", step, 2, chips))
-    for step in levels(chips)[::-1] if relay else []:
+    return mine
+
+
+def gather_doubling(rows, chips):
+    mine = [rows]
+    for step in levels(chips)[::-1]:
         fresh = []
         for piece in mine:
             fresh.append(exchange(piece, "fsdp", step, 2, chips))
         mine += fresh
-    for step, piece in zip(arrangement(chips), mine):
+    return mine
+
+
+def with_other_core(mine, members):
+    theirs = []
+    for piece in mine:
         theirs.append(swap(piece, members))
     return mine + theirs
 
@@ -62,7 +72,7 @@
     )
 
 
-def scatter_rows(mine, theirs, chips, members):
+def scatter_direct(mine, theirs, chips, members):
     terms = list(chip_sum(mine, theirs, chips, 1, members))
     for i, step in enumerate(arrangement(chips)[1:]):
         terms[i + 1] = exchange(terms[i + 1], "fsdp", step, 2, chips)
@@ -197,74 +207,112 @@
     )(*[in_hbm(w) for w in weights])
 
 
-def forward_kernel(count, chunks, keep, *refs):
-    pieces, (gate_w, up_w, down_w) = refs[:count], refs[count : count + 3]
-    rest = list(refs[count + 3 :])
-    if keep:
-        down_hbm = down_w
-        down_w, rows_all, pre_gate, pre_up, hidden = rest[:5]
-        outs, sem = rest[5:-1], rest[-1]
-        fill = pltpu.make_async_copy(down_hbm, down_w, sem)
-        fill.start()
-    else:
-        outs, (rows_all, hidden) = rest[: 2 * chunks], rest[2 * chunks :]
+def hidden_units(pieces, gate_w, up_w, rows_all, hidden, saved):
+    put_together(pieces, rows_all)
     height = gate_w.shape[0]
     step = block_of(height)
-    put_together(pieces, rows_all)
     for j in range(height // step):
         part = pl.ds(j * step, step)
         gate = contract(gate_w[part], rows_all[...], 1, 1)
         up = contract(up_w[part], rows_all[...], 1, 1)
-        if keep:
-            pre_gate[part] = gate
-            pre_up[part] = up
+        if saved:
+            saved[0][part] = gate
+            saved[1][part] = up
         hidden[part] = (gate * jax.nn.sigmoid(gate) * up).astype(hidden.dtype)
-    if keep:
-        fill.wait()
-    half = rows_all.shape[0] // 2
-    wide = down_w.shape[1] // chunks
+
+
+def down_product(hidden, down_w, first, mine, theirs):
+    half, wide = mine.shape
     tile = min(512, wide)
     across = hidden[...].T
-    for c in range(chunks):
-        for start in range(0, wide, tile):
-            value = contract(across, down_w[:, pl.ds(c * wide + start, tile)], 1, 0)
-            outs[2 * c][:, start : start + tile] = value[:half]
-            outs[2 * c + 1][:, start : start + tile] = value[half:].astype(jnp.bfloat16)
-
-
-def forward(pieces, gate_w, up_w, down_w, chunks, keep):
+    for start in range(0, wide, tile):
+        value = contract(across, down_w[:, pl.ds(first + start, tile)], 1, 0)
+        mine[:, start : start + tile] = value[:half]
+        theirs[:, start : start + tile] = value[half:].astype(theirs.dtype)
+
+
+def student_kernel(count, *refs):
+    gate_w, up_w, down_hbm, down_w, rows_all, pre_gate, pre_up, hidden = refs[count : count + 8]
+    mine, theirs, sem = refs[count + 8 :]
+    fill = pltpu.make_async_copy(down_hbm, down_w, sem)
+    fill.start()
+    hidden_units(refs[:count], gate_w, up_w, rows_all, hidden, (pre_gate, pre_up))
+    fill.wait()
+    down_product(hidden, down_w, 0, mine, theirs)
+
+
+def teacher_kernel(count, *refs):
+    gate_w, up_w, hidden, rows_all = refs[count:]
+    hidden_units(refs[:count], gate_w, up_w, rows_all, hidden, ())
+
+
+def product_call(kernel, operands, in_specs, shapes, scratch, flops, grant):
+    return pl.pallas_call(
+        kernel,
+        out_shape=shapes,
+        in_specs=in_specs,
+        out_specs=[VMEM] * len(shapes),
+        scratch_shapes=scratch,
+        compiler_params=pltpu.CompilerParams(vmem_limit_bytes=grant << 20),
+        cost_estimate=pl.CostEstimate(
+            flops=flops, bytes_accessed=flops // 128, transcendentals=0
+        ),
+    )(*operands)
+
+
+def halves(rows, wide):
+    return [
+        jax.ShapeDtypeStruct((rows // 2, wide), jnp.float32),
+        jax.ShapeDtypeStruct((rows // 2, wide), jnp.bfloat16),
+    ]
+
+
+def student_forward(pieces, gate_w, up_w, down_w):
     height, depth = gate_w.shape
     rows = len(pieces) * pieces[0].shape[0]
-    wide = depth // chunks
-    shapes, scratch = [], []
-    if keep:
-        scratch += [pltpu.SemaphoreType.DMA]
-        shapes += [
-            pltpu.VMEM((height, depth), jnp.bfloat16),
-            jax.ShapeDtypeStruct((rows, depth), jnp.bfloat16),
-            jax.ShapeDtypeStruct((height, rows), jnp.float32),
-            jax.ShapeDtypeStruct((height, rows), jnp.float32),
-            jax.ShapeDtypeStruct((height, rows), jnp.bfloat16),
-        ]
-    else:
-        scratch += [pltpu.VMEM((rows, depth), jnp.bfloat16), pltpu.VMEM((height, rows), jnp.bfloat16)]
-    for _ in range(chunks):
-        shapes.append(jax.ShapeDtypeStruct((rows // 2, wide), jnp.float32))
-        shapes.append(jax.ShapeDtypeStruct((rows // 2, wide), jnp.bfloat16))
-    return pl.pallas_call(
-        functools.partial(forward_kernel, len(pieces), chunks, keep),
-        out_shape=shapes,
-        in_specs=[VMEM] * (len(pieces) + 2) + [ANY if keep else VMEM],
-        out_specs=[VMEM] * len(shapes),
-        scratch_shapes=scratch,
-        compiler_params=pltpu.CompilerParams(vmem_limit_bytes=12 << 20),
-        cost_estimate=pl.CostEstimate(
-            flops=6 * rows * height * depth,
-            bytes_accessed=6 * height * depth,
-            transcendentals=rows * height,
-        ),
-        name="student_forward" if keep else "teacher_forward",
-    )(*pieces, in_vmem(gate_w), in_vmem(up_w), (in_hbm if keep else in_vmem)(down_w))
+    shapes = [
+        pltpu.VMEM((height, depth), jnp.bfloat16),
+        jax.ShapeDtypeStruct((rows, depth), jnp.bfloat16),
+        jax.ShapeDtypeStruct((height, rows), jnp.float32),
+        jax.ShapeDtypeStruct((height, rows), jnp.float32),
+        jax.ShapeDtypeStruct((height, rows), jnp.bfloat16),
+    ] + halves(rows, depth)
+    return product_call(
+        functools.partial(student_kernel, len(pieces)),
+        [*pieces, in_vmem(gate_w), in_vmem(up_w), in_hbm(down_w)],
+        [VMEM] * (len(pieces) + 2) + [ANY],
+        shapes,
+        [pltpu.SemaphoreType.DMA],
+        6 * rows * height * depth,
+        12,
+    )
+
+
+def teacher_hidden(pieces, gate_w, up_w):
+    height, depth = gate_w.shape
+    rows = len(pieces) * pieces[0].shape[0]
+    return product_call(
+        functools.partial(teacher_kernel, len(pieces)),
+        [*pieces, in_vmem(gate_w), in_vmem(up_w)],
+        [VMEM] * (len(pieces) + 2),
+        [jax.ShapeDtypeStruct((height, rows), jnp.bfloat16)],
+        [pltpu.VMEM((rows, depth), jnp.bfloat16)],
+        4 * rows * height * depth,
+        12,
+    )[0]
+
+
+def teacher_down(hidden, down_w, first, wide):
+    height, rows = hidden.shape
+    return product_call(
+        lambda hidden, down_w, *outs: down_product(hidden, down_w, first, *outs),
+        [hidden, in_vmem(down_w)],
+        [VMEM] * 2,
+        halves(rows, wide),
+        [],
+        2 * rows * height * wide,
+        8,
+    )
 
 
 def backward_kernel(count, first, final, start, *refs):
@@ -379,18 +427,19 @@
         partner,
     )
     gate_w, up_w = load(gate_w, up_w)
-    own_pieces = gather_rows(rows, chips, members, relay=True)
-    down_w, rows_all, pre_gate, pre_up, hidden, mine, theirs = forward(
-        own_pieces, gate_w, up_w, down_w, 1, True
+    own = with_other_core(gather_doubling(rows, chips), members)
+    down_w, rows_all, pre_gate, pre_up, hidden, mine, theirs = student_forward(
+        own, gate_w, up_w, down_w
     )
     student = scatter_halving(mine, theirs, chips, members)
-    foreign_pieces = gather_rows(foreign, chips, members)
-    parts = forward(foreign_pieces, gate_w, up_w, down_w, CHUNKS, False)
+    other = with_other_core(gather_direct(foreign, chips), members)
+    teacher_units = teacher_hidden(other, gate_w, up_w)
     wide = rows.shape[1] // CHUNKS
     part = jax.ShapeDtypeStruct((rows.shape[0], wide), jnp.bfloat16)
     carried = None
     for c in range(CHUNKS):
-        terms = scatter_rows(parts[2 * c], parts[2 * c + 1], chips, members)
+        mine, theirs = teacher_down(teacher_units, down_w, c * wide, wide)
+        terms = scatter_direct(mine, theirs, chips, members)
         taught = small_call(sum_kernel, terms, part)
         cotangent = small_call(
             functools.partial(cotangent_kernel, len(student), c * wide, scale),
@@ -398,7 +447,8 @@
             part,
             partner,
         )
-        pieces = gather_rows(cotangent, chips, members)
+        mine = gather_direct(cotangent, chips)
+        pieces = with_other_core(mine, members)
         saved = (pre_gate, pre_up, rows_all) if c == CHUNKS - 1 else None
         grads = backward(pieces, hidden, down_w, carried, saved, c * wide)
         carried = (grads[1], grads[0])

time: 95.6 us -> 96.4 us (level)
  starting transfers between devices: 45.7 us -> 47.4 us
  waiting for transfers between devices: 19.6 us -> 18.5 us
    ppermute x30, starting transfers between devices: 41.9 us -> 43.8 us  [exchange(): return lax.ppermute(value, axis, pairs)]
    pallas_call x2 -> x4, Pallas kernels: 10.5 us -> 10.7 us  [product_call(): pl.pallas_call(kernel, out_shape=shapes, in_specs=in_specs, out_specs=[VM...]
where the time goes in v2:
time: 96.4 us; the launch traced here: 96.2 us
  starting transfers between devices  47.4 us (49%)
  Pallas kernels  28.6 us (30%)
  waiting for transfers between devices  18.5 us (19%)
  between operations  1.01 us (1%)
    ppermute x30, starting transfers between devices, exchange(): return lax.ppermute(value, axis, pairs)  43.8 us
    ppermute x30, waiting for transfers between devices, exchange(): return lax.ppermute(value, axis, pairs)  18.4 us
    pallas_call x4, Pallas kernels, product_call(): pl.pallas_call(kernel, out_shape=shapes, in_specs=in_specs, out_specs=[VM...  10.7 us
    pallas_call x2, Pallas kernels, backward(): pl.pallas_call(functools.partial(backward_kernel, len(pieces), first, fin...  10.7 us
    pallas_call x1, Pallas kernels, load(): pl.pallas_call(load_kernel, out_shape=[pltpu.VMEM(w.shape, w.dtype) for w...  5.22 us
    ppermute x19, starting transfers between devices, swap(): return lax.ppermute(value, 'fsdp', [(i, i ^ 1) for i in range(members)])  3.59 us
    pallas_call x9, Pallas kernels, small_call(): pl.pallas_call(kernel, out_shape=shapes, in_specs=[pl.BlockSpec(memory_sp...  2.02 us
  transfers between devices with their start and end apart: 49, of which 13 were waited for; matrix products, arithmetic and copies ran while one was open for 0% of the time, Pallas kernels for 21%

profile of v2, /device:TPU:0, one launch (start us, length us, event | category | flops | bytes accessed | tf_op | source)
XLA Modules:
  0.0 96.2 jit_solution(17348329768016410999)
XLA Ops:
  0.6 4.0 %collective-permute-start.13 = (bf16[16,4096]{1,0:T(8,128)(2,1)}, bf16[16,4096]{1,0:T(8,128)(2,1)S(1)}, u32[]{:S(2)}, u32[]{:S(2)}) collective-permute-start(bf16[16,4096]{1,0:T(8,128)(2,1)} %bitcast.7), channel_id=1, source_target_pairs={{24,0},{16,8},{8,16},{0,24},{25,1},{17,9},{9,17},{1,25},{26,2},{18... | collective-permute-start | bytes 393224 | tf_op jit(solution)/shard_map/ppermute | solution.py:21
  4.6 0.5 collective-permute-start.12
  5.3 3.0 %collective-permute-start = (bf16[16,4096]{1,0:T(8,128)(2,1)}, bf16[16,4096]{1,0:T(8,128)(2,1)S(1)}, u32[]{:S(2)}, u32[]{:S(2)}) collective-permute-start(bf16[16,4096]{1,0:T(8,128)(2,1)} %bitcast.10), channel_id=1, source_target_pairs={{4,0},{5,1},{6,2},{7,3},{0,4},{1,5},{2,6},{3,7},{12,8},{13,9},{14,... | collective-permute-start | bytes 393224 | tf_op jit(solution)/shard_map/ppermute | solution.py:21
  8.3 0.6 collective-permute-done.13.refs_2_
  8.8 1.6 %collective-permute-start.1 = (bf16[16,4096]{1,0:T(8,128)(2,1)}, bf16[16,4096]{1,0:T(8,128)(2,1)S(1)}, u32[]{:S(2)}, u32[]{:S(2)}) collective-permute-start(bf16[16,4096]{1,0:T(8,128)(2,1)} %bitcast.12), channel_id=1, source_target_pairs={{2,0},{3,1},{0,2},{1,3},{6,4},{7,5},{4,6},{5,7},{10,8},{11,9},{8,1... | collective-permute-start | bytes 393224 | tf_op jit(solution)/shard_map/ppermute | solution.py:21
  10.5 0.7 collective-permute-done.12.refs_1_
  11.4 0.7 copy-done.1
  12.0 0.6 shard_map.79.refs_0_
  12.6 3.7 %collective-permute-start.16 = (bf16[16,4096]{1,0:T(8,128)(2,1)S(1)}, bf16[16,4096]{1,0:T(8,128)(2,1)S(1)}, u32[]{:S(2)}, u32[]{:S(2)}) collective-permute-start(bf16[16,4096]{1,0:T(8,128)(2,1)S(1)} %shard_map.79.refs_0_), channel_id=1, source_target_pairs={{6,0},{7,1},{4,2},{5,3},{2,4},{3,5},{0,6},{1,7},{14,8},{15,9},{12,... | collective-permute-start | bytes 393224 | tf_op jit(solution)/shard_map/ppermute | solution.py:21
  16.3 2.0 %collective-permute-start.15 = (bf16[16,4096]{1,0:T(8,128)(2,1)S(1)}, bf16[16,4096]{1,0:T(8,128)(2,1)S(1)}, u32[]{:S(2)}, u32[]{:S(2)}) collective-permute-start(bf16[16,4096]{1,0:T(8,128)(2,1)S(1)} %shard_map.79.refs_0_), channel_id=1, source_target_pairs={{2,0},{3,1},{0,2},{1,3},{6,4},{7,5},{4,6},{5,7},{10,8},{11,9},{8,1... | collective-permute-start | bytes 393224 | tf_op jit(solution)/shard_map/ppermute | solution.py:21
  18.4 2.5 %collective-permute-done.16.refs_3_ = bf16[16,4096]{1,0:T(8,128)(2,1)S(1)} collective-permute-done((bf16[16,4096]{1,0:T(8,128)(2,1)S(1)}, bf16[16,4096]{1,0:T(8,128)(2,1)S(1)}, u32[]{:S(2)}, u32[]{:S(2)}) %collective-permute-start.16) | collective-permute-done | bytes 131104 | tf_op jit(solution)/shard_map/ppermute | solution.py:21
  20.9 5.1 %collective-permute-done.2.refs_3_ = bf16[16,4096]{1,0:T(8,128)(2,1)S(1)} collective-permute-done((bf16[16,4096]{1,0:T(8,128)(2,1)S(1)}, bf16[16,4096]{1,0:T(8,128)(2,1)S(1)}, u32[]{:S(2)}, u32[]{:S(2)}) %collective-permute-start.2) | collective-permute-done | bytes 131104 | tf_op jit(solution)/shard_map/ppermute | solution.py:21
  26.0 5.2 %load.1 = (bf16[896,4096]{1,0:T(8,128)(2,1)S(1)}, bf16[896,4096]{1,0:T(8,128)(2,1)S(1)}) custom-call(bf16[896,4096]{1,0:T(8,128)(2,1)} %bitcast.14, bf16[896,4096]{1,0:T(8,128)(2,1)} %bitcast.15), custom_call_target="tpu_custom_call" | custom-call | bytes 14680064 | tf_op jit(solution)/shard_map/load/pallas_call | solution.py:196
  31.2 0.6 collective-permute-start.17
  31.9 0.4 collective-permute-start.19
  32.4 5.3 %shard_map.76 = (bf16[896,4096]{1,0:T(8,128)(2,1)S(1)}, bf16[128,4096]{1,0:T(8,128)(2,1)S(1)}, f32[896,128]{1,0:T(8,128)S(1)}, f32[896,128]{1,0:T(8,128)S(1)}, b...) custom-call(bf16[16,4096]{1,0:T(8,128)(2,1)S(1)} %bitcast.13, ...), custom_call_target="tpu_custom_call" | custom-call | flops 2818572288 | bytes 22020096 | tf_op jit(solution)/shard_map/pallas_call | solution.py:250
  37.7 0.5 collective-permute-start.7
  38.2 4.0 %shard_map.80.hidden = bf16[896,128]{1,0:T(8,128)(2,1)S(1)} custom-call(bf16[16,4096]{1,0:T(8,128)(2,1)S(1)} %shard_map.79.refs_0_, bf16[16,4096]{1,0:T(8,128)(2,1)S(1)} %collective-permute-done.14.refs_1_, bf16[16,4096]{1,0:T(8,128)(2,1)S(1)} %collective-permute-done.15.refs_2_, bf16[16,4096]{1,0:T(8,128)(2,1)S(1)} %collective-permute-done.16.refs_3_, ...), custom_call_target="tpu_custom_call" | custom-call | flops 1879048192 | bytes 14680064 | tf_op jit(solution)/shard_map/pallas_call | solution.py:250
  42.2 0.7 shard_map.85
  43.1 0.7 shard_map.81
  43.8 0.5 collective-permute-start.21
  44.6 3.7 %collective-permute-start.36 = (bf16[16,2048]{1,0:T(8,128)(2,1)S(1)}, bf16[16,2048]{1,0:T(8,128)(2,1)S(1)}, u32[]{:S(2)}, u32[]{:S(2)}) collective-permute-start(bf16[16,2048]{1,0:T(8,128)(2,1)S(1)} %get-tuple-element.52), channel_id=1, source_target_pairs={{4,0},{5,1},{6,2},{7,3},{0,4},{1,5},{2,6},{3,7},{12,8},{13,9},{14,... | collective-permute-start | bytes 196616 | tf_op jit(solution)/shard_map/ppermute | solution.py:21
  48.4 1.5 %collective-permute-start.38 = (bf16[16,2048]{1,0:T(8,128)(2,1)S(1)}, bf16[16,2048]{1,0:T(8,128)(2,1)S(1)}, u32[]{:S(2)}, u32[]{:S(2)}) collective-permute-start(bf16[16,2048]{1,0:T(8,128)(2,1)S(1)} %get-tuple-element.54), channel_id=1, source_target_pairs={{6,0},{7,1},{4,2},{5,3},{2,4},{3,5},{0,6},{1,7},{14,8},{15,9},{12,... | collective-permute-start | bytes 196616 | tf_op jit(solution)/shard_map/ppermute | solution.py:21
  49.9 2.0 %collective-permute-start.22 = (bf16[16,2048]{1,0:T(8,128)(2,1)S(1)}, bf16[16,2048]{1,0:T(8,128)(2,1)S(1)}, u32[]{:S(2)}, u32[]{:S(2)}) collective-permute-start(bf16[16,2048]{1,0:T(8,128)(2,1)S(1)} %get-tuple-element.45), channel_id=1, source_target_pairs={{4,0},{5,1},{6,2},{7,3},{0,4},{1,5},{2,6},{3,7},{12,8},{13,9},{14,... | collective-permute-start | bytes 196616 | tf_op jit(solution)/shard_map/ppermute | solution.py:21
  51.9 2.0 %collective-permute-start.23 = (bf16[16,2048]{1,0:T(8,128)(2,1)S(1)}, bf16[16,2048]{1,0:T(8,128)(2,1)S(1)}, u32[]{:S(2)}, u32[]{:S(2)}) collective-permute-start(bf16[16,2048]{1,0:T(8,128)(2,1)S(1)} %get-tuple-element.46), channel_id=1, source_target_pairs={{2,0},{3,1},{0,2},{1,3},{6,4},{7,5},{4,6},{5,7},{10,8},{11,9},{8,1... | collective-permute-start | bytes 196616 | tf_op jit(solution)/shard_map/ppermute | solution.py:21
  54.0 2.2 %collective-permute-start.24 = (bf16[16,2048]{1,0:T(8,128)(2,1)S(1)}, bf16[16,2048]{1,0:T(8,128)(2,1)S(1)}, u32[]{:S(2)}, u32[]{:S(2)}) collective-permute-start(bf16[16,2048]{1,0:T(8,128)(2,1)S(1)} %get-tuple-element.47), channel_id=1, source_target_pairs={{6,0},{7,1},{4,2},{5,3},{2,4},{3,5},{0,6},{1,7},{14,8},{15,9},{12,... | collective-permute-start | bytes 196616 | tf_op jit(solution)/shard_map/ppermute | solution.py:21
  56.5 2.3 %collective-permute-start.10 = (bf16[16,4096]{1,0:T(8,128)(2,1)S(1)}, bf16[16,4096]{1,0:T(8,128)(2,1)S(1)}, u32[]{:S(2)}, u32[]{:S(2)}) collective-permute-start(bf16[16,4096]{1,0:T(8,128)(2,1)S(1)} %shard_map.78), channel_id=1, source_target_pairs={{4,0},{5,1},{6,2},{7,3},{0,4},{1,5},{2,6},{3,7},{12,8},{13,9},{14,... | collective-permute-start | bytes 393224 | tf_op jit(solution)/shard_map/ppermute | solution.py:21
  58.9 1.2 %collective-permute-done.22.refs_1_ = bf16[16,2048]{1,0:T(8,128)(2,1)S(1)} collective-permute-done((bf16[16,2048]{1,0:T(8,128)(2,1)S(1)}, bf16[16,2048]{1,0:T(8,128)(2,1)S(1)}, u32[]{:S(2)}, u32[]{:S(2)}) %collective-permute-start.22) | collective-permute-done | bytes 65568 | tf_op jit(solution)/shard_map/ppermute | solution.py:21
  60.1 1.4 %collective-permute-start.41 = (bf16[16,2048]{1,0:T(8,128)(2,1)S(1)}, bf16[16,2048]{1,0:T(8,128)(2,1)S(1)}, u32[]{:S(2)}, u32[]{:S(2)}) collective-permute-start(bf16[16,2048]{1,0:T(8,128)(2,1)S(1)} %shard_map.87), channel_id=1, source_target_pairs={{24,0},{16,8},{8,16},{0,24},{25,1},{17,9},{9,17},{1,25},{26,2},{18... | collective-permute-start | bytes 196616 | tf_op jit(solution)/shard_map/ppermute | solution.py:21
  61.4 1.6 %collective-permute-start.40 = (bf16[16,2048]{1,0:T(8,128)(2,1)S(1)}, bf16[16,2048]{1,0:T(8,128)(2,1)S(1)}, u32[]{:S(2)}, u32[]{:S(2)}) collective-permute-start(bf16[16,2048]{1,0:T(8,128)(2,1)S(1)} %shard_map.87), channel_id=1, source_target_pairs={{16,0},{24,8},{0,16},{8,24},{17,1},{25,9},{1,17},{9,25},{18,2},{26... | collective-permute-start | bytes 196616 | tf_op jit(solution)/shard_map/ppermute | solution.py:21
  63.0 0.5 collective-permute-start.39
  63.6 2.1 %collective-permute-done.41.refs_5_ = bf16[16,2048]{1,0:T(8,128)(2,1)S(1)} collective-permute-done((bf16[16,2048]{1,0:T(8,128)(2,1)S(1)}, bf16[16,2048]{1,0:T(8,128)(2,1)S(1)}, u32[]{:S(2)}, u32[]{:S(2)}) %collective-permute-start.41) | collective-permute-done | bytes 65568 | tf_op jit(solution)/shard_map/ppermute | solution.py:21
  65.7 1.4 %collective-permute-start.27 = (bf16[16,2048]{1,0:T(8,128)(2,1)S(1)}, bf16[16,2048]{1,0:T(8,128)(2,1)S(1)}, u32[]{:S(2)}, u32[]{:S(2)}) collective-permute-start(bf16[16,2048]{1,0:T(8,128)(2,1)S(1)} %shard_map.83), channel_id=1, source_target_pairs={{24,0},{16,8},{8,16},{0,24},{25,1},{17,9},{9,17},{1,25},{26,2},{18... | collective-permute-start | bytes 196616 | tf_op jit(solution)/shard_map/ppermute | solution.py:21
  67.3 1.5 %collective-permute-start.26 = (bf16[16,2048]{1,0:T(8,128)(2,1)S(1)}, bf16[16,2048]{1,0:T(8,128)(2,1)S(1)}, u32[]{:S(2)}, u32[]{:S(2)}) collective-permute-start(bf16[16,2048]{1,0:T(8,128)(2,1)S(1)} %shard_map.83), channel_id=1, source_target_pairs={{16,0},{24,8},{0,16},{8,24},{17,1},{25,9},{1,17},{9,25},{18,2},{26... | collective-permute-start | bytes 196616 | tf_op jit(solution)/shard_map/ppermute | solution.py:21
  69.3 0.6 shard_map.88.refs_0_
  69.9 1.1 %collective-permute-start.44 = (bf16[16,2048]{1,0:T(8,128)(2,1)S(1)}, bf16[16,2048]{1,0:T(8,128)(2,1)S(1)}, u32[]{:S(2)}, u32[]{:S(2)}) collective-permute-start(bf16[16,2048]{1,0:T(8,128)(2,1)S(1)} %shard_map.88.refs_0_), channel_id=1, source_target_pairs={{6,0},{7,1},{4,2},{5,3},{2,4},{3,5},{0,6},{1,7},{14,8},{15,9},{12,... | collective-permute-start | bytes 196616 | tf_op jit(solution)/shard_map/ppermute | solution.py:21
  71.6 2.8 %collective-permute-start.42 = (bf16[16,2048]{1,0:T(8,128)(2,1)S(1)}, bf16[16,2048]{1,0:T(8,128)(2,1)S(1)}, u32[]{:S(2)}, u32[]{:S(2)}) collective-permute-start(bf16[16,2048]{1,0:T(8,128)(2,1)S(1)} %shard_map.88.refs_0_), channel_id=1, source_target_pairs={{4,0},{5,1},{6,2},{7,3},{0,4},{1,5},{2,6},{3,7},{12,8},{13,9},{14,... | collective-permute-start | bytes 196616 | tf_op jit(solution)/shard_map/ppermute | solution.py:21
  74.4 0.6 shard_map.84.refs_0_
  75.0 1.1 %collective-permute-start.30 = (bf16[16,2048]{1,0:T(8,128)(2,1)S(1)}, bf16[16,2048]{1,0:T(8,128)(2,1)S(1)}, u32[]{:S(2)}, u32[]{:S(2)}) collective-permute-start(bf16[16,2048]{1,0:T(8,128)(2,1)S(1)} %shard_map.84.refs_0_), channel_id=1, source_target_pairs={{6,0},{7,1},{4,2},{5,3},{2,4},{3,5},{0,6},{1,7},{14,8},{15,9},{12,... | collective-permute-start | bytes 196616 | tf_op jit(solution)/shard_map/ppermute | solution.py:21
  76.1 0.8 collective-permute-done.44.refs_3_
  76.8 2.6 %collective-permute-start.28 = (bf16[16,2048]{1,0:T(8,128)(2,1)S(1)}, bf16[16,2048]{1,0:T(8,128)(2,1)S(1)}, u32[]{:S(2)}, u32[]{:S(2)}) collective-permute-start(bf16[16,2048]{1,0:T(8,128)(2,1)S(1)} %shard_map.84.refs_0_), channel_id=1, source_target_pairs={{4,0},{5,1},{6,2},{7,3},{0,4},{1,5},{2,6},{3,7},{12,8},{13,9},{14,... | collective-permute-start | bytes 196616 | tf_op jit(solution)/shard_map/ppermute | solution.py:21
  79.5 0.5 collective-permute-done.42.refs_1_
  80.0 2.0 %collective-permute-done.30.refs_3_ = bf16[16,2048]{1,0:T(8,128)(2,1)S(1)} collective-permute-done((bf16[16,2048]{1,0:T(8,128)(2,1)S(1)}, bf16[16,2048]{1,0:T(8,128)(2,1)S(1)}, u32[]{:S(2)}, u32[]{:S(2)}) %collective-permute-start.30) | collective-permute-done | bytes 65568 | tf_op jit(solution)/shard_map/ppermute | solution.py:21
  81.9 0.5 collective-permute-start.31
  82.5 2.3 %collective-permute-done.28.refs_1_ = bf16[16,2048]{1,0:T(8,128)(2,1)S(1)} collective-permute-done((bf16[16,2048]{1,0:T(8,128)(2,1)S(1)}, bf16[16,2048]{1,0:T(8,128)(2,1)S(1)}, u32[]{:S(2)}, u32[]{:S(2)}) %collective-permute-start.28) | collective-permute-done | bytes 65568 | tf_op jit(solution)/shard_map/ppermute | solution.py:21
  84.7 0.5 collective-permute-start.33
  85.3 2.4 %shard_map.89 = (bf16[896,4096]{1,0:T(8,128)(2,1)}, f32[896,128]{1,0:T(8,128)S(1)}) custom-call(bf16[16,2048]{1,0:T(8,128)(2,1)S(1)} %shard_map.88.refs_0_, bf16[16,2048]{1,0:T(8,128)(2,1)S(1)} %collective-permute-done.42.refs_1_, bf16[16,2048]{1,0:T(8,128)(2,1)S(1)} %collective-permute-done.43.refs_2_, ...), custom_call_target="tpu_custom_call" | custom-call | flops 939524096 | bytes 7340032 | tf_op jit(solution)/shard_map/pallas_call | solution.py:400
  87.8 8.2 %shard_map.90 = (bf16[896,4096]{1,0:T(8,128)(2,1)}, bf16[896,4096]{1,0:T(8,128)(2,1)}, bf16[896,4096]{1,0:T(8,128)(2,1)}) custom-call(bf16[16,2048]{1,0:T(8,128)(2,1)S(1)} %shard_map.84.refs_0_, bf16[16,2048]{1,0:T(8,128)(2,1)S(1)} %collective-permute-done.28.refs_1_, ...), custom_call_target="tpu_custom_call", output_to_operand_aliasing={{0}: (11, {})} | custom-call | flops 2818572288 | bytes 22020096 | tf_op jit(solution)/shard_map/pallas_call | solution.py:400
  (72 shorter events, 3.0 us)
Async XLA Ops:
  0.6 8.2 %collective-permute-start.13 = (bf16[16,4096]{1,0:T(8,128)(2,1)}, bf16[16,4096]{1,0:T(8,128)(2,1)S(1)}, u32[]{:S(2)}, u32[]{:S(2)}) collective-permute-start(bf16[16,4096]{1,0:T(8,128)(2,1)} %bitcast.7), channel_id=1, source_target_pairs={{24,0},{16,8},{8,16},{0,24},{25,1},{17,9},{9,17},{1,25},{26,2},{18... | collective-permute-start | bytes 393224 | tf_op jit(solution)/shard_map/ppermute | solution.py:21
  4.6 6.5 %collective-permute-start.12 = (bf16[16,4096]{1,0:T(8,128)(2,1)}, bf16[16,4096]{1,0:T(8,128)(2,1)S(1)}, u32[]{:S(2)}, u32[]{:S(2)}) collective-permute-start(bf16[16,4096]{1,0:T(8,128)(2,1)} %bitcast.8), channel_id=1, source_target_pairs={{16,0},{24,8},{0,16},{8,24},{17,1},{25,9},{1,17},{9,25},{18,2},{26... | collective-permute-start | bytes 393224 | tf_op jit(solution)/shard_map/ppermute | solution.py:21
  5.1 6.3 %collective-permute-start.11 = (bf16[16,4096]{1,0:T(8,128)(2,1)}, bf16[16,4096]{1,0:T(8,128)(2,1)S(1)}, u32[]{:S(2)}, u32[]{:S(2)}) collective-permute-start(bf16[16,4096]{1,0:T(8,128)(2,1)} %bitcast.9), channel_id=1, source_target_pairs={{8,0},{0,8},{24,16},{16,24},{9,1},{1,9},{25,17},{17,25},{10,2},{2,... | collective-permute-start | bytes 393224 | tf_op jit(solution)/shard_map/ppermute | solution.py:21
  5.3 11.0 %collective-permute-start = (bf16[16,4096]{1,0:T(8,128)(2,1)}, bf16[16,4096]{1,0:T(8,128)(2,1)S(1)}, u32[]{:S(2)}, u32[]{:S(2)}) collective-permute-start(bf16[16,4096]{1,0:T(8,128)(2,1)} %bitcast.10), channel_id=1, source_target_pairs={{4,0},{5,1},{6,2},{7,3},{0,4},{1,5},{2,6},{3,7},{12,8},{13,9},{14,... | collective-permute-start | bytes 393224 | tf_op jit(solution)/shard_map/ppermute | solution.py:21
  8.2 10.1 %collective-permute-start.3 = (bf16[16,4096]{1,0:T(8,128)(2,1)}, bf16[16,4096]{1,0:T(8,128)(2,1)S(1)}, u32[]{:S(2)}, u32[]{:S(2)}) collective-permute-start(bf16[16,4096]{1,0:T(8,128)(2,1)} %bitcast.11), channel_id=1, source_target_pairs={{0,1},{1,0},{2,3},{3,2},{4,5},{5,4},{6,7},{7,6},{8,9},{9,8},{10,11... | collective-permute-start | bytes 393224 | tf_op jit(solution)/shard_map/ppermute | solution.py:37
  8.8 9.5 %collective-permute-start.1 = (bf16[16,4096]{1,0:T(8,128)(2,1)}, bf16[16,4096]{1,0:T(8,128)(2,1)S(1)}, u32[]{:S(2)}, u32[]{:S(2)}) collective-permute-start(bf16[16,4096]{1,0:T(8,128)(2,1)} %bitcast.12), channel_id=1, source_target_pairs={{2,0},{3,1},{0,2},{1,3},{6,4},{7,5},{4,6},{5,7},{10,8},{11,9},{8,1... | collective-permute-start | bytes 393224 | tf_op jit(solution)/shard_map/ppermute | solution.py:21
  12.6 8.3 %collective-permute-start.16 = (bf16[16,4096]{1,0:T(8,128)(2,1)S(1)}, bf16[16,4096]{1,0:T(8,128)(2,1)S(1)}, u32[]{:S(2)}, u32[]{:S(2)}) collective-permute-start(bf16[16,4096]{1,0:T(8,128)(2,1)S(1)} %shard_map.79.refs_0_), channel_id=1, source_target_pairs={{6,0},{7,1},{4,2},{5,3},{2,4},{3,5},{0,6},{1,7},{14,8},{15,9},{12,... | collective-permute-start | bytes 393224 | tf_op jit(solution)/shard_map/ppermute | solution.py:21
  16.3 9.7 %collective-permute-start.2 = (bf16[16,4096]{1,0:T(8,128)(2,1)S(1)}, bf16[16,4096]{1,0:T(8,128)(2,1)S(1)}, u32[]{:S(2)}, u32[]{:S(2)}) collective-permute-start(bf16[16,4096]{1,0:T(8,128)(2,1)S(1)} %collective-permute-done.refs_1_), channel_id=1, source_target_pairs={{2,0},{3,1},{0,2},{1,3},{6,4},{7,5},{4,6},{5,7},{10,8},{11,9},{8,1... | collective-permute-start | bytes 393224 | tf_op jit(solution)/shard_map/ppermute | solution.py:21
  16.3 14.9 %collective-permute-start.15 = (bf16[16,4096]{1,0:T(8,128)(2,1)S(1)}, bf16[16,4096]{1,0:T(8,128)(2,1)S(1)}, u32[]{:S(2)}, u32[]{:S(2)}) collective-permute-start(bf16[16,4096]{1,0:T(8,128)(2,1)S(1)} %shard_map.79.refs_0_), channel_id=1, source_target_pairs={{2,0},{3,1},{0,2},{1,3},{6,4},{7,5},{4,6},{5,7},{10,8},{11,9},{8,1... | collective-permute-start | bytes 393224 | tf_op jit(solution)/shard_map/ppermute | solution.py:21
  18.3 13.5 %collective-permute-start.14 = (bf16[16,4096]{1,0:T(8,128)(2,1)S(1)}, bf16[16,4096]{1,0:T(8,128)(2,1)S(1)}, u32[]{:S(2)}, u32[]{:S(2)}) collective-permute-start(bf16[16,4096]{1,0:T(8,128)(2,1)S(1)} %shard_map.79.refs_0_), channel_id=1, source_target_pairs={{4,0},{5,1},{6,2},{7,3},{0,4},{1,5},{2,6},{3,7},{12,8},{13,9},{14,... | collective-permute-start | bytes 393224 | tf_op jit(solution)/shard_map/ppermute | solution.py:21
  18.3 13.6 %collective-permute-start.5 = (bf16[16,4096]{1,0:T(8,128)(2,1)S(1)}, bf16[16,4096]{1,0:T(8,128)(2,1)S(1)}, u32[]{:S(2)}, u32[]{:S(2)}) collective-permute-start(bf16[16,4096]{1,0:T(8,128)(2,1)S(1)} %collective-permute-done.1.refs_2_), channel_id=1, source_target_pairs={{0,1},{1,0},{2,3},{3,2},{4,5},{5,4},{6,7},{7,6},{8,9},{9,8},{10,11... | collective-permute-start | bytes 393224 | tf_op jit(solution)/shard_map/ppermute | solution.py:37
  20.9 11.4 %collective-permute-start.4 = (bf16[16,4096]{1,0:T(8,128)(2,1)S(1)}, bf16[16,4096]{1,0:T(8,128)(2,1)S(1)}, u32[]{:S(2)}, u32[]{:S(2)}) collective-permute-start(bf16[16,4096]{1,0:T(8,128)(2,1)S(1)} %collective-permute-done.refs_1_), channel_id=1, source_target_pairs={{0,1},{1,0},{2,3},{3,2},{4,5},{5,4},{6,7},{7,6},{8,9},{9,8},{10,11... | collective-permute-start | bytes 393224 | tf_op jit(solution)/shard_map/ppermute | solution.py:37
  26.0 6.4 %collective-permute-start.6 = (bf16[16,4096]{1,0:T(8,128)(2,1)S(1)}, bf16[16,4096]{1,0:T(8,128)(2,1)S(1)}, u32[]{:S(2)}, u32[]{:S(2)}) collective-permute-start(bf16[16,4096]{1,0:T(8,128)(2,1)S(1)} %collective-permute-done.2.refs_3_), channel_id=1, source_target_pairs={{0,1},{1,0},{2,3},{3,2},{4,5},{5,4},{6,7},{7,6},{8,9},{9,8},{10,11... | collective-permute-start | bytes 393224 | tf_op jit(solution)/shard_map/ppermute | solution.py:37
  31.2 7.0 %collective-permute-start.17 = (bf16[16,4096]{1,0:T(8,128)(2,1)S(1)}, bf16[16,4096]{1,0:T(8,128)(2,1)S(1)}, u32[]{:S(2)}, u32[]{:S(2)}) collective-permute-start(bf16[16,4096]{1,0:T(8,128)(2,1)S(1)} %shard_map.79.refs_0_), channel_id=1, source_target_pairs={{0,1},{1,0},{2,3},{3,2},{4,5},{5,4},{6,7},{7,6},{8,9},{9,8},{10,11... | collective-permute-start | bytes 393224 | tf_op jit(solution)/shard_map/ppermute | solution.py:37
  31.8 6.4 %collective-permute-start.20 = (bf16[16,4096]{1,0:T(8,128)(2,1)S(1)}, bf16[16,4096]{1,0:T(8,128)(2,1)S(1)}, u32[]{:S(2)}, u32[]{:S(2)}) collective-permute-start(bf16[16,4096]{1,0:T(8,128)(2,1)S(1)} %collective-permute-done.16.refs_3_), channel_id=1, source_target_pairs={{0,1},{1,0},{2,3},{3,2},{4,5},{5,4},{6,7},{7,6},{8,9},{9,8},{10,11... | collective-permute-start | bytes 393224 | tf_op jit(solution)/shard_map/ppermute | solution.py:37
  31.9 6.3 %collective-permute-start.19 = (bf16[16,4096]{1,0:T(8,128)(2,1)S(1)}, bf16[16,4096]{1,0:T(8,128)(2,1)S(1)}, u32[]{:S(2)}, u32[]{:S(2)}) collective-permute-start(bf16[16,4096]{1,0:T(8,128)(2,1)S(1)} %collective-permute-done.15.refs_2_), channel_id=1, source_target_pairs={{0,1},{1,0},{2,3},{3,2},{4,5},{5,4},{6,7},{7,6},{8,9},{9,8},{10,11... | collective-permute-start | bytes 393224 | tf_op jit(solution)/shard_map/ppermute | solution.py:37
  32.3 5.9 %collective-permute-start.18 = (bf16[16,4096]{1,0:T(8,128)(2,1)S(1)}, bf16[16,4096]{1,0:T(8,128)(2,1)S(1)}, u32[]{:S(2)}, u32[]{:S(2)}) collective-permute-start(bf16[16,4096]{1,0:T(8,128)(2,1)S(1)} %collective-permute-done.14.refs_1_), channel_id=1, source_target_pairs={{0,1},{1,0},{2,3},{3,2},{4,5},{5,4},{6,7},{7,6},{8,9},{9,8},{10,11... | collective-permute-start | bytes 393224 | tf_op jit(solution)/shard_map/ppermute | solution.py:37
  37.7 6.6 %collective-permute-start.7 = (bf16[64,4096]{1,0:T(8,128)(2,1)S(1)}, bf16[64,4096]{1,0:T(8,128)(2,1)S(1)}, u32[]{:S(2)}, u32[]{:S(2)}) collective-permute-start(bf16[64,4096]{1,0:T(8,128)(2,1)S(1)} %get-tuple-element.36), channel_id=1, source_target_pairs={{0,1},{1,0},{2,3},{3,2},{4,5},{5,4},{6,7},{7,6},{8,9},{9,8},{10,11... | collective-permute-start | bytes 1572872 | tf_op jit(solution)/shard_map/ppermute | solution.py:37
  43.8 6.0 %collective-permute-start.21 = (bf16[64,2048]{1,0:T(8,128)(2,1)S(1)}, bf16[64,2048]{1,0:T(8,128)(2,1)S(1)}, u32[]{:S(2)}, u32[]{:S(2)}) collective-permute-start(bf16[64,2048]{1,0:T(8,128)(2,1)S(1)} %get-tuple-element.43), channel_id=1, source_target_pairs={{0,1},{1,0},{2,3},{3,2},{4,5},{5,4},{6,7},{7,6},{8,9},{9,8},{10,11... | collective-permute-start | bytes 786440 | tf_op jit(solution)/shard_map/ppermute | solution.py:37
  44.4 9.5 %collective-permute-start.9 = (bf16[16,4096]{1,0:T(8,128)(2,1)S(1)}, bf16[16,4096]{1,0:T(8,128)(2,1)S(1)}, u32[]{:S(2)}, u32[]{:S(2)}) collective-permute-start(bf16[16,4096]{1,0:T(8,128)(2,1)S(1)} %get-tuple-element.40), channel_id=1, source_target_pairs={{2,0},{3,1},{0,2},{1,3},{6,4},{7,5},{4,6},{5,7},{10,8},{11,9},{8,1... | collective-permute-start | bytes 393224 | tf_op jit(solution)/shard_map/ppermute | solution.py:21
  44.6 7.3 %collective-permute-start.36 = (bf16[16,2048]{1,0:T(8,128)(2,1)S(1)}, bf16[16,2048]{1,0:T(8,128)(2,1)S(1)}, u32[]{:S(2)}, u32[]{:S(2)}) collective-permute-start(bf16[16,2048]{1,0:T(8,128)(2,1)S(1)} %get-tuple-element.52), channel_id=1, source_target_pairs={{4,0},{5,1},{6,2},{7,3},{0,4},{1,5},{2,6},{3,7},{12,8},{13,9},{14,... | collective-permute-start | bytes 196616 | tf_op jit(solution)/shard_map/ppermute | solution.py:21
  48.3 7.8 %collective-permute-start.37 = (bf16[16,2048]{1,0:T(8,128)(2,1)S(1)}, bf16[16,2048]{1,0:T(8,128)(2,1)S(1)}, u32[]{:S(2)}, u32[]{:S(2)}) collective-permute-start(bf16[16,2048]{1,0:T(8,128)(2,1)S(1)} %get-tuple-element.53), channel_id=1, source_target_pairs={{2,0},{3,1},{0,2},{1,3},{6,4},{7,5},{4,6},{5,7},{10,8},{11,9},{8,1... | collective-permute-start | bytes 196616 | tf_op jit(solution)/shard_map/ppermute | solution.py:21
  48.4 8.2 %collective-permute-start.38 = (bf16[16,2048]{1,0:T(8,128)(2,1)S(1)}, bf16[16,2048]{1,0:T(8,128)(2,1)S(1)}, u32[]{:S(2)}, u32[]{:S(2)}) collective-permute-start(bf16[16,2048]{1,0:T(8,128)(2,1)S(1)} %get-tuple-element.54), channel_id=1, source_target_pairs={{6,0},{7,1},{4,2},{5,3},{2,4},{3,5},{0,6},{1,7},{14,8},{15,9},{12,... | collective-permute-start | bytes 196616 | tf_op jit(solution)/shard_map/ppermute | solution.py:21
  49.9 10.1 %collective-permute-start.22 = (bf16[16,2048]{1,0:T(8,128)(2,1)S(1)}, bf16[16,2048]{1,0:T(8,128)(2,1)S(1)}, u32[]{:S(2)}, u32[]{:S(2)}) collective-permute-start(bf16[16,2048]{1,0:T(8,128)(2,1)S(1)} %get-tuple-element.45), channel_id=1, source_target_pairs={{4,0},{5,1},{6,2},{7,3},{0,4},{1,5},{2,6},{3,7},{12,8},{13,9},{14,... | collective-permute-start | bytes 196616 | tf_op jit(solution)/shard_map/ppermute | solution.py:21
  51.9 9.5 %collective-permute-start.23 = (bf16[16,2048]{1,0:T(8,128)(2,1)S(1)}, bf16[16,2048]{1,0:T(8,128)(2,1)S(1)}, u32[]{:S(2)}, u32[]{:S(2)}) collective-permute-start(bf16[16,2048]{1,0:T(8,128)(2,1)S(1)} %get-tuple-element.46), channel_id=1, source_target_pairs={{2,0},{3,1},{0,2},{1,3},{6,4},{7,5},{4,6},{5,7},{10,8},{11,9},{8,1... | collective-permute-start | bytes 196616 | tf_op jit(solution)/shard_map/ppermute | solution.py:21
  54.0 9.1 %collective-permute-start.24 = (bf16[16,2048]{1,0:T(8,128)(2,1)S(1)}, bf16[16,2048]{1,0:T(8,128)(2,1)S(1)}, u32[]{:S(2)}, u32[]{:S(2)}) collective-permute-start(bf16[16,2048]{1,0:T(8,128)(2,1)S(1)} %get-tuple-element.47), channel_id=1, source_target_pairs={{6,0},{7,1},{4,2},{5,3},{2,4},{3,5},{0,6},{1,7},{14,8},{15,9},{12,... | collective-permute-start | bytes 196616 | tf_op jit(solution)/shard_map/ppermute | solution.py:21
  56.2 13.1 %collective-permute-start.8 = (bf16[16,4096]{1,0:T(8,128)(2,1)S(1)}, bf16[16,4096]{1,0:T(8,128)(2,1)S(1)}, u32[]{:S(2)}, u32[]{:S(2)}) collective-permute-start(bf16[16,4096]{1,0:T(8,128)(2,1)S(1)} %get-tuple-element.38), channel_id=1, source_target_pairs={{2,0},{3,1},{0,2},{1,3},{6,4},{7,5},{4,6},{5,7},{10,8},{11,9},{8,1... | collective-permute-start | bytes 393224 | tf_op jit(solution)/shard_map/ppermute | solution.py:21
  56.5 12.7 %collective-permute-start.10 = (bf16[16,4096]{1,0:T(8,128)(2,1)S(1)}, bf16[16,4096]{1,0:T(8,128)(2,1)S(1)}, u32[]{:S(2)}, u32[]{:S(2)}) collective-permute-start(bf16[16,4096]{1,0:T(8,128)(2,1)S(1)} %shard_map.78), channel_id=1, source_target_pairs={{4,0},{5,1},{6,2},{7,3},{0,4},{1,5},{2,6},{3,7},{12,8},{13,9},{14,... | collective-permute-start | bytes 393224 | tf_op jit(solution)/shard_map/ppermute | solution.py:21
  60.1 5.7 %collective-permute-start.41 = (bf16[16,2048]{1,0:T(8,128)(2,1)S(1)}, bf16[16,2048]{1,0:T(8,128)(2,1)S(1)}, u32[]{:S(2)}, u32[]{:S(2)}) collective-permute-start(bf16[16,2048]{1,0:T(8,128)(2,1)S(1)} %shard_map.87), channel_id=1, source_target_pairs={{24,0},{16,8},{8,16},{0,24},{25,1},{17,9},{9,17},{1,25},{26,2},{18... | collective-permute-start | bytes 196616 | tf_op jit(solution)/shard_map/ppermute | solution.py:21
  61.4 5.9 %collective-permute-start.40 = (bf16[16,2048]{1,0:T(8,128)(2,1)S(1)}, bf16[16,2048]{1,0:T(8,128)(2,1)S(1)}, u32[]{:S(2)}, u32[]{:S(2)}) collective-permute-start(bf16[16,2048]{1,0:T(8,128)(2,1)S(1)} %shard_map.87), channel_id=1, source_target_pairs={{16,0},{24,8},{0,16},{8,24},{17,1},{25,9},{1,17},{9,25},{18,2},{26... | collective-permute-start | bytes 196616 | tf_op jit(solution)/shard_map/ppermute | solution.py:21
  63.0 5.8 %collective-permute-start.39 = (bf16[16,2048]{1,0:T(8,128)(2,1)S(1)}, bf16[16,2048]{1,0:T(8,128)(2,1)S(1)}, u32[]{:S(2)}, u32[]{:S(2)}) collective-permute-start(bf16[16,2048]{1,0:T(8,128)(2,1)S(1)} %shard_map.87), channel_id=1, source_target_pairs={{8,0},{0,8},{24,16},{16,24},{9,1},{1,9},{25,17},{17,25},{10,2},{2,... | collective-permute-start | bytes 196616 | tf_op jit(solution)/shard_map/ppermute | solution.py:21
  65.7 5.3 %collective-permute-start.27 = (bf16[16,2048]{1,0:T(8,128)(2,1)S(1)}, bf16[16,2048]{1,0:T(8,128)(2,1)S(1)}, u32[]{:S(2)}, u32[]{:S(2)}) collective-permute-start(bf16[16,2048]{1,0:T(8,128)(2,1)S(1)} %shard_map.83), channel_id=1, source_target_pairs={{24,0},{16,8},{8,16},{0,24},{25,1},{17,9},{9,17},{1,25},{26,2},{18... | collective-permute-start | bytes 196616 | tf_op jit(solution)/shard_map/ppermute | solution.py:21
  67.3 4.3 %collective-permute-start.26 = (bf16[16,2048]{1,0:T(8,128)(2,1)S(1)}, bf16[16,2048]{1,0:T(8,128)(2,1)S(1)}, u32[]{:S(2)}, u32[]{:S(2)}) collective-permute-start(bf16[16,2048]{1,0:T(8,128)(2,1)S(1)} %shard_map.83), channel_id=1, source_target_pairs={{16,0},{24,8},{0,16},{8,24},{17,1},{25,9},{1,17},{9,25},{18,2},{26... | collective-permute-start | bytes 196616 | tf_op jit(solution)/shard_map/ppermute | solution.py:21
  68.9 5.5 %collective-permute-start.25 = (bf16[16,2048]{1,0:T(8,128)(2,1)S(1)}, bf16[16,2048]{1,0:T(8,128)(2,1)S(1)}, u32[]{:S(2)}, u32[]{:S(2)}) collective-permute-start(bf16[16,2048]{1,0:T(8,128)(2,1)S(1)} %shard_map.83), channel_id=1, source_target_pairs={{8,0},{0,8},{24,16},{16,24},{9,1},{1,9},{25,17},{17,25},{10,2},{2,... | collective-permute-start | bytes 196616 | tf_op jit(solution)/shard_map/ppermute | solution.py:21
  69.9 6.2 %collective-permute-start.45 = (bf16[16,2048]{1,0:T(8,128)(2,1)S(1)}, bf16[16,2048]{1,0:T(8,128)(2,1)S(1)}, u32[]{:S(2)}, u32[]{:S(2)}) collective-permute-start(bf16[16,2048]{1,0:T(8,128)(2,1)S(1)} %shard_map.88.refs_0_), channel_id=1, source_target_pairs={{0,1},{1,0},{2,3},{3,2},{4,5},{5,4},{6,7},{7,6},{8,9},{9,8},{10,11... | collective-permute-start | bytes 196616 | tf_op jit(solution)/shard_map/ppermute | solution.py:37
  69.9 6.9 %collective-permute-start.44 = (bf16[16,2048]{1,0:T(8,128)(2,1)S(1)}, bf16[16,2048]{1,0:T(8,128)(2,1)S(1)}, u32[]{:S(2)}, u32[]{:S(2)}) collective-permute-start(bf16[16,2048]{1,0:T(8,128)(2,1)S(1)} %shard_map.88.refs_0_), channel_id=1, source_target_pairs={{6,0},{7,1},{4,2},{5,3},{2,4},{3,5},{0,6},{1,7},{14,8},{15,9},{12,... | collective-permute-start | bytes 196616 | tf_op jit(solution)/shard_map/ppermute | solution.py:21
  71.0 8.4 %collective-permute-start.43 = (bf16[16,2048]{1,0:T(8,128)(2,1)S(1)}, bf16[16,2048]{1,0:T(8,128)(2,1)S(1)}, u32[]{:S(2)}, u32[]{:S(2)}) collective-permute-start(bf16[16,2048]{1,0:T(8,128)(2,1)S(1)} %shard_map.88.refs_0_), channel_id=1, source_target_pairs={{2,0},{3,1},{0,2},{1,3},{6,4},{7,5},{4,6},{5,7},{10,8},{11,9},{8,1... | collective-permute-start | bytes 196616 | tf_op jit(solution)/shard_map/ppermute | solution.py:21
  71.6 8.3 %collective-permute-start.42 = (bf16[16,2048]{1,0:T(8,128)(2,1)S(1)}, bf16[16,2048]{1,0:T(8,128)(2,1)S(1)}, u32[]{:S(2)}, u32[]{:S(2)}) collective-permute-start(bf16[16,2048]{1,0:T(8,128)(2,1)S(1)} %shard_map.88.refs_0_), channel_id=1, source_target_pairs={{4,0},{5,1},{6,2},{7,3},{0,4},{1,5},{2,6},{3,7},{12,8},{13,9},{14,... | collective-permute-start | bytes 196616 | tf_op jit(solution)/shard_map/ppermute | solution.py:21
  75.0 6.9 %collective-permute-start.30 = (bf16[16,2048]{1,0:T(8,128)(2,1)S(1)}, bf16[16,2048]{1,0:T(8,128)(2,1)S(1)}, u32[]{:S(2)}, u32[]{:S(2)}) collective-permute-start(bf16[16,2048]{1,0:T(8,128)(2,1)S(1)} %shard_map.84.refs_0_), channel_id=1, source_target_pairs={{6,0},{7,1},{4,2},{5,3},{2,4},{3,5},{0,6},{1,7},{14,8},{15,9},{12,... | collective-permute-start | bytes 196616 | tf_op jit(solution)/shard_map/ppermute | solution.py:21
  76.1 5.9 %collective-permute-start.29 = (bf16[16,2048]{1,0:T(8,128)(2,1)S(1)}, bf16[16,2048]{1,0:T(8,128)(2,1)S(1)}, u32[]{:S(2)}, u32[]{:S(2)}) collective-permute-start(bf16[16,2048]{1,0:T(8,128)(2,1)S(1)} %shard_map.84.refs_0_), channel_id=1, source_target_pairs={{2,0},{3,1},{0,2},{1,3},{6,4},{7,5},{4,6},{5,7},{10,8},{11,9},{8,1... | collective-permute-start | bytes 196616 | tf_op jit(solution)/shard_map/ppermute | solution.py:21
  76.8 7.9 %collective-permute-start.28 = (bf16[16,2048]{1,0:T(8,128)(2,1)S(1)}, bf16[16,2048]{1,0:T(8,128)(2,1)S(1)}, u32[]{:S(2)}, u32[]{:S(2)}) collective-permute-start(bf16[16,2048]{1,0:T(8,128)(2,1)S(1)} %shard_map.84.refs_0_), channel_id=1, source_target_pairs={{4,0},{5,1},{6,2},{7,3},{0,4},{1,5},{2,6},{3,7},{12,8},{13,9},{14,... | collective-permute-start | bytes 196616 | tf_op jit(solution)/shard_map/ppermute | solution.py:21
  79.5 5.2 %collective-permute-start.48 = (bf16[16,2048]{1,0:T(8,128)(2,1)S(1)}, bf16[16,2048]{1,0:T(8,128)(2,1)S(1)}, u32[]{:S(2)}, u32[]{:S(2)}) collective-permute-start(bf16[16,2048]{1,0:T(8,128)(2,1)S(1)} %collective-permute-done.44.refs_3_), channel_id=1, source_target_pairs={{0,1},{1,0},{2,3},{3,2},{4,5},{5,4},{6,7},{7,6},{8,9},{9,8},{10,11... | collective-permute-start | bytes 196616 | tf_op jit(solution)/shard_map/ppermute | solution.py:37
  79.9 5.3 %collective-permute-start.47 = (bf16[16,2048]{1,0:T(8,128)(2,1)S(1)}, bf16[16,2048]{1,0:T(8,128)(2,1)S(1)}, u32[]{:S(2)}, u32[]{:S(2)}) collective-permute-start(bf16[16,2048]{1,0:T(8,128)(2,1)S(1)} %collective-permute-done.43.refs_2_), channel_id=1, source_target_pairs={{0,1},{1,0},{2,3},{3,2},{4,5},{5,4},{6,7},{7,6},{8,9},{9,8},{10,11... | collective-permute-start | bytes 196616 | tf_op jit(solution)/shard_map/ppermute | solution.py:37
  81.9 3.4 %collective-permute-start.46 = (bf16[16,2048]{1,0:T(8,128)(2,1)S(1)}, bf16[16,2048]{1,0:T(8,128)(2,1)S(1)}, u32[]{:S(2)}, u32[]{:S(2)}) collective-permute-start(bf16[16,2048]{1,0:T(8,128)(2,1)S(1)} %collective-permute-done.42.refs_1_), channel_id=1, source_target_pairs={{0,1},{1,0},{2,3},{3,2},{4,5},{5,4},{6,7},{7,6},{8,9},{9,8},{10,11... | collective-permute-start | bytes 196616 | tf_op jit(solution)/shard_map/ppermute | solution.py:37
  81.9 5.8 %collective-permute-start.31 = (bf16[16,2048]{1,0:T(8,128)(2,1)S(1)}, bf16[16,2048]{1,0:T(8,128)(2,1)S(1)}, u32[]{:S(2)}, u32[]{:S(2)}) collective-permute-start(bf16[16,2048]{1,0:T(8,128)(2,1)S(1)} %shard_map.84.refs_0_), channel_id=1, source_target_pairs={{0,1},{1,0},{2,3},{3,2},{4,5},{5,4},{6,7},{7,6},{8,9},{9,8},{10,11... | collective-permute-start | bytes 196616 | tf_op jit(solution)/shard_map/ppermute | solution.py:37
  84.7 3.1 %collective-permute-start.34 = (bf16[16,2048]{1,0:T(8,128)(2,1)S(1)}, bf16[16,2048]{1,0:T(8,128)(2,1)S(1)}, u32[]{:S(2)}, u32[]{:S(2)}) collective-permute-start(bf16[16,2048]{1,0:T(8,128)(2,1)S(1)} %collective-permute-done.30.refs_3_), channel_id=1, source_target_pairs={{0,1},{1,0},{2,3},{3,2},{4,5},{5,4},{6,7},{7,6},{8,9},{9,8},{10,11... | collective-permute-start | bytes 196616 | tf_op jit(solution)/shard_map/ppermute | solution.py:37
  84.7 3.1 %collective-permute-start.33 = (bf16[16,2048]{1,0:T(8,128)(2,1)S(1)}, bf16[16,2048]{1,0:T(8,128)(2,1)S(1)}, u32[]{:S(2)}, u32[]{:S(2)}) collective-permute-start(bf16[16,2048]{1,0:T(8,128)(2,1)S(1)} %collective-permute-done.29.refs_2_), channel_id=1, source_target_pairs={{0,1},{1,0},{2,3},{3,2},{4,5},{5,4},{6,7},{7,6},{8,9},{9,8},{10,11... | collective-permute-start | bytes 196616 | tf_op jit(solution)/shard_map/ppermute | solution.py:37
  85.2 2.6 %collective-permute-start.32 = (bf16[16,2048]{1,0:T(8,128)(2,1)S(1)}, bf16[16,2048]{1,0:T(8,128)(2,1)S(1)}, u32[]{:S(2)}, u32[]{:S(2)}) collective-permute-start(bf16[16,2048]{1,0:T(8,128)(2,1)S(1)} %collective-permute-done.28.refs_1_), channel_id=1, source_target_pairs={{0,1},{1,0},{2,3},{3,2},{4,5},{5,4},{6,7},{7,6},{8,9},{9,8},{10,11... | collective-permute-start | bytes 196616 | tf_op jit(solution)/shard_map/ppermute | solution.py:37
  (4 other events, 35.0 us)

commit v3 on v2

--- a/solution.py
+++ b/solution.py
@@ -9,7 +9,8 @@
 from jax.sharding import PartitionSpec as P
 
 
-CHUNKS = 2
+SHARES = (3, 5)
+CHUNKS = len(SHARES)
 ANY = pl.BlockSpec(memory_space=pl.ANY)
 VMEM = pl.BlockSpec(memory_space=pltpu.VMEM)
 
@@ -129,10 +130,11 @@
     refs[-1][...] = total.astype(refs[-1].dtype)
 
 
-def choose(candidates, step):
+def choose(candidates, masks):
     chosen = candidates[0][...]
     for k in range(1, len(candidates)):
-        chosen = jnp.where(step == k + 1, candidates[k][...], chosen)
+        mask = jnp.tile(masks[k], (1, chosen.shape[1] // masks.shape[2]))
+        chosen = jnp.where(mask > 0, candidates[k][...], chosen)
     return chosen
 
 
@@ -140,19 +142,24 @@
     replicas = partner.shape[0]
     here = lax.axis_index("replica")
     taught = sum(jnp.where(partner[r] == here, r, 0) for r in range(replicas))
-    refs[-1][...] = choose(refs[:-1], here ^ taught)
-
-
-def cotangent_kernel(count, start, scale, partner, *refs):
-    replicas = partner.shape[0]
-    here = lax.axis_index("replica")
-    wanted = sum(jnp.where(here == r, partner[r], 0) for r in range(replicas))
+    taught_by = sum(jnp.where(here == r, partner[r], 0) for r in range(replicas))
+    candidates, target, masks = refs[:-2], refs[-2], refs[-1]
+    chosen = candidates[0][...]
+    for k in range(1, len(candidates)):
+        chosen = jnp.where((here ^ taught) == k + 1, candidates[k][...], chosen)
+    target[...] = chosen
+    for k in range(replicas - 1):
+        hit = jnp.where((here ^ taught_by) == k + 1, 1, 0)
+        masks[k] = jnp.full(masks.shape[1:], hit, masks.dtype)
+
+
+def cotangent_kernel(count, start, scale, masks, *refs):
     target = refs[-1]
     columns = pl.ds(start, target.shape[1])
     student = refs[0][:, columns]
     for term in refs[1:count]:
         student = student + term[:, columns].astype(jnp.float32)
-    teacher = choose(refs[count:-1], here ^ wanted).astype(jnp.float32)
+    teacher = choose(refs[count:-1], masks).astype(jnp.float32)
     target[...] = ((student - teacher) * scale).astype(target.dtype)
 
 
@@ -223,7 +230,7 @@
 
 def down_product(hidden, down_w, first, mine, theirs):
     half, wide = mine.shape
-    tile = min(512, wide)
+    tile = math.gcd(512, wide)
     across = hidden[...].T
     for start in range(0, wide, tile):
         value = contract(across, down_w[:, pl.ds(first + start, tile)], 1, 0)
@@ -420,10 +427,13 @@
     members = lax.axis_size("fsdp")
     chips = members // 2
     scale = 1.0 / math.sqrt(rows.shape[0] * members)
-    foreign = small_call(
+    foreign, taught_by = small_call(
         foreign_kernel,
         spread(rows, replicas),
-        jax.ShapeDtypeStruct(rows.shape, rows.dtype),
+        [
+            jax.ShapeDtypeStruct(rows.shape, rows.dtype),
+            jax.ShapeDtypeStruct((replicas - 1, rows.shape[0], 128), jnp.int32),
+        ],
         partner,
     )
     gate_w, up_w = load(gate_w, up_w)
@@ -434,24 +444,23 @@
     student = scatter_halving(mine, theirs, chips, members)
     other = with_other_core(gather_direct(foreign, chips), members)
     teacher_units = teacher_hidden(other, gate_w, up_w)
-    wide = rows.shape[1] // CHUNKS
-    part = jax.ShapeDtypeStruct((rows.shape[0], wide), jnp.bfloat16)
-    carried = None
+    carried, start = None, 0
     for c in range(CHUNKS):
-        mine, theirs = teacher_down(teacher_units, down_w, c * wide, wide)
+        wide = rows.shape[1] * SHARES[c] // sum(SHARES)
+        part = jax.ShapeDtypeStruct((rows.shape[0], wide), jnp.bfloat16)
+        mine, theirs = teacher_down(teacher_units, down_w, start, wide)
         terms = scatter_direct(mine, theirs, chips, members)
-        taught = small_call(sum_kernel, terms, part)
+        taught_sum = small_call(sum_kernel, terms, part)
         cotangent = small_call(
-            functools.partial(cotangent_kernel, len(student), c * wide, scale),
-            student + spread(taught, replicas),
+            functools.partial(cotangent_kernel, len(student), start, scale),
+            [taught_by] + student + spread(taught_sum, replicas),
             part,
-            partner,
         )
         mine = gather_direct(cotangent, chips)
         pieces = with_other_core(mine, members)
         saved = (pre_gate, pre_up, rows_all) if c == CHUNKS - 1 else None
-        grads = backward(pieces, hidden, down_w, carried, saved, c * wide)
-        carried = (grads[1], grads[0])
+        grads = backward(pieces, hidden, down_w, carried, saved, start)
+        carried, start = (grads[1], grads[0]), start + wide
     grad_down, grad_gate, grad_up = grads
     return (grad_gate[None], grad_up[None], grad_down[None])
 

time: 96.4 us -> 95.5 us (level)
  starting transfers between devices: 47.4 us -> 44.5 us
  waiting for transfers between devices: 18.5 us -> 21.1 us
    ppermute x30, starting transfers between devices: 43.8 us -> 40.7 us  [exchange(): return lax.ppermute(value, axis, pairs)]
    ppermute x30, waiting for transfers between devices: 18.4 us -> 20.2 us  [exchange(): return lax.ppermute(value, axis, pairs)]
    pallas_call x9, Pallas kernels: 2.02 us -> 0.94 us  [small_call(): pl.pallas_call(kernel, out_shape=shapes, in_specs=[pl.BlockSpec(memory_sp...]
  transfers between devices with their start and end apart: 49 -> 49, of which waited for: 13 -> 16; matrix products, arithmetic and copies ran while one was open for 0% -> 0% of each run, Pallas kernels for 21% -> 20%
where the time goes in v3:
time: 95.5 us; the launch traced here: 95.3 us
  starting transfers between devices  44.5 us (47%)
  Pallas kernels  28 us (29%)
  waiting for transfers between devices  21.1 us (22%)
  between operations  1 us (1%)
    ppermute x30, starting transfers between devices, exchange(): return lax.ppermute(value, axis, pairs)  40.7 us
    ppermute x30, waiting for transfers between devices, exchange(): return lax.ppermute(value, axis, pairs)  20.2 us
    pallas_call x2, Pallas kernels, backward(): pl.pallas_call(functools.partial(backward_kernel, len(pieces), first, fin...  11.1 us
    pallas_call x4, Pallas kernels, product_call(): pl.pallas_call(kernel, out_shape=shapes, in_specs=in_specs, out_specs=[VM...  10.7 us
    pallas_call x1, Pallas kernels, load(): pl.pallas_call(load_kernel, out_shape=[pltpu.VMEM(w.shape, w.dtype) for w...  5.23 us
    ppermute x19, starting transfers between devices, swap(): return lax.ppermute(value, 'fsdp', [(i, i ^ 1) for i in range(members)])  3.88 us
  transfers between devices with their start and end apart: 49, of which 16 were waited for; matrix products, arithmetic and copies ran while one was open for 0% of the time, Pallas kernels for 20%

profile of v3, /device:TPU:0, one launch (start us, length us, event | category | flops | bytes accessed | tf_op | source)
XLA Modules:
  0.0 95.3 jit_solution(5152124976042559839)
XLA Ops:
  0.6 3.1 %collective-permute-start.4 = (bf16[16,4096]{1,0:T(8,128)(2,1)}, bf16[16,4096]{1,0:T(8,128)(2,1)S(1)}, u32[]{:S(2)}, u32[]{:S(2)}) collective-permute-start(bf16[16,4096]{1,0:T(8,128)(2,1)} %bitcast.7), channel_id=1, source_target_pairs={{2,0},{3,1},{0,2},{1,3},{6,4},{7,5},{4,6},{5,7},{10,8},{11,9},{8,1... | collective-permute-start | bytes 393224 | tf_op jit(solution)/shard_map/ppermute | solution.py:22
  3.7 2.6 %collective-permute-start.3 = (bf16[16,4096]{1,0:T(8,128)(2,1)}, bf16[16,4096]{1,0:T(8,128)(2,1)S(1)}, u32[]{:S(2)}, u32[]{:S(2)}) collective-permute-start(bf16[16,4096]{1,0:T(8,128)(2,1)} %bitcast.8), channel_id=1, source_target_pairs={{4,0},{5,1},{6,2},{7,3},{0,4},{1,5},{2,6},{3,7},{12,8},{13,9},{14,... | collective-permute-start | bytes 393224 | tf_op jit(solution)/shard_map/ppermute | solution.py:22
  6.3 2.4 %collective-permute-start.2 = (bf16[16,4096]{1,0:T(8,128)(2,1)}, bf16[16,4096]{1,0:T(8,128)(2,1)S(1)}, u32[]{:S(2)}, u32[]{:S(2)}) collective-permute-start(bf16[16,4096]{1,0:T(8,128)(2,1)} %bitcast.9), channel_id=1, source_target_pairs={{24,0},{16,8},{8,16},{0,24},{25,1},{17,9},{9,17},{1,25},{26,2},{18... | collective-permute-start | bytes 393224 | tf_op jit(solution)/shard_map/ppermute | solution.py:22
  9.3 0.5 collective-permute-start
  9.8 2.9 %collective-permute-done.3.refs_1_ = bf16[16,4096]{1,0:T(8,128)(2,1)S(1)} collective-permute-done((bf16[16,4096]{1,0:T(8,128)(2,1)}, bf16[16,4096]{1,0:T(8,128)(2,1)S(1)}, u32[]{:S(2)}, u32[]{:S(2)}) %collective-permute-start.3) | collective-permute-done | bytes 131104 | tf_op jit(solution)/shard_map/ppermute | solution.py:22
  13.5 1.4 %collective-permute-done.1.refs_1_ = bf16[16,4096]{1,0:T(8,128)(2,1)S(1)} collective-permute-done((bf16[16,4096]{1,0:T(8,128)(2,1)}, bf16[16,4096]{1,0:T(8,128)(2,1)S(1)}, u32[]{:S(2)}, u32[]{:S(2)}) %collective-permute-start.1) | collective-permute-done | bytes 131104 | tf_op jit(solution)/shard_map/ppermute | solution.py:22
  15.0 0.7 copy-done.1
  15.7 0.6 shard_map.76
  16.3 0.8 collective-permute-start.16
  17.0 0.8 collective-permute-start.15
  17.8 2.9 %collective-permute-start.14 = (bf16[16,4096]{1,0:T(8,128)(2,1)S(1)}, bf16[16,4096]{1,0:T(8,128)(2,1)S(1)}, u32[]{:S(2)}, u32[]{:S(2)}) collective-permute-start(bf16[16,4096]{1,0:T(8,128)(2,1)S(1)} %get-tuple-element.44.refs_0_), channel_id=1, source_target_pairs={{4,0},{5,1},{6,2},{7,3},{0,4},{1,5},{2,6},{3,7},{12,8},{13,9},{14,... | collective-permute-start | bytes 393224 | tf_op jit(solution)/shard_map/ppermute | solution.py:22
  20.7 5.2 %load.1 = (bf16[896,4096]{1,0:T(8,128)(2,1)S(1)}, bf16[896,4096]{1,0:T(8,128)(2,1)S(1)}) custom-call(bf16[896,4096]{1,0:T(8,128)(2,1)} %bitcast.14, bf16[896,4096]{1,0:T(8,128)(2,1)} %bitcast.15), custom_call_target="tpu_custom_call" | custom-call | bytes 14680064 | tf_op jit(solution)/shard_map/load/pallas_call | solution.py:203
  26.0 0.6 collective-permute-start.17
  27.1 3.4 %collective-permute-done.14.refs_1_ = bf16[16,4096]{1,0:T(8,128)(2,1)S(1)} collective-permute-done((bf16[16,4096]{1,0:T(8,128)(2,1)S(1)}, bf16[16,4096]{1,0:T(8,128)(2,1)S(1)}, u32[]{:S(2)}, u32[]{:S(2)}) %collective-permute-start.14) | collective-permute-done | bytes 131104 | tf_op jit(solution)/shard_map/ppermute | solution.py:22
  30.5 5.3 %shard_map.77 = (bf16[896,4096]{1,0:T(8,128)(2,1)S(1)}, bf16[128,4096]{1,0:T(8,128)(2,1)S(1)}, f32[896,128]{1,0:T(8,128)S(1)}, f32[896,128]{1,0:T(8,128)S(1)}, b...) custom-call(bf16[16,4096]{1,0:T(8,128)(2,1)S(1)} %bitcast.13, ...), custom_call_target="tpu_custom_call" | custom-call | flops 2818572288 | bytes 22020096 | tf_op jit(solution)/shard_map/pallas_call | solution.py:257
  35.8 0.6 collective-permute-start.10
  36.3 4.0 %shard_map.80.hidden = bf16[896,128]{1,0:T(8,128)(2,1)S(1)} custom-call(bf16[16,4096]{1,0:T(8,128)(2,1)S(1)} %get-tuple-element.44.refs_0_, bf16[16,4096]{1,0:T(8,128)(2,1)S(1)} %collective-permute-done.14.refs_1_, bf16[16,4096]{1,0:T(8,128)(2,1)S(1)} %collective-permute-done.15.refs_2_, bf16[16,4096]{1,0:T(8,128)(2,1)S(1)} %collective-permute-done.16.refs_3_, ...), custom_call_target="tpu_custom_call" | custom-call | flops 1879048192 | bytes 14680064 | tf_op jit(solution)/shard_map/pallas_call | solution.py:257
  40.3 0.9 shard_map.81
  41.3 0.6 shard_map.85
  41.9 0.6 collective-permute-start.35
  42.6 0.9 collective-permute-done.35.other
  43.6 1.5 %collective-permute-start.36 = (bf16[16,1536]{1,0:T(8,128)(2,1)S(1)}, bf16[16,1536]{1,0:T(8,128)(2,1)S(1)}, u32[]{:S(2)}, u32[]{:S(2)}) collective-permute-start(bf16[16,1536]{1,0:T(8,128)(2,1)S(1)} %get-tuple-element.56), channel_id=1, source_target_pairs={{4,0},{5,1},{6,2},{7,3},{0,4},{1,5},{2,6},{3,7},{12,8},{13,9},{14,... | collective-permute-start | bytes 147464 | tf_op jit(solution)/shard_map/ppermute | solution.py:22
  45.1 1.5 %collective-permute-start.22 = (bf16[16,2560]{1,0:T(8,128)(2,1)S(1)}, bf16[16,2560]{1,0:T(8,128)(2,1)S(1)}, u32[]{:S(2)}, u32[]{:S(2)}) collective-permute-start(bf16[16,2560]{1,0:T(8,128)(2,1)S(1)} %get-tuple-element.49), channel_id=1, source_target_pairs={{4,0},{5,1},{6,2},{7,3},{0,4},{1,5},{2,6},{3,7},{12,8},{13,9},{14,... | collective-permute-start | bytes 245768 | tf_op jit(solution)/shard_map/ppermute | solution.py:22
  46.7 1.1 %collective-permute-start.23 = (bf16[16,2560]{1,0:T(8,128)(2,1)S(1)}, bf16[16,2560]{1,0:T(8,128)(2,1)S(1)}, u32[]{:S(2)}, u32[]{:S(2)}) collective-permute-start(bf16[16,2560]{1,0:T(8,128)(2,1)S(1)} %get-tuple-element.50), channel_id=1, source_target_pairs={{2,0},{3,1},{0,2},{1,3},{6,4},{7,5},{4,6},{5,7},{10,8},{11,9},{8,1... | collective-permute-start | bytes 245768 | tf_op jit(solution)/shard_map/ppermute | solution.py:22
  47.8 1.8 %collective-permute-start.24 = (bf16[16,2560]{1,0:T(8,128)(2,1)S(1)}, bf16[16,2560]{1,0:T(8,128)(2,1)S(1)}, u32[]{:S(2)}, u32[]{:S(2)}) collective-permute-start(bf16[16,2560]{1,0:T(8,128)(2,1)S(1)} %get-tuple-element.51), channel_id=1, source_target_pairs={{6,0},{7,1},{4,2},{5,3},{2,4},{3,5},{0,6},{1,7},{14,8},{15,9},{12,... | collective-permute-start | bytes 245768 | tf_op jit(solution)/shard_map/ppermute | solution.py:22
  49.6 1.9 %collective-permute-done.36.refs_1_ = bf16[16,1536]{1,0:T(8,128)(2,1)S(1)} collective-permute-done((bf16[16,1536]{1,0:T(8,128)(2,1)S(1)}, bf16[16,1536]{1,0:T(8,128)(2,1)S(1)}, u32[]{:S(2)}, u32[]{:S(2)}) %collective-permute-start.36) | collective-permute-done | bytes 49184 | tf_op jit(solution)/shard_map/ppermute | solution.py:22
  51.5 1.7 %collective-permute-start.38 = (bf16[16,1536]{1,0:T(8,128)(2,1)S(1)}, bf16[16,1536]{1,0:T(8,128)(2,1)S(1)}, u32[]{:S(2)}, u32[]{:S(2)}) collective-permute-start(bf16[16,1536]{1,0:T(8,128)(2,1)S(1)} %get-tuple-element.58), channel_id=1, source_target_pairs={{6,0},{7,1},{4,2},{5,3},{2,4},{3,5},{0,6},{1,7},{14,8},{15,9},{12,... | collective-permute-start | bytes 147464 | tf_op jit(solution)/shard_map/ppermute | solution.py:22
  53.3 3.2 %collective-permute-done.37.refs_2_ = bf16[16,1536]{1,0:T(8,128)(2,1)S(1)} collective-permute-done((bf16[16,1536]{1,0:T(8,128)(2,1)S(1)}, bf16[16,1536]{1,0:T(8,128)(2,1)S(1)}, u32[]{:S(2)}, u32[]{:S(2)}) %collective-permute-start.37) | collective-permute-done | bytes 49184 | tf_op jit(solution)/shard_map/ppermute | solution.py:22
  56.5 1.0 %collective-permute-done.38.refs_3_ = bf16[16,1536]{1,0:T(8,128)(2,1)S(1)} collective-permute-done((bf16[16,1536]{1,0:T(8,128)(2,1)S(1)}, bf16[16,1536]{1,0:T(8,128)(2,1)S(1)}, u32[]{:S(2)}, u32[]{:S(2)}) %collective-permute-start.38) | collective-permute-done | bytes 49184 | tf_op jit(solution)/shard_map/ppermute | solution.py:22
  57.5 2.2 %collective-permute-start.13 = (bf16[16,4096]{1,0:T(8,128)(2,1)S(1)}, bf16[16,4096]{1,0:T(8,128)(2,1)S(1)}, u32[]{:S(2)}, u32[]{:S(2)}) collective-permute-start(bf16[16,4096]{1,0:T(8,128)(2,1)S(1)} %shard_map.79), channel_id=1, source_target_pairs={{4,0},{5,1},{6,2},{7,3},{0,4},{1,5},{2,6},{3,7},{12,8},{13,9},{14,... | collective-permute-start | bytes 393224 | tf_op jit(solution)/shard_map/ppermute | solution.py:22
  59.7 2.5 %collective-permute-start.41 = (bf16[16,1536]{1,0:T(8,128)(2,1)S(1)}, bf16[16,1536]{1,0:T(8,128)(2,1)S(1)}, u32[]{:S(2)}, u32[]{:S(2)}) collective-permute-start(bf16[16,1536]{1,0:T(8,128)(2,1)S(1)} %shard_map.87), channel_id=1, source_target_pairs={{24,0},{16,8},{8,16},{0,24},{25,1},{17,9},{9,17},{1,25},{26,2},{18... | collective-permute-start | bytes 147464 | tf_op jit(solution)/shard_map/ppermute | solution.py:22
  62.2 0.5 collective-permute-start.40
  62.7 0.5 collective-permute-start.39
  63.3 1.5 %collective-permute-done.41.refs_5_ = bf16[16,1536]{1,0:T(8,128)(2,1)S(1)} collective-permute-done((bf16[16,1536]{1,0:T(8,128)(2,1)S(1)}, bf16[16,1536]{1,0:T(8,128)(2,1)S(1)}, u32[]{:S(2)}, u32[]{:S(2)}) %collective-permute-start.41) | collective-permute-done | bytes 49184 | tf_op jit(solution)/shard_map/ppermute | solution.py:22
  64.9 2.5 %collective-permute-start.27 = (bf16[16,2560]{1,0:T(8,128)(2,1)S(1)}, bf16[16,2560]{1,0:T(8,128)(2,1)S(1)}, u32[]{:S(2)}, u32[]{:S(2)}) collective-permute-start(bf16[16,2560]{1,0:T(8,128)(2,1)S(1)} %shard_map.83), channel_id=1, source_target_pairs={{24,0},{16,8},{8,16},{0,24},{25,1},{17,9},{9,17},{1,25},{26,2},{18... | collective-permute-start | bytes 245768 | tf_op jit(solution)/shard_map/ppermute | solution.py:22
  67.3 0.9 collective-permute-start.26
  68.5 2.2 %collective-permute-start.44 = (bf16[16,1536]{1,0:T(8,128)(2,1)S(1)}, bf16[16,1536]{1,0:T(8,128)(2,1)S(1)}, u32[]{:S(2)}, u32[]{:S(2)}) collective-permute-start(bf16[16,1536]{1,0:T(8,128)(2,1)S(1)} %shard_map.88.refs_0_), channel_id=1, source_target_pairs={{6,0},{7,1},{4,2},{5,3},{2,4},{3,5},{0,6},{1,7},{14,8},{15,9},{12,... | collective-permute-start | bytes 147464 | tf_op jit(solution)/shard_map/ppermute | solution.py:22
  71.0 0.8 collective-permute-done.26.refs_4_
  71.8 0.8 collective-permute-done.25.refs_3_
  72.7 2.4 %collective-permute-start.30 = (bf16[16,2560]{1,0:T(8,128)(2,1)S(1)}, bf16[16,2560]{1,0:T(8,128)(2,1)S(1)}, u32[]{:S(2)}, u32[]{:S(2)}) collective-permute-start(bf16[16,2560]{1,0:T(8,128)(2,1)S(1)} %shard_map.84.refs_0_), channel_id=1, source_target_pairs={{6,0},{7,1},{4,2},{5,3},{2,4},{3,5},{0,6},{1,7},{14,8},{15,9},{12,... | collective-permute-start | bytes 245768 | tf_op jit(solution)/shard_map/ppermute | solution.py:22
  75.1 2.1 %collective-permute-start.42 = (bf16[16,1536]{1,0:T(8,128)(2,1)S(1)}, bf16[16,1536]{1,0:T(8,128)(2,1)S(1)}, u32[]{:S(2)}, u32[]{:S(2)}) collective-permute-start(bf16[16,1536]{1,0:T(8,128)(2,1)S(1)} %shard_map.88.refs_0_), channel_id=1, source_target_pairs={{4,0},{5,1},{6,2},{7,3},{0,4},{1,5},{2,6},{3,7},{12,8},{13,9},{14,... | collective-permute-start | bytes 147464 | tf_op jit(solution)/shard_map/ppermute | solution.py:22
  77.2 2.9 %collective-permute-start.28 = (bf16[16,2560]{1,0:T(8,128)(2,1)S(1)}, bf16[16,2560]{1,0:T(8,128)(2,1)S(1)}, u32[]{:S(2)}, u32[]{:S(2)}) collective-permute-start(bf16[16,2560]{1,0:T(8,128)(2,1)S(1)} %shard_map.84.refs_0_), channel_id=1, source_target_pairs={{4,0},{5,1},{6,2},{7,3},{0,4},{1,5},{2,6},{3,7},{12,8},{13,9},{14,... | collective-permute-start | bytes 245768 | tf_op jit(solution)/shard_map/ppermute | solution.py:22
  80.0 0.6 collective-permute-done.43.refs_2_
  80.7 1.4 %collective-permute-done.42.refs_1_ = bf16[16,1536]{1,0:T(8,128)(2,1)S(1)} collective-permute-done((bf16[16,1536]{1,0:T(8,128)(2,1)S(1)}, bf16[16,1536]{1,0:T(8,128)(2,1)S(1)}, u32[]{:S(2)}, u32[]{:S(2)}) %collective-permute-start.42) | collective-permute-done | bytes 49184 | tf_op jit(solution)/shard_map/ppermute | solution.py:22
  82.0 0.5 collective-permute-start.46
  83.0 0.5 collective-permute-start.34
  84.0 2.3 %shard_map.89 = (bf16[896,4096]{1,0:T(8,128)(2,1)}, f32[896,128]{1,0:T(8,128)S(1)}) custom-call(bf16[16,1536]{1,0:T(8,128)(2,1)S(1)} %shard_map.88.refs_0_, bf16[16,1536]{1,0:T(8,128)(2,1)S(1)} %collective-permute-done.42.refs_1_, bf16[16,1536]{1,0:T(8,128)(2,1)S(1)} %collective-permute-done.43.refs_2_, ...), custom_call_target="tpu_custom_call" | custom-call | flops 704643072 | bytes 5505024 | tf_op jit(solution)/shard_map/pallas_call | solution.py:407
  86.4 8.7 %shard_map.90 = (bf16[896,4096]{1,0:T(8,128)(2,1)}, bf16[896,4096]{1,0:T(8,128)(2,1)}, bf16[896,4096]{1,0:T(8,128)(2,1)}) custom-call(bf16[16,2560]{1,0:T(8,128)(2,1)S(1)} %shard_map.84.refs_0_, bf16[16,2560]{1,0:T(8,128)(2,1)S(1)} %collective-permute-done.28.refs_1_, ...), custom_call_target="tpu_custom_call", output_to_operand_aliasing={{0}: (11, {})} | custom-call | flops 3053453312 | bytes 23855104 | tf_op jit(solution)/shard_map/pallas_call | solution.py:407
  (70 shorter events, 4.0 us)
Async XLA Ops:
  0.6 9.2 %collective-permute-start.4 = (bf16[16,4096]{1,0:T(8,128)(2,1)}, bf16[16,4096]{1,0:T(8,128)(2,1)S(1)}, u32[]{:S(2)}, u32[]{:S(2)}) collective-permute-start(bf16[16,4096]{1,0:T(8,128)(2,1)} %bitcast.7), channel_id=1, source_target_pairs={{2,0},{3,1},{0,2},{1,3},{6,4},{7,5},{4,6},{5,7},{10,8},{11,9},{8,1... | collective-permute-start | bytes 393224 | tf_op jit(solution)/shard_map/ppermute | solution.py:22
  3.7 8.9 %collective-permute-start.3 = (bf16[16,4096]{1,0:T(8,128)(2,1)}, bf16[16,4096]{1,0:T(8,128)(2,1)S(1)}, u32[]{:S(2)}, u32[]{:S(2)}) collective-permute-start(bf16[16,4096]{1,0:T(8,128)(2,1)} %bitcast.8), channel_id=1, source_target_pairs={{4,0},{5,1},{6,2},{7,3},{0,4},{1,5},{2,6},{3,7},{12,8},{13,9},{14,... | collective-permute-start | bytes 393224 | tf_op jit(solution)/shard_map/ppermute | solution.py:22
  6.3 6.7 %collective-permute-start.2 = (bf16[16,4096]{1,0:T(8,128)(2,1)}, bf16[16,4096]{1,0:T(8,128)(2,1)S(1)}, u32[]{:S(2)}, u32[]{:S(2)}) collective-permute-start(bf16[16,4096]{1,0:T(8,128)(2,1)} %bitcast.9), channel_id=1, source_target_pairs={{24,0},{16,8},{8,16},{0,24},{25,1},{17,9},{9,17},{1,25},{26,2},{18... | collective-permute-start | bytes 393224 | tf_op jit(solution)/shard_map/ppermute | solution.py:22
  8.8 6.1 %collective-permute-start.1 = (bf16[16,4096]{1,0:T(8,128)(2,1)}, bf16[16,4096]{1,0:T(8,128)(2,1)S(1)}, u32[]{:S(2)}, u32[]{:S(2)}) collective-permute-start(bf16[16,4096]{1,0:T(8,128)(2,1)} %bitcast.10), channel_id=1, source_target_pairs={{16,0},{24,8},{0,16},{8,24},{17,1},{25,9},{1,17},{9,25},{18,2},{26... | collective-permute-start | bytes 393224 | tf_op jit(solution)/shard_map/ppermute | solution.py:22
  9.3 5.7 %collective-permute-start = (bf16[16,4096]{1,0:T(8,128)(2,1)}, bf16[16,4096]{1,0:T(8,128)(2,1)S(1)}, u32[]{:S(2)}, u32[]{:S(2)}) collective-permute-start(bf16[16,4096]{1,0:T(8,128)(2,1)} %bitcast.11), channel_id=1, source_target_pairs={{8,0},{0,8},{24,16},{16,24},{9,1},{1,9},{25,17},{17,25},{10,2},{2,... | collective-permute-start | bytes 393224 | tf_op jit(solution)/shard_map/ppermute | solution.py:22
  9.8 7.2 %collective-permute-start.6 = (bf16[16,4096]{1,0:T(8,128)(2,1)}, bf16[16,4096]{1,0:T(8,128)(2,1)S(1)}, u32[]{:S(2)}, u32[]{:S(2)}) collective-permute-start(bf16[16,4096]{1,0:T(8,128)(2,1)} %bitcast.12), channel_id=1, source_target_pairs={{0,1},{1,0},{2,3},{3,2},{4,5},{5,4},{6,7},{7,6},{8,9},{9,8},{10,11... | collective-permute-start | bytes 393224 | tf_op jit(solution)/shard_map/ppermute | solution.py:38
  12.7 5.1 %collective-permute-start.8 = (bf16[16,4096]{1,0:T(8,128)(2,1)S(1)}, bf16[16,4096]{1,0:T(8,128)(2,1)S(1)}, u32[]{:S(2)}, u32[]{:S(2)}) collective-permute-start(bf16[16,4096]{1,0:T(8,128)(2,1)S(1)} %collective-permute-done.4.refs_2_), channel_id=1, source_target_pairs={{0,1},{1,0},{2,3},{3,2},{4,5},{5,4},{6,7},{7,6},{8,9},{9,8},{10,11... | collective-permute-start | bytes 393224 | tf_op jit(solution)/shard_map/ppermute | solution.py:38
  13.1 7.7 %collective-permute-start.5 = (bf16[16,4096]{1,0:T(8,128)(2,1)S(1)}, bf16[16,4096]{1,0:T(8,128)(2,1)S(1)}, u32[]{:S(2)}, u32[]{:S(2)}) collective-permute-start(bf16[16,4096]{1,0:T(8,128)(2,1)S(1)} %collective-permute-done.3.refs_1_), channel_id=1, source_target_pairs={{2,0},{3,1},{0,2},{1,3},{6,4},{7,5},{4,6},{5,7},{10,8},{11,9},{8,1... | collective-permute-start | bytes 393224 | tf_op jit(solution)/shard_map/ppermute | solution.py:22
  14.9 11.0 %collective-permute-start.7 = (bf16[16,4096]{1,0:T(8,128)(2,1)S(1)}, bf16[16,4096]{1,0:T(8,128)(2,1)S(1)}, u32[]{:S(2)}, u32[]{:S(2)}) collective-permute-start(bf16[16,4096]{1,0:T(8,128)(2,1)S(1)} %collective-permute-done.3.refs_1_), channel_id=1, source_target_pairs={{0,1},{1,0},{2,3},{3,2},{4,5},{5,4},{6,7},{7,6},{8,9},{9,8},{10,11... | collective-permute-start | bytes 393224 | tf_op jit(solution)/shard_map/ppermute | solution.py:38
  16.3 10.3 %collective-permute-start.16 = (bf16[16,4096]{1,0:T(8,128)(2,1)S(1)}, bf16[16,4096]{1,0:T(8,128)(2,1)S(1)}, u32[]{:S(2)}, u32[]{:S(2)}) collective-permute-start(bf16[16,4096]{1,0:T(8,128)(2,1)S(1)} %get-tuple-element.44.refs_0_), channel_id=1, source_target_pairs={{6,0},{7,1},{4,2},{5,3},{2,4},{3,5},{0,6},{1,7},{14,8},{15,9},{12,... | collective-permute-start | bytes 393224 | tf_op jit(solution)/shard_map/ppermute | solution.py:22
  17.0 9.6 %collective-permute-start.15 = (bf16[16,4096]{1,0:T(8,128)(2,1)S(1)}, bf16[16,4096]{1,0:T(8,128)(2,1)S(1)}, u32[]{:S(2)}, u32[]{:S(2)}) collective-permute-start(bf16[16,4096]{1,0:T(8,128)(2,1)S(1)} %get-tuple-element.44.refs_0_), channel_id=1, source_target_pairs={{2,0},{3,1},{0,2},{1,3},{6,4},{7,5},{4,6},{5,7},{10,8},{11,9},{8,1... | collective-permute-start | bytes 393224 | tf_op jit(solution)/shard_map/ppermute | solution.py:22
  17.8 12.6 %collective-permute-start.14 = (bf16[16,4096]{1,0:T(8,128)(2,1)S(1)}, bf16[16,4096]{1,0:T(8,128)(2,1)S(1)}, u32[]{:S(2)}, u32[]{:S(2)}) collective-permute-start(bf16[16,4096]{1,0:T(8,128)(2,1)S(1)} %get-tuple-element.44.refs_0_), channel_id=1, source_target_pairs={{4,0},{5,1},{6,2},{7,3},{0,4},{1,5},{2,6},{3,7},{12,8},{13,9},{14,... | collective-permute-start | bytes 393224 | tf_op jit(solution)/shard_map/ppermute | solution.py:22
  20.7 9.7 %collective-permute-start.9 = (bf16[16,4096]{1,0:T(8,128)(2,1)S(1)}, bf16[16,4096]{1,0:T(8,128)(2,1)S(1)}, u32[]{:S(2)}, u32[]{:S(2)}) collective-permute-start(bf16[16,4096]{1,0:T(8,128)(2,1)S(1)} %collective-permute-done.5.refs_3_), channel_id=1, source_target_pairs={{0,1},{1,0},{2,3},{3,2},{4,5},{5,4},{6,7},{7,6},{8,9},{9,8},{10,11... | collective-permute-start | bytes 393224 | tf_op jit(solution)/shard_map/ppermute | solution.py:38
  26.0 10.3 %collective-permute-start.17 = (bf16[16,4096]{1,0:T(8,128)(2,1)S(1)}, bf16[16,4096]{1,0:T(8,128)(2,1)S(1)}, u32[]{:S(2)}, u32[]{:S(2)}) collective-permute-start(bf16[16,4096]{1,0:T(8,128)(2,1)S(1)} %get-tuple-element.44.refs_0_), channel_id=1, source_target_pairs={{0,1},{1,0},{2,3},{3,2},{4,5},{5,4},{6,7},{7,6},{8,9},{9,8},{10,11... | collective-permute-start | bytes 393224 | tf_op jit(solution)/shard_map/ppermute | solution.py:38
  26.5 9.8 %collective-permute-start.20 = (bf16[16,4096]{1,0:T(8,128)(2,1)S(1)}, bf16[16,4096]{1,0:T(8,128)(2,1)S(1)}, u32[]{:S(2)}, u32[]{:S(2)}) collective-permute-start(bf16[16,4096]{1,0:T(8,128)(2,1)S(1)} %collective-permute-done.16.refs_3_), channel_id=1, source_target_pairs={{0,1},{1,0},{2,3},{3,2},{4,5},{5,4},{6,7},{7,6},{8,9},{9,8},{10,11... | collective-permute-start | bytes 393224 | tf_op jit(solution)/shard_map/ppermute | solution.py:38
  26.7 9.7 %collective-permute-start.19 = (bf16[16,4096]{1,0:T(8,128)(2,1)S(1)}, bf16[16,4096]{1,0:T(8,128)(2,1)S(1)}, u32[]{:S(2)}, u32[]{:S(2)}) collective-permute-start(bf16[16,4096]{1,0:T(8,128)(2,1)S(1)} %collective-permute-done.15.refs_2_), channel_id=1, source_target_pairs={{0,1},{1,0},{2,3},{3,2},{4,5},{5,4},{6,7},{7,6},{8,9},{9,8},{10,11... | collective-permute-start | bytes 393224 | tf_op jit(solution)/shard_map/ppermute | solution.py:38
  30.5 5.9 %collective-permute-start.18 = (bf16[16,4096]{1,0:T(8,128)(2,1)S(1)}, bf16[16,4096]{1,0:T(8,128)(2,1)S(1)}, u32[]{:S(2)}, u32[]{:S(2)}) collective-permute-start(bf16[16,4096]{1,0:T(8,128)(2,1)S(1)} %collective-permute-done.14.refs_1_), channel_id=1, source_target_pairs={{0,1},{1,0},{2,3},{3,2},{4,5},{5,4},{6,7},{7,6},{8,9},{9,8},{10,11... | collective-permute-start | bytes 393224 | tf_op jit(solution)/shard_map/ppermute | solution.py:38
  35.8 6.7 %collective-permute-start.10 = (bf16[64,4096]{1,0:T(8,128)(2,1)S(1)}, bf16[64,4096]{1,0:T(8,128)(2,1)S(1)}, u32[]{:S(2)}, u32[]{:S(2)}) collective-permute-start(bf16[64,4096]{1,0:T(8,128)(2,1)S(1)} %get-tuple-element.39), channel_id=1, source_target_pairs={{0,1},{1,0},{2,3},{3,2},{4,5},{5,4},{6,7},{7,6},{8,9},{9,8},{10,11... | collective-permute-start | bytes 1572872 | tf_op jit(solution)/shard_map/ppermute | solution.py:38
  41.2 3.9 %collective-permute-start.21 = (bf16[64,2560]{1,0:T(8,128)(2,1)S(1)}, bf16[64,2560]{1,0:T(8,128)(2,1)S(1)}, u32[]{:S(2)}, u32[]{:S(2)}) collective-permute-start(bf16[64,2560]{1,0:T(8,128)(2,1)S(1)} %get-tuple-element.47), channel_id=1, source_target_pairs={{0,1},{1,0},{2,3},{3,2},{4,5},{5,4},{6,7},{7,6},{8,9},{9,8},{10,11... | collective-permute-start | bytes 983048 | tf_op jit(solution)/shard_map/ppermute | solution.py:38
  41.9 1.6 %collective-permute-start.35 = (bf16[64,1536]{1,0:T(8,128)(2,1)S(1)}, bf16[64,1536]{1,0:T(8,128)(2,1)S(1)}, u32[]{:S(2)}, u32[]{:S(2)}) collective-permute-start(bf16[64,1536]{1,0:T(8,128)(2,1)S(1)} %get-tuple-element.54), channel_id=1, source_target_pairs={{0,1},{1,0},{2,3},{3,2},{4,5},{5,4},{6,7},{7,6},{8,9},{9,8},{10,11... | collective-permute-start | bytes 589832 | tf_op jit(solution)/shard_map/ppermute | solution.py:38
  42.5 9.0 %collective-permute-start.12 = (bf16[16,4096]{1,0:T(8,128)(2,1)S(1)}, bf16[16,4096]{1,0:T(8,128)(2,1)S(1)}, u32[]{:S(2)}, u32[]{:S(2)}) collective-permute-start(bf16[16,4096]{1,0:T(8,128)(2,1)S(1)} %get-tuple-element.43), channel_id=1, source_target_pairs={{2,0},{3,1},{0,2},{1,3},{6,4},{7,5},{4,6},{5,7},{10,8},{11,9},{8,1... | collective-permute-start | bytes 393224 | tf_op jit(solution)/shard_map/ppermute | solution.py:22
  43.6 7.9 %collective-permute-start.36 = (bf16[16,1536]{1,0:T(8,128)(2,1)S(1)}, bf16[16,1536]{1,0:T(8,128)(2,1)S(1)}, u32[]{:S(2)}, u32[]{:S(2)}) collective-permute-start(bf16[16,1536]{1,0:T(8,128)(2,1)S(1)} %get-tuple-element.56), channel_id=1, source_target_pairs={{4,0},{5,1},{6,2},{7,3},{0,4},{1,5},{2,6},{3,7},{12,8},{13,9},{14,... | collective-permute-start | bytes 147464 | tf_op jit(solution)/shard_map/ppermute | solution.py:22
  45.1 14.6 %collective-permute-start.22 = (bf16[16,2560]{1,0:T(8,128)(2,1)S(1)}, bf16[16,2560]{1,0:T(8,128)(2,1)S(1)}, u32[]{:S(2)}, u32[]{:S(2)}) collective-permute-start(bf16[16,2560]{1,0:T(8,128)(2,1)S(1)} %get-tuple-element.49), channel_id=1, source_target_pairs={{4,0},{5,1},{6,2},{7,3},{0,4},{1,5},{2,6},{3,7},{12,8},{13,9},{14,... | collective-permute-start | bytes 245768 | tf_op jit(solution)/shard_map/ppermute | solution.py:22
  46.7 15.5 %collective-permute-start.23 = (bf16[16,2560]{1,0:T(8,128)(2,1)S(1)}, bf16[16,2560]{1,0:T(8,128)(2,1)S(1)}, u32[]{:S(2)}, u32[]{:S(2)}) collective-permute-start(bf16[16,2560]{1,0:T(8,128)(2,1)S(1)} %get-tuple-element.50), channel_id=1, source_target_pairs={{2,0},{3,1},{0,2},{1,3},{6,4},{7,5},{4,6},{5,7},{10,8},{11,9},{8,1... | collective-permute-start | bytes 245768 | tf_op jit(solution)/shard_map/ppermute | solution.py:22
  47.8 14.9 %collective-permute-start.24 = (bf16[16,2560]{1,0:T(8,128)(2,1)S(1)}, bf16[16,2560]{1,0:T(8,128)(2,1)S(1)}, u32[]{:S(2)}, u32[]{:S(2)}) collective-permute-start(bf16[16,2560]{1,0:T(8,128)(2,1)S(1)} %get-tuple-element.51), channel_id=1, source_target_pairs={{6,0},{7,1},{4,2},{5,3},{2,4},{3,5},{0,6},{1,7},{14,8},{15,9},{12,... | collective-permute-start | bytes 245768 | tf_op jit(solution)/shard_map/ppermute | solution.py:22
  51.5 5.0 %collective-permute-start.37 = (bf16[16,1536]{1,0:T(8,128)(2,1)S(1)}, bf16[16,1536]{1,0:T(8,128)(2,1)S(1)}, u32[]{:S(2)}, u32[]{:S(2)}) collective-permute-start(bf16[16,1536]{1,0:T(8,128)(2,1)S(1)} %get-tuple-element.57), channel_id=1, source_target_pairs={{2,0},{3,1},{0,2},{1,3},{6,4},{7,5},{4,6},{5,7},{10,8},{11,9},{8,1... | collective-permute-start | bytes 147464 | tf_op jit(solution)/shard_map/ppermute | solution.py:22
  51.5 6.0 %collective-permute-start.38 = (bf16[16,1536]{1,0:T(8,128)(2,1)S(1)}, bf16[16,1536]{1,0:T(8,128)(2,1)S(1)}, u32[]{:S(2)}, u32[]{:S(2)}) collective-permute-start(bf16[16,1536]{1,0:T(8,128)(2,1)S(1)} %get-tuple-element.58), channel_id=1, source_target_pairs={{6,0},{7,1},{4,2},{5,3},{2,4},{3,5},{0,6},{1,7},{14,8},{15,9},{12,... | collective-permute-start | bytes 147464 | tf_op jit(solution)/shard_map/ppermute | solution.py:22
  56.5 11.8 %collective-permute-start.11 = (bf16[16,4096]{1,0:T(8,128)(2,1)S(1)}, bf16[16,4096]{1,0:T(8,128)(2,1)S(1)}, u32[]{:S(2)}, u32[]{:S(2)}) collective-permute-start(bf16[16,4096]{1,0:T(8,128)(2,1)S(1)} %get-tuple-element.41), channel_id=1, source_target_pairs={{2,0},{3,1},{0,2},{1,3},{6,4},{7,5},{4,6},{5,7},{10,8},{11,9},{8,1... | collective-permute-start | bytes 393224 | tf_op jit(solution)/shard_map/ppermute | solution.py:22
  57.5 10.8 %collective-permute-start.13 = (bf16[16,4096]{1,0:T(8,128)(2,1)S(1)}, bf16[16,4096]{1,0:T(8,128)(2,1)S(1)}, u32[]{:S(2)}, u32[]{:S(2)}) collective-permute-start(bf16[16,4096]{1,0:T(8,128)(2,1)S(1)} %shard_map.79), channel_id=1, source_target_pairs={{4,0},{5,1},{6,2},{7,3},{0,4},{1,5},{2,6},{3,7},{12,8},{13,9},{14,... | collective-permute-start | bytes 393224 | tf_op jit(solution)/shard_map/ppermute | solution.py:22
  59.7 5.2 %collective-permute-start.41 = (bf16[16,1536]{1,0:T(8,128)(2,1)S(1)}, bf16[16,1536]{1,0:T(8,128)(2,1)S(1)}, u32[]{:S(2)}, u32[]{:S(2)}) collective-permute-start(bf16[16,1536]{1,0:T(8,128)(2,1)S(1)} %shard_map.87), channel_id=1, source_target_pairs={{24,0},{16,8},{8,16},{0,24},{25,1},{17,9},{9,17},{1,25},{26,2},{18... | collective-permute-start | bytes 147464 | tf_op jit(solution)/shard_map/ppermute | solution.py:22
  62.2 5.1 %collective-permute-start.40 = (bf16[16,1536]{1,0:T(8,128)(2,1)S(1)}, bf16[16,1536]{1,0:T(8,128)(2,1)S(1)}, u32[]{:S(2)}, u32[]{:S(2)}) collective-permute-start(bf16[16,1536]{1,0:T(8,128)(2,1)S(1)} %shard_map.87), channel_id=1, source_target_pairs={{16,0},{24,8},{0,16},{8,24},{17,1},{25,9},{1,17},{9,25},{18,2},{26... | collective-permute-start | bytes 147464 | tf_op jit(solution)/shard_map/ppermute | solution.py:22
  62.7 5.4 %collective-permute-start.39 = (bf16[16,1536]{1,0:T(8,128)(2,1)S(1)}, bf16[16,1536]{1,0:T(8,128)(2,1)S(1)}, u32[]{:S(2)}, u32[]{:S(2)}) collective-permute-start(bf16[16,1536]{1,0:T(8,128)(2,1)S(1)} %shard_map.87), channel_id=1, source_target_pairs={{8,0},{0,8},{24,16},{16,24},{9,1},{1,9},{25,17},{17,25},{10,2},{2,... | collective-permute-start | bytes 147464 | tf_op jit(solution)/shard_map/ppermute | solution.py:22
  64.9 6.1 %collective-permute-start.27 = (bf16[16,2560]{1,0:T(8,128)(2,1)S(1)}, bf16[16,2560]{1,0:T(8,128)(2,1)S(1)}, u32[]{:S(2)}, u32[]{:S(2)}) collective-permute-start(bf16[16,2560]{1,0:T(8,128)(2,1)S(1)} %shard_map.83), channel_id=1, source_target_pairs={{24,0},{16,8},{8,16},{0,24},{25,1},{17,9},{9,17},{1,25},{26,2},{18... | collective-permute-start | bytes 245768 | tf_op jit(solution)/shard_map/ppermute | solution.py:22
  67.3 4.5 %collective-permute-start.26 = (bf16[16,2560]{1,0:T(8,128)(2,1)S(1)}, bf16[16,2560]{1,0:T(8,128)(2,1)S(1)}, u32[]{:S(2)}, u32[]{:S(2)}) collective-permute-start(bf16[16,2560]{1,0:T(8,128)(2,1)S(1)} %shard_map.83), channel_id=1, source_target_pairs={{16,0},{24,8},{0,16},{8,24},{17,1},{25,9},{1,17},{9,25},{18,2},{26... | collective-permute-start | bytes 245768 | tf_op jit(solution)/shard_map/ppermute | solution.py:22
  68.2 4.4 %collective-permute-start.25 = (bf16[16,2560]{1,0:T(8,128)(2,1)S(1)}, bf16[16,2560]{1,0:T(8,128)(2,1)S(1)}, u32[]{:S(2)}, u32[]{:S(2)}) collective-permute-start(bf16[16,2560]{1,0:T(8,128)(2,1)S(1)} %shard_map.83), channel_id=1, source_target_pairs={{8,0},{0,8},{24,16},{16,24},{9,1},{1,9},{25,17},{17,25},{10,2},{2,... | collective-permute-start | bytes 245768 | tf_op jit(solution)/shard_map/ppermute | solution.py:22
  68.4 8.8 %collective-permute-start.45 = (bf16[16,1536]{1,0:T(8,128)(2,1)S(1)}, bf16[16,1536]{1,0:T(8,128)(2,1)S(1)}, u32[]{:S(2)}, u32[]{:S(2)}) collective-permute-start(bf16[16,1536]{1,0:T(8,128)(2,1)S(1)} %shard_map.88.refs_0_), channel_id=1, source_target_pairs={{0,1},{1,0},{2,3},{3,2},{4,5},{5,4},{6,7},{7,6},{8,9},{9,8},{10,11... | collective-permute-start | bytes 147464 | tf_op jit(solution)/shard_map/ppermute | solution.py:38
  68.5 8.7 %collective-permute-start.44 = (bf16[16,1536]{1,0:T(8,128)(2,1)S(1)}, bf16[16,1536]{1,0:T(8,128)(2,1)S(1)}, u32[]{:S(2)}, u32[]{:S(2)}) collective-permute-start(bf16[16,1536]{1,0:T(8,128)(2,1)S(1)} %shard_map.88.refs_0_), channel_id=1, source_target_pairs={{6,0},{7,1},{4,2},{5,3},{2,4},{3,5},{0,6},{1,7},{14,8},{15,9},{12,... | collective-permute-start | bytes 147464 | tf_op jit(solution)/shard_map/ppermute | solution.py:22
  72.7 9.3 %collective-permute-start.30 = (bf16[16,2560]{1,0:T(8,128)(2,1)S(1)}, bf16[16,2560]{1,0:T(8,128)(2,1)S(1)}, u32[]{:S(2)}, u32[]{:S(2)}) collective-permute-start(bf16[16,2560]{1,0:T(8,128)(2,1)S(1)} %shard_map.84.refs_0_), channel_id=1, source_target_pairs={{6,0},{7,1},{4,2},{5,3},{2,4},{3,5},{0,6},{1,7},{14,8},{15,9},{12,... | collective-permute-start | bytes 245768 | tf_op jit(solution)/shard_map/ppermute | solution.py:22
  75.1 5.6 %collective-permute-start.43 = (bf16[16,1536]{1,0:T(8,128)(2,1)S(1)}, bf16[16,1536]{1,0:T(8,128)(2,1)S(1)}, u32[]{:S(2)}, u32[]{:S(2)}) collective-permute-start(bf16[16,1536]{1,0:T(8,128)(2,1)S(1)} %shard_map.88.refs_0_), channel_id=1, source_target_pairs={{2,0},{3,1},{0,2},{1,3},{6,4},{7,5},{4,6},{5,7},{10,8},{11,9},{8,1... | collective-permute-start | bytes 147464 | tf_op jit(solution)/shard_map/ppermute | solution.py:22
  75.1 7.0 %collective-permute-start.42 = (bf16[16,1536]{1,0:T(8,128)(2,1)S(1)}, bf16[16,1536]{1,0:T(8,128)(2,1)S(1)}, u32[]{:S(2)}, u32[]{:S(2)}) collective-permute-start(bf16[16,1536]{1,0:T(8,128)(2,1)S(1)} %shard_map.88.refs_0_), channel_id=1, source_target_pairs={{4,0},{5,1},{6,2},{7,3},{0,4},{1,5},{2,6},{3,7},{12,8},{13,9},{14,... | collective-permute-start | bytes 147464 | tf_op jit(solution)/shard_map/ppermute | solution.py:22
  77.2 5.8 %collective-permute-start.29 = (bf16[16,2560]{1,0:T(8,128)(2,1)S(1)}, bf16[16,2560]{1,0:T(8,128)(2,1)S(1)}, u32[]{:S(2)}, u32[]{:S(2)}) collective-permute-start(bf16[16,2560]{1,0:T(8,128)(2,1)S(1)} %shard_map.84.refs_0_), channel_id=1, source_target_pairs={{2,0},{3,1},{0,2},{1,3},{6,4},{7,5},{4,6},{5,7},{10,8},{11,9},{8,1... | collective-permute-start | bytes 245768 | tf_op jit(solution)/shard_map/ppermute | solution.py:22
  77.2 5.8 %collective-permute-start.28 = (bf16[16,2560]{1,0:T(8,128)(2,1)S(1)}, bf16[16,2560]{1,0:T(8,128)(2,1)S(1)}, u32[]{:S(2)}, u32[]{:S(2)}) collective-permute-start(bf16[16,2560]{1,0:T(8,128)(2,1)S(1)} %shard_map.84.refs_0_), channel_id=1, source_target_pairs={{4,0},{5,1},{6,2},{7,3},{0,4},{1,5},{2,6},{3,7},{12,8},{13,9},{14,... | collective-permute-start | bytes 245768 | tf_op jit(solution)/shard_map/ppermute | solution.py:22
  80.7 2.8 %collective-permute-start.48 = (bf16[16,1536]{1,0:T(8,128)(2,1)S(1)}, bf16[16,1536]{1,0:T(8,128)(2,1)S(1)}, u32[]{:S(2)}, u32[]{:S(2)}) collective-permute-start(bf16[16,1536]{1,0:T(8,128)(2,1)S(1)} %collective-permute-done.44.refs_3_), channel_id=1, source_target_pairs={{0,1},{1,0},{2,3},{3,2},{4,5},{5,4},{6,7},{7,6},{8,9},{9,8},{10,11... | collective-permute-start | bytes 147464 | tf_op jit(solution)/shard_map/ppermute | solution.py:38
  82.0 2.0 %collective-permute-start.46 = (bf16[16,1536]{1,0:T(8,128)(2,1)S(1)}, bf16[16,1536]{1,0:T(8,128)(2,1)S(1)}, u32[]{:S(2)}, u32[]{:S(2)}) collective-permute-start(bf16[16,1536]{1,0:T(8,128)(2,1)S(1)} %collective-permute-done.42.refs_1_), channel_id=1, source_target_pairs={{0,1},{1,0},{2,3},{3,2},{4,5},{5,4},{6,7},{7,6},{8,9},{9,8},{10,11... | collective-permute-start | bytes 147464 | tf_op jit(solution)/shard_map/ppermute | solution.py:38
  83.0 3.4 %collective-permute-start.31 = (bf16[16,2560]{1,0:T(8,128)(2,1)S(1)}, bf16[16,2560]{1,0:T(8,128)(2,1)S(1)}, u32[]{:S(2)}, u32[]{:S(2)}) collective-permute-start(bf16[16,2560]{1,0:T(8,128)(2,1)S(1)} %shard_map.84.refs_0_), channel_id=1, source_target_pairs={{0,1},{1,0},{2,3},{3,2},{4,5},{5,4},{6,7},{7,6},{8,9},{9,8},{10,11... | collective-permute-start | bytes 245768 | tf_op jit(solution)/shard_map/ppermute | solution.py:38
  83.0 3.4 %collective-permute-start.34 = (bf16[16,2560]{1,0:T(8,128)(2,1)S(1)}, bf16[16,2560]{1,0:T(8,128)(2,1)S(1)}, u32[]{:S(2)}, u32[]{:S(2)}) collective-permute-start(bf16[16,2560]{1,0:T(8,128)(2,1)S(1)} %collective-permute-done.30.refs_3_), channel_id=1, source_target_pairs={{0,1},{1,0},{2,3},{3,2},{4,5},{5,4},{6,7},{7,6},{8,9},{9,8},{10,11... | collective-permute-start | bytes 245768 | tf_op jit(solution)/shard_map/ppermute | solution.py:38
  83.5 2.9 %collective-permute-start.33 = (bf16[16,2560]{1,0:T(8,128)(2,1)S(1)}, bf16[16,2560]{1,0:T(8,128)(2,1)S(1)}, u32[]{:S(2)}, u32[]{:S(2)}) collective-permute-start(bf16[16,2560]{1,0:T(8,128)(2,1)S(1)} %collective-permute-done.29.refs_2_), channel_id=1, source_target_pairs={{0,1},{1,0},{2,3},{3,2},{4,5},{5,4},{6,7},{7,6},{8,9},{9,8},{10,11... | collective-permute-start | bytes 245768 | tf_op jit(solution)/shard_map/ppermute | solution.py:38
  83.6 2.8 %collective-permute-start.32 = (bf16[16,2560]{1,0:T(8,128)(2,1)S(1)}, bf16[16,2560]{1,0:T(8,128)(2,1)S(1)}, u32[]{:S(2)}, u32[]{:S(2)}) collective-permute-start(bf16[16,2560]{1,0:T(8,128)(2,1)S(1)} %collective-permute-done.28.refs_1_), channel_id=1, source_target_pairs={{0,1},{1,0},{2,3},{3,2},{4,5},{5,4},{6,7},{7,6},{8,9},{9,8},{10,11... | collective-permute-start | bytes 245768 | tf_op jit(solution)/shard_map/ppermute | solution.py:38
  (3 other events, 11.9 us)
